TPU v7x, 256 devices: a whole 4x4x8 slice. The times are simulated.
256 devices in a mesh: tile: 64 (over z, y_lo, x), lev: 4 (over y_hi, core).
Axes of the slice: x: 4, y: 4 (y_hi: 2, y_lo: 2; y = y_hi * 2 + y_lo), z: 8, core: 2. Of those that a mesh axis runs over, the one named last changes fastest.
Arguments:
- control_static: float32 [2, 128, 512, 128], P(None, 'lev', 'tile'), may hold values from -6 to 6
- control_ens: float32 [2, 128, 512, 128], P(None, 'lev', 'tile'), may hold values from -6 to 6
- ens_perts: bfloat16 [2, 2, 128, 512, 128], P(None, None, 'lev', 'tile'), may hold values from -2.5 to 2.5
- band_sqrt: float32 [64, 2, 128, 128], P('tile', None, 'lev'), may hold values from -1 to 2
- band_owner: int32 [64], replicated, may hold values from 0 to 63, each once
- scale_class: int32 [512, 128], P('tile'), may hold values from 0 to 7
- static_scales: float32 [8], replicated, may hold values from 0.5 to 4
- local_scales: float32 [8], replicated, may hold values from 1 to 8
- obs_source: int32 [32768, 1], P('tile'), may hold values from 0 to 63; in each aligned block of 512 rows (0 to 511, 512 to 1023, ...) at most 32 rows name the same one
- obs_column: int32 [32768], P('tile'), may hold values from 0 to 1023
- obs_jac: float32 [64, 128, 2, 128], P('tile', None, None, 'lev'), may hold values from -0.375 to 0.375
- innovation: float32 [128, 32768], P(None, 'tile'), may hold values from -6 to 6
- obs_weight: float32 [128, 32768], P(None, 'tile'), may hold values from 0.2 to 5
Outputs:
- analysis_increment: float32 [2, 128, 512, 128], P(None, 'lev', 'tile')
- final_static: float32 [2, 128, 512, 128], P(None, 'lev', 'tile')
- final_ens: float32 [2, 128, 512, 128], P(None, 'lev', 'tile')
Inputs may be any that keep to these rules, and one draw needn't show every extreme that they name: `obs_source`: within each tile's block of 512 observations at most 32 name the same source tile, and some source tile is named exactly 32 times in some block. `band_owner`: each slot is named once.
All inputs are finite; a program needn't handle non-finite values.
Results may differ from a plain program's by a relative error of at most 0.0003.
Values sent between devices are 32-bit elements; how exact they have to be, the bound alone decides.
No kernel may reach another device: no remote copies, remote signals or barrier semaphores. Data moves between devices by JAX's collectives and lax.ppermute only.
A program may use at most 64 MiB of HBM per device.

v0:
```python
import functools

import jax
import jax.numpy as jnp
from jax import lax
from jax.experimental import pallas as pl
from jax.experimental.pallas import tpu as pltpu
from jax.sharding import Mesh, PartitionSpec as P

NSWEEP = 4
ITERS = 2

beta_static = 0.8
beta_ensemble = 0.6
step_length = 0.3

LEV = ("yh", "core")
TILE = ("z", "yl", "x")
PLANE = ("yl", "x", "yh", "core")
AXES = ("z", "yl", "x", "yh", "core")

f32, bf16, i32 = jnp.float32, jnp.bfloat16, jnp.int32


def iota(shape, dim):
    return lax.broadcasted_iota(i32, shape, dim)


def split(value):
    high = value.astype(bf16)
    return high, (value - high.astype(f32)).astype(bf16)


def dot_nn(a, b):
    return lax.dot_general(a, b, (((1,), (0,)), ((), ())), preferred_element_type=f32)


def dot_nt(a, b):
    return lax.dot_general(a, b, (((1,), (1,)), ((), ())), preferred_element_type=f32)


def dot_tn(a, b):
    return lax.dot_general(a, b, (((0,), (0,)), ((), ())), preferred_element_type=f32)


def three(dot, a, b):
    (ah, al), (bh, bl) = split(a), split(b)
    return dot(ah, bh) + (dot(ah, bl) + dot(al, bh))


def one_hot(mask):
    return jnp.where(mask, 1.0, 0.0).astype(bf16)


def call(kernel, outs, scratch=(), smem=0, total=0, flops=10**8, size=6 * 10**6):
    spaces = [pl.BlockSpec(memory_space=pltpu.SMEM)] * smem
    spaces += [pl.BlockSpec(memory_space=pltpu.VMEM)] * (total - smem)
    return pl.pallas_call(
        kernel,
        out_shape=[jax.ShapeDtypeStruct(shape, kind) for shape, kind in outs],
        in_specs=spaces,
        out_specs=[pl.BlockSpec(memory_space=pltpu.VMEM)] * len(outs),
        scratch_shapes=[pltpu.VMEM(shape, kind) for shape, kind in scratch],
        compiler_params=pltpu.CompilerParams(vmem_limit_bytes=24 * 2**20),
        cost_estimate=pl.CostEstimate(flops=flops, bytes_accessed=size, transcendentals=0),
    )


def selector(owner):
    row, lane = iota((512, 128), 0), iota((512, 128), 1)
    slot = (((row >> 4) & 3) * 2 + ((row >> 1) & 1)) * 8 + (row >> 6)
    hit = (owner == slot) & ((lane & 1) == (row & 1))
    pair = (row >> 2) & 3
    return jnp.concatenate([one_hot(hit & (pair == q)) for q in range(4)], axis=1)


def pack(field, owner):
    wide = jnp.concatenate([field(q) for q in range(4)], axis=1)
    high, low = split(wide)
    chosen = selector(owner)
    return dot_nt(chosen, high) + dot_nt(chosen, low)


def unpack(rows, owner):
    high, low = split(rows)
    chosen = selector(owner)
    return dot_tn(high, chosen) + dot_tn(low, chosen)


def begin_kernel(owner, static_in, packed, work):
    for lon in range(8):
        work[lon] = static_in[pl.ds(lon, 64, stride=8), :]
    packed[...] = pack(lambda q: work[2 * q : 2 * q + 2].reshape(128, 128), owner[...])


def begin_members_kernel(ens_in, perts_in, classes, up, down, ens, perts, flat):
    flat[...] = perts_in[...].astype(f32).reshape(1024, 128)
    for lon in range(8):
        member = ens_in[pl.ds(lon, 64, stride=8), :]
        ens[lon] = member
        perts[lon] = flat[pl.ds(lon, 128, stride=8), :]
        target, place = (down, lon) if lon < 4 else (up, lon - 4)
        target[place * 64 : place * 64 + 64] = member
    marks = classes[...].astype(f32)
    up[256:264] = marks
    down[256:264] = marks


def request_kernel(source_row, column_row, request, ranks):
    source = source_row[...]
    mine = iota((64, 512), 0) == source
    marks = one_hot(mine)
    earlier = one_hot(iota((512, 512), 0) < iota((512, 512), 1))
    count = dot_nn(marks, earlier)
    rank = jnp.sum(jnp.where(mine, count, 0.0), axis=0, keepdims=True).astype(i32)
    ranks[...] = rank
    wanted = column_row[...] + 1
    ranked = one_hot(iota((128, 512), 0) == rank)
    high = jnp.where(mine, (wanted >> 5).astype(f32), 0.0).astype(bf16)
    low = jnp.where(mine, (wanted & 31).astype(f32), 0.0).astype(bf16)
    request[...] = 32.0 * dot_nt(high, ranked) + dot_nt(low, ranked)


def slots_kernel(here, source_row, ranks, weight, innovation, first, second):
    z, level = here[0], here[1]
    source, rank = source_row[...], ranks[...]
    row = iota((512, 512), 0)
    place = (row >> 3) == source
    kind = (row >> 2) & 1
    terms = split(jnp.concatenate([weight[...], innovation[...]], axis=1))
    for j, target in enumerate((first, second)):
        group = 2 * level + lax.rem(z + j, 2)
        mine = place & (rank == group * 4 + (row & 3))
        hits = jnp.concatenate([one_hot(mine & (kind == w)) for w in range(2)], axis=1)
        target[...] = dot_nt(hits, terms[0]) + dot_nt(hits, terms[1])


def arrange_kernel(arrived, wanted, weights, targets):
    wanted[...] = arrived[pl.ds(16, 64, stride=24), :].astype(i32)
    for half in range(2):
        for u in range(8):
            for z in range(8):
                start = (z * 8 + u) * 24 + ((half + z) % 2) * 8
                weights[half * 8 + u, 4 * z : 4 * z + 4] = arrived[start : start + 4]
                targets[half * 8 + u, 4 * z : 4 * z + 4] = arrived[start + 4 : start + 8]


def load_matrices(here, first, second, matrices):
    z = here[0]
    for j, part in enumerate((first, second)):
        half = lax.rem(z + j, 2)
        for k in range(4):
            block = lax.bitwise_xor(lax.div(z, 2), k)
            rows = pl.ds(pl.multiple_of(block * 32, 32), 32)
            for var in range(2):
                start = k * 128 + var * 32
                matrices[half * 2 + var, rows, :] = part[start : start + 32]


def columns_of(rows):
    blocks = [
        jnp.concatenate([rows[u * 64 + l * 16 : u * 64 + l * 16 + 16] for u in range(8)], axis=0)
        for l in range(4)
    ]
    chunk = iota((128, 128), 1) >> 5
    out = []
    for c in range(4):
        joined = None
        for l in range(4):
            shift = (32 * (l - c)) % 128
            moved = pltpu.roll(blocks[l], shift, 1) if shift else blocks[l]
            joined = moved if l == 0 else jnp.where(chunk == l, moved, joined)
        out.append(joined)
    return out


def store_columns(out, columns, stride, offset):
    chunk = iota((128, 128), 1) >> 5
    for l in range(4):
        joined = None
        for c in range(4):
            shift = (32 * (c - l)) % 128
            moved = pltpu.roll(columns[c], shift, 1) if shift else columns[c]
            joined = moved if c == 0 else jnp.where(chunk == c, moved, joined)
        for u in range(8):
            start = (u * 4 + l) * stride + offset
            out[start : start + 16] = joined[u * 16 : u * 16 + 16]


def choose_half(product):
    half = (iota((256, 128), 0) >> 1) & 1
    return jnp.where(half == 0, product[:, :128], product[:, 128:])


def forward_columns(columns, matrices):
    out = [None] * 4
    for var in range(2):
        stacked = jnp.concatenate([columns[var], columns[2 + var]], axis=0)
        pair = jnp.concatenate([matrices[var], matrices[2 + var]], axis=0)
        chosen = choose_half(three(dot_nt, stacked, pair))
        out[var], out[2 + var] = chosen[:128], chosen[128:]
    return out


def backward_columns(columns, matrices):
    out = [None] * 4
    for var in range(2):
        stacked = jnp.concatenate([columns[var], columns[2 + var]], axis=0)
        pair = jnp.concatenate([matrices[var], matrices[2 + var]], axis=1)
        chosen = choose_half(three(dot_nn, stacked, pair))
        out[var], out[2 + var] = chosen[:128], chosen[128:]
    return out


def first_columns_kernel(here, rows, first, second, state, out, matrices):
    load_matrices(here, first, second, matrices)
    columns = columns_of(rows[...])
    for c in range(4):
        state[c] = columns[c]
    store_columns(out, forward_columns(columns, matrices), 16, 0)


def columns_kernel(last, here, rows, first, second, state, *refs):
    out, matrices = refs[-2], refs[-1]
    load_matrices(here, first, second, matrices)
    pulled = backward_columns(columns_of(rows[...]), matrices)
    columns = [(1.0 - step_length) * state[c] - step_length * pulled[c] for c in range(4)]
    forward = forward_columns(columns, matrices)
    if last:
        store_columns(out, forward, 32, 0)
        store_columns(out, columns, 32, 16)
    else:
        for c in range(4):
            refs[0][c] = columns[c]
        store_columns(out, forward, 16, 0)


def edges_kernel(owner, rows, low, high):
    wide = unpack(rows[...], owner[...])
    for lon in range(8):
        target, place = (low, lon) if lon < 4 else (high, lon - 4)
        q, side = lon // 2, lon % 2
        target[place] = wide[side * 64 : side * 64 + 64, q * 128 : q * 128 + 128]


def last_edges_kernel(owner, rows, low, high, final_static):
    both = rows[...]
    for kind in range(2):
        part = jnp.concatenate([both[p * 32 + kind * 16 : p * 32 + kind * 16 + 16] for p in range(32)], axis=0)
        wide = unpack(part, owner[...])
        for lon in range(8):
            q, side = lon // 2, lon % 2
            value = wide[side * 64 : side * 64 + 64, q * 128 : q * 128 + 128]
            if kind == 0:
                target, place = (low, lon) if lon < 4 else (high, lon - 4)
                target[place] = value
            else:
                final_static[pl.ds(lon, 64, stride=8), :] = value


def weights_kernel(scales, before, own, after, weights, kappa):
    marks = jnp.concatenate([before[...], own[...].astype(f32), after[...]], axis=0)
    lane = iota((16, 128), 1)
    for kind in range(2):
        value = jnp.zeros((24, 128), f32)
        for entry in range(8):
            value = jnp.where(marks == float(entry), scales[kind * 8 + entry], value)
        kappa[kind] = value
        centre = kappa[kind, 4:20]
        east = 0.5 * (centre + kappa[kind, 5:21])
        west = 0.5 * (kappa[kind, 3:19] + centre)
        north = jnp.where(lane < 127, 0.5 * (centre + pltpu.roll(centre, 127, 1)), 0.0)
        south = jnp.where(lane > 0, 0.5 * (centre + pltpu.roll(centre, 1, 1)), 0.0)
        weights[kind, 0] = east
        weights[kind, 1] = west
        weights[kind, 2] = north
        weights[kind, 3] = south
        weights[kind, 4] = 1.0 / (1.0 + east + west + north + south)


def neighbours(field, i, weight):
    return (
        weight(0, i) * field[i + 1]
        + weight(1, i) * field[i - 1]
        + weight(2, i) * pltpu.roll(field[i], 127, 1)
        + weight(3, i) * pltpu.roll(field[i], 1, 1)
    )


def diffuse(source, weight):
    current = dict(enumerate(source))
    for sweep in range(NSWEEP):
        current = {
            i: weight(4, i) * (source[i] + neighbours(current, i, weight))
            for i in range(sweep + 1, 15 - sweep)
        }
    return current


def diffuse_transposed(source, weight):
    carried = dict(enumerate(source))
    total = None
    for sweep in range(NSWEEP):
        scaled = {i: weight(4, i) * carried[i] for i in range(sweep, 16 - sweep)}
        total = {i: scaled[i] if total is None else total[i] + scaled[i] for i in range(4, 12)}
        carried = {i: neighbours(scaled, i, weight) for i in range(sweep + 1, 15 - sweep)}
    return {i: total[i] + carried[i] for i in range(4, 12)}


def weight_of(weights, kind):
    return lambda which, i: weights[kind, which, i : i + 1, :]


def wide_loader(before, low, high, after):
    parts = (before, low, high, after)
    return lambda rows: [parts[i // 4][i % 4, rows, :] for i in range(16)]


def members_kernel(ens, ens_before, ens_after, perts, weights, out):

    def ens_at(rows):
        return (
            [ens_before[pl.ds(i * 64 + rows, 8), :] for i in range(4)]
            + [ens[i, pl.ds(rows, 8), :] for i in range(8)]
            + [ens_after[pl.ds(i * 64 + rows, 8), :] for i in range(4)]
        )

    def levels(step, carry):
        base = pl.multiple_of(step * 8, 8)
        members = [diffuse(ens_at(e * 32 + base), weight_of(weights, 1)) for e in range(2)]
        for var in range(2):
            for lon in range(8):
                total = sum(
                    perts[lon, pl.ds((e * 2 + var) * 32 + base, 8), :] * members[e][lon + 4] for e in range(2)
                )
                out[lon, pl.ds(var * 32 + base, 8), :] = beta_ensemble * total
        return carry

    lax.fori_loop(0, 4, levels, 0)


def increments(loader, members, weights, target):

    def levels(step, carry):
        for var in range(2):
            rows = pl.ds(pl.multiple_of(var * 32 + step * 8, 8), 8)
            smooth = diffuse(loader(rows), weight_of(weights, 0))
            for lon in range(8):
                target[lon, rows, :] = beta_static * smooth[lon + 4] + members[lon, rows, :]
        return carry

    lax.fori_loop(0, 4, levels, 0)


def slot_columns(high, low, start, count, half):
    row = iota((count, 64), 0) + start
    repeat = one_hot((row >> 4) == iota((count, 64), 1))
    spread = 32.0 * dot_nn(repeat, high) + dot_nn(repeat, low)
    place = (iota((count, 128), 0) & 15) + half * 16
    return jnp.sum(jnp.where(iota((count, 128), 1) == place, spread, 0.0), axis=1, keepdims=True).astype(i32) - 1


def observe_kernel(request, low, high, before, after, members, weights, out, field, terms):
    increments(wide_loader(before, low, high, after), members, weights, field)
    for q in range(4):
        pair = jnp.concatenate([field[2 * q], field[2 * q + 1]], axis=1)
        terms[q] = jnp.concatenate(split(pair), axis=0)
    wanted = request[...]
    first, second = (wanted >> 5).astype(f32).astype(bf16), (wanted & 31).astype(f32).astype(bf16)
    wide = iota((512, 256), 1)

    def block(step, carry):
        start = pl.multiple_of(step * 512, 512)
        sums = []
        for half in range(2):
            column = slot_columns(first, second, start, 512, half)
            total = sum(dot_nt(one_hot(column - q * 256 == wide), terms[q]) for q in range(4))
            sums.append(total + pltpu.roll(total, 64, 1))
        out[pl.ds(start, 512), :] = jnp.where(iota((512, 128), 1) < 64, sums[0], sums[1])
        return carry

    lax.fori_loop(0, 2, block, 0)


def last_kernel(low, high, before, after, members, weights, ens, out, final_ens, field):
    increments(wide_loader(before, low, high, after), members, weights, field)
    for lon in range(8):
        out[pl.ds(lon, 64, stride=8), :] = field[lon]
        final_ens[pl.ds(lon, 64, stride=8), :] = ens[lon]


def operators_kernel(here, arrived, jacobians, weights, targets, out, columns, pulled):
    z = here[0]
    lane = iota((256, 128), 1) < 64
    for pair in range(2):
        even, odd = arrived[pair * 512 : pair * 512 + 256], arrived[pair * 512 + 256 : pair * 512 + 512]
        lanes = slice(pair * 128, pair * 128 + 128)
        columns[0, :, lanes] = jnp.where(lane, even, pltpu.roll(odd, 64, 1))
        columns[1, :, lanes] = jnp.where(lane, pltpu.roll(even, 64, 1), odd)

    def tile(u, carry):
        for half in range(2):
            j = lax.rem(z + half, 2)
            rows = pl.ds(pl.multiple_of((half * 8 + u) * 16, 16), 16)
            operator = jnp.concatenate(
                [jacobians[u, j, lax.bitwise_xor(lax.div(z, 2), l)] for l in range(4)], axis=0
            )
            values = jnp.concatenate([columns[0, rows, :], columns[1, rows, :]], axis=0)
            observed = three(dot_nn, values, operator)
            departure = weights[half * 8 + u] * (observed - targets[half * 8 + u])
            back = three(dot_nt, departure, operator)
            pulled[0, rows, :] = back[:16]
            pulled[1, rows, :] = back[16:]
        return carry

    lax.fori_loop(0, 8, tile, 0)
    for pair in range(2):
        lanes = slice(pair * 128, pair * 128 + 128)
        first, second = pulled[0, :, lanes], pulled[1, :, lanes]
        out[pair * 512 : pair * 512 + 256] = jnp.where(lane, first, pltpu.roll(second, 64, 1))
        out[pair * 512 + 256 : pair * 512 + 512] = jnp.where(lane, pltpu.roll(first, 64, 1), second)


def collect_kernel(request, arrived, perts, low, high, turned):
    value = arrived[...]
    first = value.astype(bf16).astype(f32)
    rest = value - first
    lane = iota((1024, 128), 1) < 64
    stacked = jnp.concatenate(
        [
            jnp.where(lane, first, pltpu.roll(rest, 64, 1)),
            jnp.where(lane, pltpu.roll(first, 64, 1), rest),
        ],
        axis=0,
    )
    turned[...] = stacked.T.astype(bf16)
    wanted = request[...]
    upper, lower = (wanted >> 5).astype(f32).astype(bf16), (wanted & 31).astype(f32).astype(bf16)
    columns = [slot_columns(upper, lower, 0, 1024, half) for half in range(2)]
    wide = iota((1024, 256), 1)
    for q in range(4):
        hits = jnp.concatenate([one_hot(columns[half] - q * 256 == wide) for half in range(2)], axis=0)
        both = dot_nn(turned[...], hits)
        total = both[:64] + both[64:]
        target = low if q < 2 else high
        for side in range(2):
            place = (q % 2) * 2 + side
            gradient = total[:, side * 128 : side * 128 + 128]
            target[place, 0:64] = gradient
            factor = perts[2 * q + side]
            for e in range(2):
                mixed = factor[e * 64 : e * 64 + 32] * gradient[:32] + factor[e * 64 + 32 : e * 64 + 64] * gradient[32:]
                target[place, 64 + e * 32 : 96 + e * 32] = beta_ensemble * mixed


def pull_kernel(owner, low, high, before, after, weights, packed, field):
    loader = wide_loader(before, low, high, after)

    def levels(step, carry):
        for var in range(2):
            rows = pl.ds(pl.multiple_of(var * 32 + step * 8, 8), 8)
            smooth = diffuse_transposed([beta_static * value for value in loader(rows)], weight_of(weights, 0))
            for lon in range(8):
                field[lon, rows, :] = smooth[lon + 4]
        return carry

    lax.fori_loop(0, 4, levels, 0)
    packed[...] = pack(lambda q: field[2 * q : 2 * q + 2].reshape(128, 128), owner[...])


def pull_members_kernel(low, high, before, after, ens, weights, new_ens, new_low, new_high):
    loader = wide_loader(before, low, high, after)

    def levels(step, carry):
        for e in range(2):
            base = pl.multiple_of(e * 32 + step * 8, 8)
            smooth = diffuse_transposed(loader(pl.ds(64 + base, 8)), weight_of(weights, 1))
            for lon in range(8):
                value = (1.0 - step_length) * ens[lon, pl.ds(base, 8), :] - step_length * smooth[lon + 4]
                new_ens[lon, pl.ds(base, 8), :] = value
                if lon < 4:
                    new_low[pl.ds(lon * 64 + base, 8), :] = value
                else:
                    new_high[pl.ds((lon - 4) * 64 + base, 8), :] = value
        return carry

    lax.fori_loop(0, 4, levels, 0)


def on_device(
    control_static,
    control_ens,
    ens_perts,
    band_sqrt,
    band_owner,
    scale_class,
    static_scales,
    local_scales,
    obs_source,
    obs_column,
    obs_jac,
    innovation,
    obs_weight,
):
    tiles = 64
    upward = [(i, (i + 1) % tiles) for i in range(tiles)]
    downward = [(i, (i - 1) % tiles) for i in range(tiles)]

    def to_plane(value):
        return lax.all_to_all(value, PLANE, 0, 0, tiled=True)

    def to_levels(value):
        return lax.all_to_all(value, LEV, 0, 0, tiled=True)

    here = jnp.stack([lax.axis_index("z"), lax.axis_index("yh") * 2 + lax.axis_index("core")]).astype(i32)
    scales = jnp.concatenate([static_scales, local_scales])
    owner = jnp.repeat(band_owner, 2).reshape(1, 128)

    shared = jnp.concatenate(
        [band_sqrt.reshape(64, 128), jnp.transpose(obs_jac, (0, 2, 3, 1)).reshape(64, 128)], axis=0
    )
    swap = [(0, 1), (1, 0)]
    shared = jnp.concatenate([shared, lax.ppermute(shared, "core", swap)], axis=0)
    shared = jnp.concatenate([shared, lax.ppermute(shared, "yh", swap)], axis=0)
    exchange = [(z * 4 + l, (2 * l + (j + z) % 2) * 4 + z // 2) for j in range(2) for z in range(8) for l in range(4)]

    def spread(value, j):
        return lax.ppermute(value, ("z",) + LEV, exchange[j * 32 : j * 32 + 32])

    matrices = [spread(shared, j) for j in range(2)]
    jacobians = jnp.stack([part.reshape(4, 128, 128)[:, 64:] for part in matrices]).reshape(512, 128)
    jacobians = lax.all_gather(jacobians, ("yl", "x"), axis=0, tiled=True).reshape(8, 2, 4, 64, 128)

    (packed,) = call(begin_kernel, [((512, 128), f32)], [((8, 64, 128), f32)], total=2)(
        owner, control_static.reshape(512, 128)
    )
    arrived = to_plane(packed)
    source_row, arrived, control_ens = lax.optimization_barrier((obs_source.reshape(1, 512), arrived, control_ens))

    send_up, send_down, ens, perts = call(
        begin_members_kernel,
        [((264, 128), f32), ((264, 128), f32), ((8, 64, 128), f32), ((8, 128, 128), f32)],
        [((1024, 128), f32)],
        total=3,
    )(control_ens.reshape(512, 128), ens_perts.reshape(128, 8, 128), scale_class)
    from_before = lax.ppermute(send_up, TILE, upward)
    from_after = lax.ppermute(send_down, TILE, downward)
    ens_before, marks_before = from_before[:256], from_before[256:]
    ens_after, marks_after = from_after[:256], from_after[256:]

    request, ranks = call(request_kernel, [((64, 128), f32), ((1, 512), i32)], total=2)(
        source_row, obs_column.reshape(1, 512)
    )
    slots = call(slots_kernel, [((512, 128), f32), ((512, 128), f32)], smem=1, total=5)(
        here, source_row, ranks, obs_weight, innovation
    )
    sent = jnp.concatenate(
        [spread(slots[j], j).reshape(64, 8, 128) for j in range(2)]
        + [jnp.pad(request.reshape(64, 1, 128), ((0, 0), (0, 7), (0, 0)))],
        axis=1,
    ).reshape(1536, 128)
    orders = lax.all_to_all(sent, TILE, 0, 0, tiled=True)
    arrived, orders = lax.optimization_barrier((arrived, orders))
    wanted, weights, targets = call(
        arrange_kernel, [((64, 128), i32), ((16, 32, 128), f32), ((16, 32, 128), f32)], total=1
    )(orders)

    state, out = call(
        first_columns_kernel,
        [((4, 128, 128), f32), ((512, 128), f32)],
        [((4, 128, 128), f32)],
        smem=1,
        total=4,
    )(here, arrived, *matrices)

    (faces,) = call(weights_kernel, [((2, 5, 16, 128), f32)], [((2, 24, 128), f32)], smem=1, total=4)(
        scales, marks_before, scale_class, marks_after
    )

    half_shape = ((4, 64, 128), f32)
    mixed_shape = ((4, 128, 128), f32)
    scratch = ((8, 64, 128), f32)

    def halos(low, high):
        return lax.ppermute(high, TILE, upward), lax.ppermute(low, TILE, downward)

    def members_of(ens, ens_before, ens_after):
        return call(members_kernel, [((8, 64, 128), f32)], total=5)(ens, ens_before, ens_after, perts, faces)[0]

    for iteration in range(ITERS):
        low, high = call(edges_kernel, [half_shape, half_shape], total=2)(owner, to_plane(out))
        before, after = halos(low, high)
        members = members_of(ens, ens_before, ens_after)
        (outgoing,) = call(
            observe_kernel, [((1024, 128), f32)], [scratch, ((4, 128, 256), bf16)], total=7
        )(wanted, low, high, before, after, members, faces)
        (returned,) = call(
            operators_kernel,
            [((1024, 128), f32)],
            [((2, 256, 256), f32), ((2, 256, 256), f32)],
            smem=1,
            total=5,
        )(here, to_levels(outgoing), jacobians, weights, targets)
        low, high = call(collect_kernel, [mixed_shape, mixed_shape], [((128, 2048), bf16)], total=3)(
            wanted, to_levels(returned), perts
        )
        before, after = halos(low, high)
        (packed,) = call(pull_kernel, [((512, 128), f32)], [scratch], total=6)(owner, low, high, before, after, faces)
        ens, ens_low, ens_high = call(
            pull_members_kernel, [((8, 64, 128), f32), ((256, 128), f32), ((256, 128), f32)], total=6
        )(low, high, before, after, ens, faces)
        ens_before = lax.ppermute(ens_high, TILE, upward)
        ens_after = lax.ppermute(ens_low, TILE, downward)
        last = iteration == ITERS - 1
        results = call(
            functools.partial(columns_kernel, last),
            [((1024, 128), f32)] if last else [((4, 128, 128), f32), ((512, 128), f32)],
            [((4, 128, 128), f32)],
            smem=1,
            total=5,
        )(here, to_plane(packed), *matrices, state)
        if not last:
            state = results[0]
        out = results[-1]

    low, high, final_static = call(last_edges_kernel, [half_shape, half_shape, ((512, 128), f32)], total=2)(
        owner, to_plane(out)
    )
    before, after = halos(low, high)
    members = members_of(ens, ens_before, ens_after)
    analysis, final_ens = call(last_kernel, [((512, 128), f32), ((512, 128), f32)], [scratch], total=7)(
        low, high, before, after, members, faces, ens
    )
    return tuple(value.reshape(2, 32, 8, 128) for value in (analysis, final_static, final_ens))


def solution(mesh):
    physical = Mesh(mesh.devices.reshape(8, 2, 4, 2, 2), AXES)
    return jax.shard_map(
        on_device,
        mesh=physical,
        in_specs=(
            P(None, LEV, TILE, None),
            P(None, LEV, TILE, None),
            P(None, None, LEV, TILE, None),
            P(TILE, None, LEV, None),
            P(),
            P(TILE, None),
            P(),
            P(),
            P(TILE, None),
            P(TILE),
            P(TILE, None, None, LEV),
            P(None, TILE),
            P(None, TILE),
        ),
        out_specs=(
            P(None, LEV, TILE, None),
            P(None, LEV, TILE, None),
            P(None, LEV, TILE, None),
        ),
        check_vma=False,
    )
```

profile of v0, /device:TPU:46, one launch (start us, length us, event | category | flops | bytes accessed | tf_op | source)
XLA Modules:
  0.0 353.2 jit_solution(17079879658918531805)
XLA Ops:
  12.6 4.8 %collective-permute-done.3 = f32[256,128]{1,0:T(8,128)S(1)} collective-permute-done((f32[256,128]{1,0:T(8,128)S(1)}, f32[256,128]{1,0:T(8,128)S(1)}, u32[]{:S(2)}, u32[]{:S(2)}) %collective-permute-start.3) | collective-permute-done | bytes 131104 | tf_op jit(solution)/shard_map/ppermute | solution.py:524
  19.0 6.2 %collective-permute-done.5.second = f32[512,128]{1,0:T(8,128)S(1)} collective-permute-done((f32[512,128]{1,0:T(8,128)S(1)}, f32[512,128]{1,0:T(8,128)S(1)}, u32[]{:S(2)}, u32[]{:S(2)}) %collective-permute-start.5) | collective-permute-done | bytes 262176 | tf_op jit(solution)/shard_map/ppermute | solution.py:528
  27.4 30.3 %all-to-all-start = ((f32[32,16,128]{2,1,0:T(8,128)}), f32[32,16,128]{2,1,0:T(8,128)S(1)}, u32[]{:S(2)}, u32[]{:S(2)}) async-start(f32[32,16,128]{2,1,0:T(8,128)} %bitcast.4), calls=%async_computation | async-start | bytes 524288 | tf_op jit(solution)/shard_map/all_to_all | solution.py:510
  57.8 7.1 %all-to-all-done = f32[32,16,128]{2,1,0:T(8,128)S(1)} async-done(((f32[32,16,128]{2,1,0:T(8,128)}), f32[32,16,128]{2,1,0:T(8,128)S(1)}, u32[]{:S(2)}, u32[]{:S(2)}) %all-to-all-start) | async-done | bytes 262176 | tf_op jit(solution)/shard_map/all_to_all | solution.py:510
  68.1 6.3 %collective-permute-done.1 = f32[512,128]{1,0:T(8,128)S(1)} collective-permute-done((f32[512,128]{1,0:T(8,128)S(1)}, f32[512,128]{1,0:T(8,128)S(1)}, u32[]{:S(2)}, u32[]{:S(2)}) %collective-permute-start.1) | collective-permute-done | bytes 262176 | tf_op jit(solution)/shard_map/ppermute | solution.py:528
  75.1 55.3 %all_to_all.120 = f32[64,24,128]{2,1,0:T(8,128)S(1)} all-to-all(f32[64,24,128]{2,1,0:T(8,128)S(1)} %copy.24), channel_id=1, replica_groups=mesh['z'=8,'yl'=2,'x'=4,'yh'=2,'core'=2] {'z','yl','x'}, dimensions={0} | all-to-all | bytes 1572864 | tf_op jit(solution)/shard_map/all_to_all | solution.py:562
  132.4 6.3 %all-to-all-start.2 = ((f32[32,16,128]{2,1,0:T(8,128)}), f32[32,16,128]{2,1,0:T(8,128)S(1)}, u32[]{:S(2)}, u32[]{:S(2)}) async-start(f32[32,16,128]{2,1,0:T(8,128)} %bitcast.15), calls=%async_computation.2 | async-start | bytes 524288 | tf_op jit(solution)/shard_map/all_to_all | solution.py:510
  141.0 4.1 %all-to-all-done.2 = f32[32,16,128]{2,1,0:T(8,128)S(1)} async-done(((f32[32,16,128]{2,1,0:T(8,128)}), f32[32,16,128]{2,1,0:T(8,128)S(1)}, u32[]{:S(2)}, u32[]{:S(2)}) %all-to-all-start.2) | async-done | bytes 262176 | tf_op jit(solution)/shard_map/all_to_all | solution.py:510
  145.5 5.0 %collective-permute-start.6 = (f32[4,64,128]{2,1,0:T(8,128)S(1)}, f32[4,64,128]{2,1,0:T(8,128)S(1)}, u32[]{:S(2)}, u32[]{:S(2)}) collective-permute-start(f32[4,64,128]{2,1,0:T(8,128)S(1)} %get-tuple-element.53.high), channel_id=1, source_target_pairs={{0,4},{4,8},{8,12},{12,16},{16,20},{20,24},{24,28},{28,32},{32,36}... | collective-permute-start | bytes 393224 | tf_op jit(solution)/shard_map/ppermute | solution.py:585
  154.7 4.2 %collective-permute-done.7.after = f32[4,64,128]{2,1,0:T(8,128)S(1)} collective-permute-done((f32[4,64,128]{2,1,0:T(8,128)S(1)}, f32[4,64,128]{2,1,0:T(8,128)S(1)}, u32[]{:S(2)}, u32[]{:S(2)}) %collective-permute-start.7) | collective-permute-done | bytes 131104 | tf_op jit(solution)/shard_map/ppermute | solution.py:585
  158.8 3.7 %shard_map.157 = f32[1024,128]{1,0:T(8,128)S(1)} custom-call(s32[64,128]{1,0:T(8,128)S(1)} %get-tuple-element.49.request, f32[4,64,128]{2,1,0:T(8,128)S(1)} %get-tuple-element.52.low, f32[4,64,128]{2,1,0:T(8,128)S(1)} %get-tuple-element.53.high, f32[4,64,128]{2,1,0:T(8,128)S(1)} %collective-permute-done.6.before, ...), custom_call_target="tpu_custom_call" | custom-call | flops 100000000 | bytes 6000000 | tf_op jit(solution)/shard_map/pallas_call | solution.py:594
  162.5 12.7 %all_to_all.121 = f32[4,256,128]{2,1,0:T(8,128)S(1)} all-to-all(f32[4,256,128]{2,1,0:T(8,128)S(1)} %bitcast.55), channel_id=1, replica_groups=mesh['z'=8,'yl'=2,'x'=4,'yh'=2,'core'=2] {'yh','core'}, dimensions={0} | all-to-all | bytes 1048576 | tf_op jit(solution)/shard_map/all_to_all | solution.py:513
  176.9 4.1 %shard_map.158 = f32[1024,128]{1,0:T(8,128)S(1)} custom-call(s32[2]{0:T(128)S(1)} %pad_add_fusion.here, f32[1024,128]{1,0:T(8,128)S(1)} %bitcast.54, f32[8,2,4,64,128]{4,3,2,1,0:T(8,128)S(1)} %bitcast.46, f32[16,32,128]{2,1,0:T(8,128)S(1)} %get-tuple-element.59.weights, f32[16,32,128]{2,1,0:T(8,128)S(1)} %get-tuple-element.60.targets), custom_call_target="tpu_custom_call" | custom-call | flops 100000000 | bytes 6000000 | tf_op jit(solution)/shard_map/pallas_call | solution.py:597
  181.0 12.7 %all_to_all.122 = f32[4,256,128]{2,1,0:T(8,128)S(1)} all-to-all(f32[4,256,128]{2,1,0:T(8,128)S(1)} %bitcast.59), channel_id=1, replica_groups=mesh['z'=8,'yl'=2,'x'=4,'yh'=2,'core'=2] {'yh','core'}, dimensions={0} | all-to-all | bytes 1048576 | tf_op jit(solution)/shard_map/all_to_all | solution.py:513
  198.3 5.7 %collective-permute-done.10.before = f32[4,128,128]{2,1,0:T(8,128)S(1)} collective-permute-done((f32[4,128,128]{2,1,0:T(8,128)S(1)}, f32[4,128,128]{2,1,0:T(8,128)S(1)}, u32[]{:S(2)}, u32[]{:S(2)}) %collective-permute-start.10) | collective-permute-done | bytes 262176 | tf_op jit(solution)/shard_map/ppermute | solution.py:585
  204.0 3.8 %collective-permute-done.11.after = f32[4,128,128]{2,1,0:T(8,128)S(1)} collective-permute-done((f32[4,128,128]{2,1,0:T(8,128)S(1)}, f32[4,128,128]{2,1,0:T(8,128)S(1)}, u32[]{:S(2)}, u32[]{:S(2)}) %collective-permute-start.11) | collective-permute-done | bytes 262176 | tf_op jit(solution)/shard_map/ppermute | solution.py:585
  209.9 11.3 %all_to_all.123 = f32[32,16,128]{2,1,0:T(8,128)S(1)} all-to-all(f32[32,16,128]{2,1,0:T(8,128)S(1)} %bitcast.60), channel_id=1, replica_groups=mesh['z'=8,'yl'=2,'x'=4,'yh'=2,'core'=2] {'yl','x','yh','core'}, dimensions={0} | all-to-all | bytes 524288 | tf_op jit(solution)/shard_map/all_to_all | solution.py:510
  224.2 7.0 %all-to-all-start.6 = ((f32[32,16,128]{2,1,0:T(8,128)}), f32[32,16,128]{2,1,0:T(8,128)S(1)}, u32[]{:S(2)}, u32[]{:S(2)}) async-start(f32[32,16,128]{2,1,0:T(8,128)} %bitcast.31), calls=%async_computation.6 | async-start | bytes 524288 | tf_op jit(solution)/shard_map/all_to_all | solution.py:510
  237.6 3.5 collective-permute-start.12
  244.1 5.2 %collective-permute-done.13.after = f32[4,64,128]{2,1,0:T(8,128)S(1)} collective-permute-done((f32[4,64,128]{2,1,0:T(8,128)S(1)}, f32[4,64,128]{2,1,0:T(8,128)S(1)}, u32[]{:S(2)}, u32[]{:S(2)}) %collective-permute-start.13) | collective-permute-done | bytes 131104 | tf_op jit(solution)/shard_map/ppermute | solution.py:585
  249.3 3.7 %shard_map.165 = f32[1024,128]{1,0:T(8,128)S(1)} custom-call(s32[64,128]{1,0:T(8,128)S(1)} %get-tuple-element.49.request, f32[4,64,128]{2,1,0:T(8,128)S(1)} %get-tuple-element.65.low, f32[4,64,128]{2,1,0:T(8,128)S(1)} %get-tuple-element.66.high, f32[4,64,128]{2,1,0:T(8,128)S(1)} %collective-permute-done.12.before, ...), custom_call_target="tpu_custom_call" | custom-call | flops 100000000 | bytes 6000000 | tf_op jit(solution)/shard_map/pallas_call | solution.py:594
  253.0 12.7 %all_to_all.124 = f32[4,256,128]{2,1,0:T(8,128)S(1)} all-to-all(f32[4,256,128]{2,1,0:T(8,128)S(1)} %bitcast.56), channel_id=1, replica_groups=mesh['z'=8,'yl'=2,'x'=4,'yh'=2,'core'=2] {'yh','core'}, dimensions={0} | all-to-all | bytes 1048576 | tf_op jit(solution)/shard_map/all_to_all | solution.py:513
  265.8 4.1 %shard_map.166 = f32[1024,128]{1,0:T(8,128)S(1)} custom-call(s32[2]{0:T(128)S(1)} %pad_add_fusion.here, f32[1024,128]{1,0:T(8,128)S(1)} %bitcast.57, f32[8,2,4,64,128]{4,3,2,1,0:T(8,128)S(1)} %bitcast.47, f32[16,32,128]{2,1,0:T(8,128)S(1)} %get-tuple-element.59.weights, f32[16,32,128]{2,1,0:T(8,128)S(1)} %get-tuple-element.60.targets), custom_call_target="tpu_custom_call" | custom-call | flops 100000000 | bytes 6000000 | tf_op jit(solution)/shard_map/pallas_call | solution.py:597
  269.9 12.9 %all_to_all.125 = f32[4,256,128]{2,1,0:T(8,128)S(1)} all-to-all(f32[4,256,128]{2,1,0:T(8,128)S(1)} %bitcast.58), channel_id=1, replica_groups=mesh['z'=8,'yl'=2,'x'=4,'yh'=2,'core'=2] {'yh','core'}, dimensions={0} | all-to-all | bytes 1048576 | tf_op jit(solution)/shard_map/all_to_all | solution.py:513
  287.4 5.7 %collective-permute-done.16.before = f32[4,128,128]{2,1,0:T(8,128)S(1)} collective-permute-done((f32[4,128,128]{2,1,0:T(8,128)S(1)}, f32[4,128,128]{2,1,0:T(8,128)S(1)}, u32[]{:S(2)}, u32[]{:S(2)}) %collective-permute-start.16) | collective-permute-done | bytes 262176 | tf_op jit(solution)/shard_map/ppermute | solution.py:585
  293.0 3.1 collective-permute-done.17.after
  298.2 11.3 %all_to_all.126 = f32[32,16,128]{2,1,0:T(8,128)S(1)} all-to-all(f32[32,16,128]{2,1,0:T(8,128)S(1)} %bitcast.61), channel_id=1, replica_groups=mesh['z'=8,'yl'=2,'x'=4,'yh'=2,'core'=2] {'yl','x','yh','core'}, dimensions={0} | all-to-all | bytes 524288 | tf_op jit(solution)/shard_map/all_to_all | solution.py:510
  311.9 7.1 %all-to-all-start.10 = ((f32[32,32,128]{2,1,0:T(8,128)}), f32[32,32,128]{2,1,0:T(8,128)S(1)}, u32[]{:S(2)}, u32[]{:S(2)}) async-start(f32[32,32,128]{2,1,0:T(8,128)} %bitcast.39), calls=%async_computation.10 | async-start | bytes 1048576 | tf_op jit(solution)/shard_map/all_to_all | solution.py:510
  322.7 5.3 %all-to-all-done.10 = f32[32,32,128]{2,1,0:T(8,128)S(1)} async-done(((f32[32,32,128]{2,1,0:T(8,128)}), f32[32,32,128]{2,1,0:T(8,128)S(1)}, u32[]{:S(2)}, u32[]{:S(2)}) %all-to-all-start.10) | async-done | bytes 524320 | tf_op jit(solution)/shard_map/all_to_all | solution.py:510
  329.4 5.2 %collective-permute-start.18 = (f32[4,64,128]{2,1,0:T(8,128)S(1)}, f32[4,64,128]{2,1,0:T(8,128)S(1)}, u32[]{:S(2)}, u32[]{:S(2)}) collective-permute-start(f32[4,64,128]{2,1,0:T(8,128)S(1)} %get-tuple-element.74.high), channel_id=1, source_target_pairs={{0,4},{4,8},{8,12},{12,16},{16,20},{20,24},{24,28},{28,32},{32,36}... | collective-permute-start | bytes 393224 | tf_op jit(solution)/shard_map/ppermute | solution.py:585
  338.6 5.2 %collective-permute-done.19.after = f32[4,64,128]{2,1,0:T(8,128)S(1)} collective-permute-done((f32[4,64,128]{2,1,0:T(8,128)S(1)}, f32[4,64,128]{2,1,0:T(8,128)S(1)}, u32[]{:S(2)}, u32[]{:S(2)}) %collective-permute-start.19) | collective-permute-done | bytes 131104 | tf_op jit(solution)/shard_map/ppermute | solution.py:585
  343.8 2.6 shard_map.173
  (104 shorter events, 60.7 us)
Async XLA Ops:
  7.2 168.1 %all-gather.2.cloned.1.call-start = ((), (), s32[]{:S(2)}) async-start(), calls=%async_computation.11 | async-start | bytes 2359296 | tf_op jit(solution)/shard_map/all_gather | solution.py:532
  8.1 1.3 collective-permute-start.2
  10.2 7.2 %collective-permute-start.3 = (f32[256,128]{1,0:T(8,128)S(1)}, f32[256,128]{1,0:T(8,128)S(1)}, u32[]{:S(2)}, u32[]{:S(2)}) collective-permute-start(f32[256,128]{1,0:T(8,128)S(1)} %pad_maximum_fusion.2), channel_id=1, source_target_pairs={{0,2},{2,0},{1,3},{3,1},{4,6},{6,4},{5,7},{7,5},{8,10},{10,8},{9,1... | collective-permute-start | bytes 393224 | tf_op jit(solution)/shard_map/ppermute | solution.py:524
  18.1 7.1 %collective-permute-start.5 = (f32[512,128]{1,0:T(8,128)S(1)}, f32[512,128]{1,0:T(8,128)S(1)}, u32[]{:S(2)}, u32[]{:S(2)}) collective-permute-start(f32[512,128]{1,0:T(8,128)S(1)} %pad_maximum_fusion), channel_id=1, source_target_pairs={{0,32},{1,96},{2,160},{3,224},{32,0},{33,64},{34,128},{35,192},{64... | collective-permute-start | bytes 786440 | tf_op jit(solution)/shard_map/ppermute | solution.py:528
  18.3 6.9 %collective-permute-start.4 = (f32[512,128]{1,0:T(8,128)S(1)}, f32[512,128]{1,0:T(8,128)S(1)}, u32[]{:S(2)}, u32[]{:S(2)}) collective-permute-start(f32[512,128]{1,0:T(8,128)S(1)} %pad_maximum_fusion), channel_id=1, source_target_pairs={{0,0},{1,64},{2,128},{3,192},{32,32},{33,96},{34,160},{35,224},{64... | collective-permute-start | bytes 786440 | tf_op jit(solution)/shard_map/ppermute | solution.py:528
  27.4 37.5 %all-to-all-start = ((f32[32,16,128]{2,1,0:T(8,128)}), f32[32,16,128]{2,1,0:T(8,128)S(1)}, u32[]{:S(2)}, u32[]{:S(2)}) async-start(f32[32,16,128]{2,1,0:T(8,128)} %bitcast.4), calls=%async_computation | async-start | bytes 524288 | tf_op jit(solution)/shard_map/all_to_all | solution.py:510
  67.3 0.8 collective-permute-start
  68.0 6.5 %collective-permute-start.1 = (f32[512,128]{1,0:T(8,128)S(1)}, f32[512,128]{1,0:T(8,128)S(1)}, u32[]{:S(2)}, u32[]{:S(2)}) collective-permute-start(f32[512,128]{1,0:T(8,128)S(1)} %get-tuple-element.46), channel_id=1, source_target_pairs={{0,32},{1,96},{2,160},{3,224},{32,0},{33,64},{34,128},{35,192},{64... | collective-permute-start | bytes 786440 | tf_op jit(solution)/shard_map/ppermute | solution.py:528
  74.6 64.1 %copy-start.5 = (f32[2,32,8,128]{3,2,1,0:T(8,128)S(1)}, f32[2,32,8,128]{3,2,1,0:T(8,128)}, u32[]{:S(2)}) copy-start(f32[2,32,8,128]{3,2,1,0:T(8,128)} %param.14) | copy-start | bytes 786436
  74.6 64.1 %copy-start.6 = (bf16[2,2,32,8,128]{4,3,2,1,0:T(8,128)(2,1)S(1)}, bf16[2,2,32,8,128]{4,3,2,1,0:T(8,128)(2,1)}, u32[]{:S(2)}) copy-start(bf16[2,2,32,8,128]{4,3,2,1,0:T(8,128)(2,1)} %param.15) | copy-start | bytes 786436
  74.6 64.1 %copy-start.9 = (s32[8,128]{1,0:T(8,128)S(1)}, s32[8,128]{1,0:T(8,128)}, u32[]{:S(2)}) copy-start(s32[8,128]{1,0:T(8,128)} %own.1) | copy-start | bytes 12292
  75.1 75.4 %copy-start.13 = (f32[8]{0:T(128)S(1)}, f32[8]{0:T(128)}, u32[]{:S(2)}) copy-start(f32[8]{0:T(128)} %param.20) | copy-start | bytes 100
  75.1 75.4 %copy-start.14 = (f32[8]{0:T(128)S(1)}, f32[8]{0:T(128)}, u32[]{:S(2)}) copy-start(f32[8]{0:T(128)} %param.19) | copy-start | bytes 100
  132.4 12.7 %all-to-all-start.2 = ((f32[32,16,128]{2,1,0:T(8,128)}), f32[32,16,128]{2,1,0:T(8,128)S(1)}, u32[]{:S(2)}, u32[]{:S(2)}) async-start(f32[32,16,128]{2,1,0:T(8,128)} %bitcast.15), calls=%async_computation.2 | async-start | bytes 524288 | tf_op jit(solution)/shard_map/all_to_all | solution.py:510
  138.9 11.7 %collective-permute-start.8 = (f32[264,128]{1,0:T(8,128)S(1)}, f32[264,128]{1,0:T(8,128)}, u32[]{:S(2)}, u32[]{:S(2)}) collective-permute-start(f32[264,128]{1,0:T(8,128)S(1)} %get-tuple-element.56), channel_id=1, source_target_pairs={{0,4},{4,8},{8,12},{12,16},{16,20},{20,24},{24,28},{28,32},{32,36}... | collective-permute-start | bytes 405512 | tf_op jit(solution)/shard_map/ppermute | solution.py:546
  139.0 13.2 %collective-permute-start.9 = (f32[264,128]{1,0:T(8,128)S(1)}, f32[264,128]{1,0:T(8,128)S(1)}, u32[]{:S(2)}, u32[]{:S(2)}) collective-permute-start(f32[264,128]{1,0:T(8,128)S(1)} %get-tuple-element.57), channel_id=1, source_target_pairs={{0,252},{4,0},{8,4},{12,8},{16,12},{20,16},{24,20},{28,24},{32,28}... | collective-permute-start | bytes 405512 | tf_op jit(solution)/shard_map/ppermute | solution.py:547
  145.5 9.1 %collective-permute-start.6 = (f32[4,64,128]{2,1,0:T(8,128)S(1)}, f32[4,64,128]{2,1,0:T(8,128)S(1)}, u32[]{:S(2)}, u32[]{:S(2)}) collective-permute-start(f32[4,64,128]{2,1,0:T(8,128)S(1)} %get-tuple-element.53.high), channel_id=1, source_target_pairs={{0,4},{4,8},{8,12},{12,16},{16,20},{20,24},{24,28},{28,32},{32,36}... | collective-permute-start | bytes 393224 | tf_op jit(solution)/shard_map/ppermute | solution.py:585
  150.5 8.4 %collective-permute-start.7 = (f32[4,64,128]{2,1,0:T(8,128)S(1)}, f32[4,64,128]{2,1,0:T(8,128)S(1)}, u32[]{:S(2)}, u32[]{:S(2)}) collective-permute-start(f32[4,64,128]{2,1,0:T(8,128)S(1)} %get-tuple-element.52.low), channel_id=1, source_target_pairs={{0,252},{4,0},{8,4},{12,8},{16,12},{20,16},{24,20},{28,24},{32,28}... | collective-permute-start | bytes 393224 | tf_op jit(solution)/shard_map/ppermute | solution.py:585
  196.2 7.8 %collective-permute-start.10 = (f32[4,128,128]{2,1,0:T(8,128)S(1)}, f32[4,128,128]{2,1,0:T(8,128)S(1)}, u32[]{:S(2)}, u32[]{:S(2)}) collective-permute-start(f32[4,128,128]{2,1,0:T(8,128)S(1)} %get-tuple-element.62.high), channel_id=1, source_target_pairs={{0,4},{4,8},{8,12},{12,16},{16,20},{20,24},{24,28},{28,32},{32,36}... | collective-permute-start | bytes 786440 | tf_op jit(solution)/shard_map/ppermute | solution.py:585
  197.4 10.4 %collective-permute-start.11 = (f32[4,128,128]{2,1,0:T(8,128)S(1)}, f32[4,128,128]{2,1,0:T(8,128)S(1)}, u32[]{:S(2)}, u32[]{:S(2)}) collective-permute-start(f32[4,128,128]{2,1,0:T(8,128)S(1)} %get-tuple-element.61.low), channel_id=1, source_target_pairs={{0,252},{4,0},{8,4},{12,8},{16,12},{20,16},{24,20},{28,24},{32,28}... | collective-permute-start | bytes 786440 | tf_op jit(solution)/shard_map/ppermute | solution.py:585
  224.2 12.9 %all-to-all-start.6 = ((f32[32,16,128]{2,1,0:T(8,128)}), f32[32,16,128]{2,1,0:T(8,128)S(1)}, u32[]{:S(2)}, u32[]{:S(2)}) async-start(f32[32,16,128]{2,1,0:T(8,128)} %bitcast.31), calls=%async_computation.6 | async-start | bytes 524288 | tf_op jit(solution)/shard_map/all_to_all | solution.py:510
  233.6 7.5 %collective-permute-start.14 = (f32[256,128]{1,0:T(8,128)}, f32[256,128]{1,0:T(8,128)S(1)}, u32[]{:S(2)}, u32[]{:S(2)}) collective-permute-start(f32[256,128]{1,0:T(8,128)} %get-tuple-element.68), channel_id=1, source_target_pairs={{0,4},{4,8},{8,12},{12,16},{16,20},{20,24},{24,28},{28,32},{32,36}... | collective-permute-start | bytes 393224 | tf_op jit(solution)/shard_map/ppermute | solution.py:612
  233.9 8.5 %collective-permute-start.15 = (f32[256,128]{1,0:T(8,128)}, f32[256,128]{1,0:T(8,128)S(1)}, u32[]{:S(2)}, u32[]{:S(2)}) collective-permute-start(f32[256,128]{1,0:T(8,128)} %get-tuple-element.69), channel_id=1, source_target_pairs={{0,252},{4,0},{8,4},{12,8},{16,12},{20,16},{24,20},{28,24},{32,28}... | collective-permute-start | bytes 393224 | tf_op jit(solution)/shard_map/ppermute | solution.py:613
  237.6 6.5 %collective-permute-start.12 = (f32[4,64,128]{2,1,0:T(8,128)S(1)}, f32[4,64,128]{2,1,0:T(8,128)S(1)}, u32[]{:S(2)}, u32[]{:S(2)}) collective-permute-start(f32[4,64,128]{2,1,0:T(8,128)S(1)} %get-tuple-element.66.high), channel_id=1, source_target_pairs={{0,4},{4,8},{8,12},{12,16},{16,20},{20,24},{24,28},{28,32},{32,36}... | collective-permute-start | bytes 393224 | tf_op jit(solution)/shard_map/ppermute | solution.py:585
  241.1 8.2 %collective-permute-start.13 = (f32[4,64,128]{2,1,0:T(8,128)S(1)}, f32[4,64,128]{2,1,0:T(8,128)S(1)}, u32[]{:S(2)}, u32[]{:S(2)}) collective-permute-start(f32[4,64,128]{2,1,0:T(8,128)S(1)} %get-tuple-element.65.low), channel_id=1, source_target_pairs={{0,252},{4,0},{8,4},{12,8},{16,12},{20,16},{24,20},{28,24},{32,28}... | collective-permute-start | bytes 393224 | tf_op jit(solution)/shard_map/ppermute | solution.py:585
  285.3 7.8 %collective-permute-start.16 = (f32[4,128,128]{2,1,0:T(8,128)S(1)}, f32[4,128,128]{2,1,0:T(8,128)S(1)}, u32[]{:S(2)}, u32[]{:S(2)}) collective-permute-start(f32[4,128,128]{2,1,0:T(8,128)S(1)} %get-tuple-element.71.high), channel_id=1, source_target_pairs={{0,4},{4,8},{8,12},{12,16},{16,20},{20,24},{24,28},{28,32},{32,36}... | collective-permute-start | bytes 786440 | tf_op jit(solution)/shard_map/ppermute | solution.py:585
  285.6 10.5 %collective-permute-start.17 = (f32[4,128,128]{2,1,0:T(8,128)S(1)}, f32[4,128,128]{2,1,0:T(8,128)S(1)}, u32[]{:S(2)}, u32[]{:S(2)}) collective-permute-start(f32[4,128,128]{2,1,0:T(8,128)S(1)} %get-tuple-element.70.low), channel_id=1, source_target_pairs={{0,252},{4,0},{8,4},{12,8},{16,12},{20,16},{24,20},{28,24},{32,28}... | collective-permute-start | bytes 786440 | tf_op jit(solution)/shard_map/ppermute | solution.py:585
  311.9 16.2 %all-to-all-start.10 = ((f32[32,32,128]{2,1,0:T(8,128)}), f32[32,32,128]{2,1,0:T(8,128)S(1)}, u32[]{:S(2)}, u32[]{:S(2)}) async-start(f32[32,32,128]{2,1,0:T(8,128)} %bitcast.39), calls=%async_computation.10 | async-start | bytes 1048576 | tf_op jit(solution)/shard_map/all_to_all | solution.py:510
  320.6 14.1 %collective-permute-start.20 = (f32[256,128]{1,0:T(8,128)S(1)}, f32[256,128]{1,0:T(8,128)S(1)}, u32[]{:S(2)}, u32[]{:S(2)}) collective-permute-start(f32[256,128]{1,0:T(8,128)S(1)} %get-tuple-element.76), channel_id=1, source_target_pairs={{0,4},{4,8},{8,12},{12,16},{16,20},{20,24},{24,28},{28,32},{32,36}... | collective-permute-start | bytes 393224 | tf_op jit(solution)/shard_map/ppermute | solution.py:612
  321.4 13.3 %collective-permute-start.21 = (f32[256,128]{1,0:T(8,128)S(1)}, f32[256,128]{1,0:T(8,128)S(1)}, u32[]{:S(2)}, u32[]{:S(2)}) collective-permute-start(f32[256,128]{1,0:T(8,128)S(1)} %get-tuple-element.77), channel_id=1, source_target_pairs={{0,252},{4,0},{8,4},{12,8},{16,12},{20,16},{24,20},{28,24},{32,28}... | collective-permute-start | bytes 393224 | tf_op jit(solution)/shard_map/ppermute | solution.py:613
  329.4 9.1 %collective-permute-start.18 = (f32[4,64,128]{2,1,0:T(8,128)S(1)}, f32[4,64,128]{2,1,0:T(8,128)S(1)}, u32[]{:S(2)}, u32[]{:S(2)}) collective-permute-start(f32[4,64,128]{2,1,0:T(8,128)S(1)} %get-tuple-element.74.high), channel_id=1, source_target_pairs={{0,4},{4,8},{8,12},{12,16},{16,20},{20,24},{24,28},{28,32},{32,36}... | collective-permute-start | bytes 393224 | tf_op jit(solution)/shard_map/ppermute | solution.py:585
  334.7 9.1 %collective-permute-start.19 = (f32[4,64,128]{2,1,0:T(8,128)S(1)}, f32[4,64,128]{2,1,0:T(8,128)S(1)}, u32[]{:S(2)}, u32[]{:S(2)}) collective-permute-start(f32[4,64,128]{2,1,0:T(8,128)S(1)} %get-tuple-element.73.low), channel_id=1, source_target_pairs={{0,252},{4,0},{8,4},{12,8},{16,12},{20,16},{24,20},{28,24},{32,28}... | collective-permute-start | bytes 393224 | tf_op jit(solution)/shard_map/ppermute | solution.py:585
  (10 other events, 340.1 us)
Sparse Core Ops, SparseCore 0:
  26.1 69.8 all-gather.1
where the time goes:
time: 357 us; the launch traced here: 353 us
  blocking collectives  129 us (36%)
  starting transfers between devices  78.9 us (22%)
  waiting for transfers between devices  72.8 us (20%)
  Pallas kernels  49.8 us (14%)
  between operations  14.5 us (4%)
  local copies, waits for them, and re-layouts  4.77 us (1%)
    all_to_all x1, blocking collectives, on_device(): orders = lax.all_to_all(sent, TILE, 0, 0, tiled=True)  55.3 us
    all_to_all x4, blocking collectives, to_levels(): return lax.all_to_all(value, LEV, 0, 0, tiled=True)  51.1 us
    all_to_all x4, starting transfers between devices, to_plane(): return lax.all_to_all(value, PLANE, 0, 0, tiled=True)  50.7 us
    ppermute x10, waiting for transfers between devices, halos(): return (lax.ppermute(high, TILE, upward), lax.ppermute(low, TILE, downward))  35 us
    all_to_all x2, blocking collectives, to_plane(): return lax.all_to_all(value, PLANE, 0, 0, tiled=True)  22.5 us
    all_to_all x4, waiting for transfers between devices, to_plane(): return lax.all_to_all(value, PLANE, 0, 0, tiled=True)  18 us
    ppermute x10, starting transfers between devices, halos(): return (lax.ppermute(high, TILE, upward), lax.ppermute(low, TILE, downward))  17.9 us
    ppermute x4, waiting for transfers between devices, spread(): return lax.ppermute(value, ('z',) + LEV, exchange[j * 32:j * 32 + 32])  12.5 us
  transfers between devices with their start and end apart: 27, of which 17 were waited for; matrix products, arithmetic and copies ran while one was open for 1% of the time, Pallas kernels for 6%

commit v1 on v0

--- a/solution.py
+++ b/solution.py
@@ -124,25 +124,14 @@
 def slots_kernel(here, source_row, ranks, weight, innovation, first, second):
     z, level = here[0], here[1]
     source, rank = source_row[...], ranks[...]
-    row = iota((512, 512), 0)
-    place = (row >> 3) == source
-    kind = (row >> 2) & 1
-    terms = split(jnp.concatenate([weight[...], innovation[...]], axis=1))
+    row = iota((256, 512), 0)
+    place = ((row >> 7) & 1) * 16 + (row & 15)
     for j, target in enumerate((first, second)):
-        group = 2 * level + lax.rem(z + j, 2)
-        mine = place & (rank == group * 4 + (row & 3))
-        hits = jnp.concatenate([one_hot(mine & (kind == w)) for w in range(2)], axis=1)
-        target[...] = dot_nt(hits, terms[0]) + dot_nt(hits, terms[1])
-
-
-def arrange_kernel(arrived, wanted, weights, targets):
-    wanted[...] = arrived[pl.ds(16, 64, stride=24), :].astype(i32)
-    for half in range(2):
-        for u in range(8):
-            for z in range(8):
-                start = (z * 8 + u) * 24 + ((half + z) % 2) * 8
-                weights[half * 8 + u, 4 * z : 4 * z + 4] = arrived[start : start + 4]
-                targets[half * 8 + u, 4 * z : 4 * z + 4] = arrived[start + 4 : start + 8]
+        tile = (2 * level + lax.rem(z + j, 2)) * 8 + ((row >> 4) & 7)
+        mine = one_hot((source == tile) & (rank == place))
+        for kind, values in enumerate((weight, innovation)):
+            terms = split(values[...])
+            target[kind * 256 : kind * 256 + 256] = dot_nt(mine, terms[0]) + dot_nt(mine, terms[1])
 
 
 def load_matrices(here, first, second, matrices):
@@ -354,7 +343,8 @@
 
 def slot_columns(high, low, start, count, half):
     row = iota((count, 64), 0) + start
-    repeat = one_hot((row >> 4) == iota((count, 64), 1))
+    tile = ((row >> 4) & 7) * 8 + (row >> 7)
+    repeat = one_hot(tile == iota((count, 64), 1))
     spread = 32.0 * dot_nn(repeat, high) + dot_nn(repeat, low)
     place = (iota((count, 128), 0) & 15) + half * 16
     return jnp.sum(jnp.where(iota((count, 128), 1) == place, spread, 0.0), axis=1, keepdims=True).astype(i32) - 1
@@ -365,7 +355,7 @@
     for q in range(4):
         pair = jnp.concatenate([field[2 * q], field[2 * q + 1]], axis=1)
         terms[q] = jnp.concatenate(split(pair), axis=0)
-    wanted = request[...]
+    wanted = request[...].astype(i32)
     first, second = (wanted >> 5).astype(f32).astype(bf16), (wanted & 31).astype(f32).astype(bf16)
     wide = iota((512, 256), 1)
 
@@ -389,36 +379,38 @@
         final_ens[pl.ds(lon, 64, stride=8), :] = ens[lon]
 
 
-def operators_kernel(here, arrived, jacobians, weights, targets, out, columns, pulled):
+def operators_kernel(here, arrived, first, second, first_slots, second_slots, out, stacked):
     z = here[0]
-    lane = iota((256, 128), 1) < 64
-    for pair in range(2):
-        even, odd = arrived[pair * 512 : pair * 512 + 256], arrived[pair * 512 + 256 : pair * 512 + 512]
-        lanes = slice(pair * 128, pair * 128 + 128)
-        columns[0, :, lanes] = jnp.where(lane, even, pltpu.roll(odd, 64, 1))
-        columns[1, :, lanes] = jnp.where(lane, pltpu.roll(even, 64, 1), odd)
-
-    def tile(u, carry):
-        for half in range(2):
-            j = lax.rem(z + half, 2)
-            rows = pl.ds(pl.multiple_of((half * 8 + u) * 16, 16), 16)
-            operator = jnp.concatenate(
-                [jacobians[u, j, lax.bitwise_xor(lax.div(z, 2), l)] for l in range(4)], axis=0
+    lane = iota((128, 128), 1) < 64
+
+    def start(u, k, half):
+        level = lax.bitwise_xor(lax.div(z, 2), k)
+        return pl.ds(pl.multiple_of((u * 4 + level) * 32 + half * 16, 16), 16)
+
+    for j, (part, slots) in enumerate(((first, first_slots), (second, second_slots))):
+        half = lax.rem(z + j, 2)
+        blocks = [
+            jnp.concatenate([arrived[start(u, k, half), :] for u in range(8)], axis=0) for k in range(4)
+        ]
+        operator = jnp.concatenate([part[k * 128 + 64 : k * 128 + 128] for k in range(4)], axis=0)
+        for pair in range(2):
+            even, odd = blocks[2 * pair], blocks[2 * pair + 1]
+            lanes = slice(pair * 128, pair * 128 + 128)
+            stacked[0:128, lanes] = jnp.where(lane, even, pltpu.roll(odd, 64, 1))
+            stacked[128:256, lanes] = jnp.where(lane, pltpu.roll(even, 64, 1), odd)
+        observed = three(dot_nn, stacked[...], operator)
+        departure = slots[0:256] * (observed - slots[256:512])
+        pulled = three(dot_nt, departure, operator)
+        for pair in range(2):
+            lanes = slice(pair * 128, pair * 128 + 128)
+            upper, lower = pulled[:128, lanes], pulled[128:, lanes]
+            values = (
+                jnp.where(lane, upper, pltpu.roll(lower, 64, 1)),
+                jnp.where(lane, pltpu.roll(upper, 64, 1), lower),
             )
-            values = jnp.concatenate([columns[0, rows, :], columns[1, rows, :]], axis=0)
-            observed = three(dot_nn, values, operator)
-            departure = weights[half * 8 + u] * (observed - targets[half * 8 + u])
-            back = three(dot_nt, departure, operator)
-            pulled[0, rows, :] = back[:16]
-            pulled[1, rows, :] = back[16:]
-        return carry
-
-    lax.fori_loop(0, 8, tile, 0)
-    for pair in range(2):
-        lanes = slice(pair * 128, pair * 128 + 128)
-        first, second = pulled[0, :, lanes], pulled[1, :, lanes]
-        out[pair * 512 : pair * 512 + 256] = jnp.where(lane, first, pltpu.roll(second, 64, 1))
-        out[pair * 512 + 256 : pair * 512 + 512] = jnp.where(lane, pltpu.roll(first, 64, 1), second)
+            for side in range(2):
+                for u in range(8):
+                    out[start(u, 2 * pair + side, half), :] = values[side][u * 16 : u * 16 + 16]
 
 
 def collect_kernel(request, arrived, perts, low, high, turned):
@@ -434,7 +426,7 @@
         axis=0,
     )
     turned[...] = stacked.T.astype(bf16)
-    wanted = request[...]
+    wanted = request[...].astype(i32)
     upper, lower = (wanted >> 5).astype(f32).astype(bf16), (wanted & 31).astype(f32).astype(bf16)
     columns = [slot_columns(upper, lower, 0, 1024, half) for half in range(2)]
     wide = iota((1024, 256), 1)
@@ -509,9 +501,6 @@
     def to_plane(value):
         return lax.all_to_all(value, PLANE, 0, 0, tiled=True)
 
-    def to_levels(value):
-        return lax.all_to_all(value, LEV, 0, 0, tiled=True)
-
     here = jnp.stack([lax.axis_index("z"), lax.axis_index("yh") * 2 + lax.axis_index("core")]).astype(i32)
     scales = jnp.concatenate([static_scales, local_scales])
     owner = jnp.repeat(band_owner, 2).reshape(1, 128)
@@ -528,14 +517,21 @@
         return lax.ppermute(value, ("z",) + LEV, exchange[j * 32 : j * 32 + 32])
 
     matrices = [spread(shared, j) for j in range(2)]
-    jacobians = jnp.stack([part.reshape(4, 128, 128)[:, 64:] for part in matrices]).reshape(512, 128)
-    jacobians = lax.all_gather(jacobians, ("yl", "x"), axis=0, tiled=True).reshape(8, 2, 4, 64, 128)
-
     (packed,) = call(begin_kernel, [((512, 128), f32)], [((8, 64, 128), f32)], total=2)(
         owner, control_static.reshape(512, 128)
     )
     arrived = to_plane(packed)
-    source_row, arrived, control_ens = lax.optimization_barrier((obs_source.reshape(1, 512), arrived, control_ens))
+    source_row = obs_source.reshape(1, 512)
+    request, ranks = call(request_kernel, [((64, 128), f32), ((1, 512), i32)], total=2)(
+        source_row, obs_column.reshape(1, 512)
+    )
+    request, arrived = lax.optimization_barrier((request, arrived))
+    wanted = lax.all_to_all(request, TILE, 0, 0, tiled=True)
+    arrived, wanted, control_ens, ranks = lax.optimization_barrier((arrived, wanted, control_ens, ranks))
+    slots = call(slots_kernel, [((512, 128), f32), ((512, 128), f32)], smem=1, total=5)(
+        here, source_row, ranks, obs_weight, innovation
+    )
+    slots = [spread(slots[j], j) for j in range(2)]
 
     send_up, send_down, ens, perts = call(
         begin_members_kernel,
@@ -548,23 +544,6 @@
     ens_before, marks_before = from_before[:256], from_before[256:]
     ens_after, marks_after = from_after[:256], from_after[256:]
 
-    request, ranks = call(request_kernel, [((64, 128), f32), ((1, 512), i32)], total=2)(
-        source_row, obs_column.reshape(1, 512)
-    )
-    slots = call(slots_kernel, [((512, 128), f32), ((512, 128), f32)], smem=1, total=5)(
-        here, source_row, ranks, obs_weight, innovation
-    )
-    sent = jnp.concatenate(
-        [spread(slots[j], j).reshape(64, 8, 128) for j in range(2)]
-        + [jnp.pad(request.reshape(64, 1, 128), ((0, 0), (0, 7), (0, 0)))],
-        axis=1,
-    ).reshape(1536, 128)
-    orders = lax.all_to_all(sent, TILE, 0, 0, tiled=True)
-    arrived, orders = lax.optimization_barrier((arrived, orders))
-    wanted, weights, targets = call(
-        arrange_kernel, [((64, 128), i32), ((16, 32, 128), f32), ((16, 32, 128), f32)], total=1
-    )(orders)
-
     state, out = call(
         first_columns_kernel,
         [((4, 128, 128), f32), ((512, 128), f32)],
@@ -594,15 +573,11 @@
         (outgoing,) = call(
             observe_kernel, [((1024, 128), f32)], [scratch, ((4, 128, 256), bf16)], total=7
         )(wanted, low, high, before, after, members, faces)
-        (returned,) = call(
-            operators_kernel,
-            [((1024, 128), f32)],
-            [((2, 256, 256), f32), ((2, 256, 256), f32)],
-            smem=1,
-            total=5,
-        )(here, to_levels(outgoing), jacobians, weights, targets)
+        (returned,) = call(operators_kernel, [((1024, 128), f32)], [((256, 256), f32)], smem=1, total=6)(
+            here, to_plane(outgoing), *matrices, *slots
+        )
         low, high = call(collect_kernel, [mixed_shape, mixed_shape], [((128, 2048), bf16)], total=3)(
-            wanted, to_levels(returned), perts
+            wanted, to_plane(returned), perts
         )
         before, after = halos(low, high)
         (packed,) = call(pull_kernel, [((512, 128), f32)], [scratch], total=6)(owner, low, high, before, after, faces)

time: 357 us -> 320 us (0.90)
  blocking collectives: 129 us -> 91.1 us
  starting transfers between devices: 78.9 us -> 101 us
  between operations: 14.5 us -> 1.24 us
  Pallas kernels: 49.8 us -> 45.7 us
    all_to_all x5 -> x0, blocking collectives: 106 us -> none  [the longest x1 55.3 us: on_device(): orders = lax.all_to_all(sent, TILE, 0, 0, tiled=True)]
    all_to_all x2 -> x5, blocking collectives: 22.5 us -> 91.1 us  [to_plane(): return lax.all_to_all(value, PLANE, 0, 0, tiled=True)]
    ppermute x10, starting transfers between devices: 17.9 us -> 38.1 us  [halos(): return (lax.ppermute(high, TILE, upward), lax.ppermute(low, TILE, downward))]
    all_to_all x0 -> x1, starting transfers between devices: none -> 18.3 us  [on_device(): wanted = lax.all_to_all(request, TILE, 0, 0, tiled=True)]
    all_to_all x4 -> x5, starting transfers between devices: 50.7 us -> 32.8 us  [to_plane(): return lax.all_to_all(value, PLANE, 0, 0, tiled=True)]
    all_to_all x0 -> x1, waiting for transfers between devices: none -> 9.14 us  [on_device(): wanted = lax.all_to_all(request, TILE, 0, 0, tiled=True)]
    ppermute x10, waiting for transfers between devices: 35 us -> 41.4 us  [halos(): return (lax.ppermute(high, TILE, upward), lax.ppermute(low, TILE, downward))]
    ppermute x4, waiting for transfers between devices: 12.5 us -> 6.7 us  [spread(): return lax.ppermute(value, ('z',) + LEV, exchange[j * 32:j * 32 + 32])]
  transfers between devices with their start and end apart: 27 -> 28, of which waited for: 17 -> 16; matrix products, arithmetic and copies ran while one was open for 1% -> 0% of each run, Pallas kernels for 6% -> 5%
where the time goes in v1:
time: 320 us; the launch traced here: 315 us
  starting transfers between devices  101 us (32%)
  blocking collectives  91.1 us (28%)
  waiting for transfers between devices  71.6 us (22%)
  Pallas kernels  45.7 us (14%)
    all_to_all x5, blocking collectives, to_plane(): return lax.all_to_all(value, PLANE, 0, 0, tiled=True)  91.1 us
    ppermute x10, waiting for transfers between devices, halos(): return (lax.ppermute(high, TILE, upward), lax.ppermute(low, TILE, downward))  41.4 us
    ppermute x10, starting transfers between devices, halos(): return (lax.ppermute(high, TILE, upward), lax.ppermute(low, TILE, downward))  38.1 us
    all_to_all x5, starting transfers between devices, to_plane(): return lax.all_to_all(value, PLANE, 0, 0, tiled=True)  32.8 us
    all_to_all x1, starting transfers between devices, on_device(): wanted = lax.all_to_all(request, TILE, 0, 0, tiled=True)  18.3 us
    all_to_all x5, waiting for transfers between devices, to_plane(): return lax.all_to_all(value, PLANE, 0, 0, tiled=True)  13.1 us
    all_to_all x1, waiting for transfers between devices, on_device(): wanted = lax.all_to_all(request, TILE, 0, 0, tiled=True)  9.14 us
    pallas_call x2, Pallas kernels, on_device(): call(observe_kernel, [((1024, 128), f32)], [scratch, ((4, 128, 256), bf16...  8.2 us
  transfers between devices with their start and end apart: 28, of which 16 were waited for; matrix products, arithmetic and copies ran while one was open for 0% of the time, Pallas kernels for 5%

profile of v1, /device:TPU:46, one launch (start us, length us, event | category | flops | bytes accessed | tf_op | source)
XLA Modules:
  0.0 315.3 jit_solution(1167034433013298534)
XLA Ops:
  7.4 6.4 %all-to-all-start = ((f32[32,16,128]{2,1,0:T(8,128)}), f32[32,16,128]{2,1,0:T(8,128)S(1)}, u32[]{:S(2)}, u32[]{:S(2)}) async-start(f32[32,16,128]{2,1,0:T(8,128)} %bitcast.5), calls=%async_computation | async-start | bytes 524288 | tf_op jit(solution)/shard_map/all_to_all | solution.py:502
  16.5 3.2 %all-to-all-done = f32[32,16,128]{2,1,0:T(8,128)S(1)} async-done(((f32[32,16,128]{2,1,0:T(8,128)}), f32[32,16,128]{2,1,0:T(8,128)S(1)}, u32[]{:S(2)}, u32[]{:S(2)}) %all-to-all-start) | async-done | bytes 262176 | tf_op jit(solution)/shard_map/all_to_all | solution.py:502
  19.6 18.3 %all-to-all-start.1 = ((f32[64,1,128]{2,1,0:T(1,128)}), f32[64,1,128]{2,1,0:T(1,128)S(1)}, u32[]{:S(2)}, u32[]{:S(2)}) async-start(f32[64,1,128]{2,1,0:T(1,128)} %bitcast.8), calls=%async_computation.1 | async-start | bytes 65536 | tf_op jit(solution)/shard_map/all_to_all | solution.py:529
  38.0 9.1 %all-to-all-done.1 = f32[64,1,128]{2,1,0:T(1,128)S(1)} async-done(((f32[64,1,128]{2,1,0:T(1,128)}), f32[64,1,128]{2,1,0:T(1,128)S(1)}, u32[]{:S(2)}, u32[]{:S(2)}) %all-to-all-start.1) | async-done | bytes 32800 | tf_op jit(solution)/shard_map/all_to_all | solution.py:529
  49.8 6.5 %all-to-all-start.2 = ((f32[32,16,128]{2,1,0:T(8,128)}), f32[32,16,128]{2,1,0:T(8,128)S(1)}, u32[]{:S(2)}, u32[]{:S(2)}) async-start(f32[32,16,128]{2,1,0:T(8,128)} %bitcast.14), calls=%async_computation.2 | async-start | bytes 524288 | tf_op jit(solution)/shard_map/all_to_all | solution.py:502
  58.7 4.1 %all-to-all-done.2 = f32[32,16,128]{2,1,0:T(8,128)S(1)} async-done(((f32[32,16,128]{2,1,0:T(8,128)}), f32[32,16,128]{2,1,0:T(8,128)S(1)}, u32[]{:S(2)}, u32[]{:S(2)}) %all-to-all-start.2) | async-done | bytes 262176 | tf_op jit(solution)/shard_map/all_to_all | solution.py:502
  63.3 6.2 %collective-permute-start.4 = (f32[4,64,128]{2,1,0:T(8,128)S(1)}, f32[4,64,128]{2,1,0:T(8,128)S(1)}, u32[]{:S(2)}, u32[]{:S(2)}) collective-permute-start(f32[4,64,128]{2,1,0:T(8,128)S(1)} %get-tuple-element.48.high), channel_id=1, source_target_pairs={{0,4},{4,8},{8,12},{12,16},{16,20},{20,24},{24,28},{28,32},{32,36}... | collective-permute-start | bytes 393224 | tf_op jit(solution)/shard_map/ppermute | solution.py:564
  72.6 5.2 %collective-permute-done.5.after = f32[4,64,128]{2,1,0:T(8,128)S(1)} collective-permute-done((f32[4,64,128]{2,1,0:T(8,128)S(1)}, f32[4,64,128]{2,1,0:T(8,128)S(1)}, u32[]{:S(2)}, u32[]{:S(2)}) %collective-permute-start.5) | collective-permute-done | bytes 131104 | tf_op jit(solution)/shard_map/ppermute | solution.py:564
  77.8 4.5 %shard_map.155 = f32[1024,128]{1,0:T(8,128)} custom-call(f32[64,128]{1,0:T(8,128)S(1)} %bitcast.51, f32[4,64,128]{2,1,0:T(8,128)S(1)} %get-tuple-element.47.low, f32[4,64,128]{2,1,0:T(8,128)S(1)} %get-tuple-element.48.high, f32[4,64,128]{2,1,0:T(8,128)S(1)} %collective-permute-done.4.before, f32[4,64,128]{2,1,0:T(8,128)S(1)} %collective-permute-done.5.after, ...), custom_call_target="tpu_custom_call" | custom-call | flops 100000000 | bytes 6000000 | tf_op jit(solution)/shard_map/pallas_call | solution.py:573
  82.3 5.8 %all-to-all-start.3 = ((f32[32,32,128]{2,1,0:T(8,128)}), f32[32,32,128]{2,1,0:T(8,128)S(1)}, u32[]{:S(2)}, u32[]{:S(2)}) async-start(f32[32,32,128]{2,1,0:T(8,128)} %bitcast.18), calls=%async_computation.3 | async-start | bytes 1048576 | tf_op jit(solution)/shard_map/all_to_all | solution.py:502
  91.2 6.7 %collective-permute-done.9.second_slots = f32[512,128]{1,0:T(8,128)S(1)} collective-permute-done((f32[512,128]{1,0:T(8,128)S(1)}, f32[512,128]{1,0:T(8,128)S(1)}, u32[]{:S(2)}, u32[]{:S(2)}) %collective-permute-start.9) | collective-permute-done | bytes 262176 | tf_op jit(solution)/shard_map/ppermute | solution.py:517
  99.5 39.2 %all_to_all.123 = f32[32,32,128]{2,1,0:T(8,128)S(1)} all-to-all(f32[32,32,128]{2,1,0:T(8,128)S(1)} %bitcast.41), channel_id=1, replica_groups=mesh['z'=8,'yl'=2,'x'=4,'yh'=2,'core'=2] {'yl','x','yh','core'}, dimensions={0} | all-to-all | bytes 1048576 | tf_op jit(solution)/shard_map/all_to_all | solution.py:502
  141.2 2.8 collective-permute-start.10
  144.0 5.8 %collective-permute-done.10.before = f32[4,128,128]{2,1,0:T(8,128)S(1)} collective-permute-done((f32[4,128,128]{2,1,0:T(8,128)S(1)}, f32[4,128,128]{2,1,0:T(8,128)S(1)}, u32[]{:S(2)}, u32[]{:S(2)}) %collective-permute-start.10) | collective-permute-done | bytes 262176 | tf_op jit(solution)/shard_map/ppermute | solution.py:564
  149.9 5.0 %collective-permute-done.11.after = f32[4,128,128]{2,1,0:T(8,128)S(1)} collective-permute-done((f32[4,128,128]{2,1,0:T(8,128)S(1)}, f32[4,128,128]{2,1,0:T(8,128)S(1)}, u32[]{:S(2)}, u32[]{:S(2)}) %collective-permute-start.11) | collective-permute-done | bytes 262176 | tf_op jit(solution)/shard_map/ppermute | solution.py:564
  157.0 11.4 %all_to_all.124 = f32[32,16,128]{2,1,0:T(8,128)S(1)} all-to-all(f32[32,16,128]{2,1,0:T(8,128)S(1)} %bitcast.46), channel_id=1, replica_groups=mesh['z'=8,'yl'=2,'x'=4,'yh'=2,'core'=2] {'yl','x','yh','core'}, dimensions={0} | all-to-all | bytes 524288 | tf_op jit(solution)/shard_map/all_to_all | solution.py:502
  171.4 7.0 %all-to-all-start.6 = ((f32[32,16,128]{2,1,0:T(8,128)}), f32[32,16,128]{2,1,0:T(8,128)S(1)}, u32[]{:S(2)}, u32[]{:S(2)}) async-start(f32[32,16,128]{2,1,0:T(8,128)} %bitcast.24), calls=%async_computation.6 | async-start | bytes 524288 | tf_op jit(solution)/shard_map/all_to_all | solution.py:502
  180.8 2.9 collective-permute-start.14
  184.8 6.1 %collective-permute-start.12 = (f32[4,64,128]{2,1,0:T(8,128)S(1)}, f32[4,64,128]{2,1,0:T(8,128)S(1)}, u32[]{:S(2)}, u32[]{:S(2)}) collective-permute-start(f32[4,64,128]{2,1,0:T(8,128)S(1)} %get-tuple-element.62.high), channel_id=1, source_target_pairs={{0,4},{4,8},{8,12},{12,16},{16,20},{20,24},{24,28},{28,32},{32,36}... | collective-permute-start | bytes 393224 | tf_op jit(solution)/shard_map/ppermute | solution.py:564
  190.9 9.5 %collective-permute-start.13 = (f32[4,64,128]{2,1,0:T(8,128)S(1)}, f32[4,64,128]{2,1,0:T(8,128)S(1)}, u32[]{:S(2)}, u32[]{:S(2)}) collective-permute-start(f32[4,64,128]{2,1,0:T(8,128)S(1)} %get-tuple-element.61.low), channel_id=1, source_target_pairs={{0,252},{4,0},{8,4},{12,8},{16,12},{20,16},{24,20},{28,24},{32,28}... | collective-permute-start | bytes 393224 | tf_op jit(solution)/shard_map/ppermute | solution.py:564
  202.1 6.5 %collective-permute-done.13.after = f32[4,64,128]{2,1,0:T(8,128)S(1)} collective-permute-done((f32[4,64,128]{2,1,0:T(8,128)S(1)}, f32[4,64,128]{2,1,0:T(8,128)S(1)}, u32[]{:S(2)}, u32[]{:S(2)}) %collective-permute-start.13) | collective-permute-done | bytes 131104 | tf_op jit(solution)/shard_map/ppermute | solution.py:564
  208.6 3.7 %shard_map.164 = f32[1024,128]{1,0:T(8,128)S(1)} custom-call(f32[64,128]{1,0:T(8,128)S(1)} %bitcast.53, f32[4,64,128]{2,1,0:T(8,128)S(1)} %get-tuple-element.61.low, f32[4,64,128]{2,1,0:T(8,128)S(1)} %get-tuple-element.62.high, f32[4,64,128]{2,1,0:T(8,128)S(1)} %collective-permute-done.12.before, f32[4,64,128]{2,1,0:T(8,128)S(1)} %collective-permute-done.13.after, ...), custom_call_target="tpu_custom_call" | custom-call | flops 100000000 | bytes 6000000 | tf_op jit(solution)/shard_map/pallas_call | solution.py:573
  212.3 14.0 %all_to_all.125 = f32[32,32,128]{2,1,0:T(8,128)S(1)} all-to-all(f32[32,32,128]{2,1,0:T(8,128)S(1)} %bitcast.45), channel_id=1, replica_groups=mesh['z'=8,'yl'=2,'x'=4,'yh'=2,'core'=2] {'yl','x','yh','core'}, dimensions={0} | all-to-all | bytes 1048576 | tf_op jit(solution)/shard_map/all_to_all | solution.py:502
  227.9 15.1 %all_to_all.126 = f32[32,32,128]{2,1,0:T(8,128)S(1)} all-to-all(f32[32,32,128]{2,1,0:T(8,128)S(1)} %bitcast.40), channel_id=1, replica_groups=mesh['z'=8,'yl'=2,'x'=4,'yh'=2,'core'=2] {'yl','x','yh','core'}, dimensions={0} | all-to-all | bytes 1048576 | tf_op jit(solution)/shard_map/all_to_all | solution.py:502
  245.6 7.2 %collective-permute-start.16 = (f32[4,128,128]{2,1,0:T(8,128)S(1)}, f32[4,128,128]{2,1,0:T(8,128)S(1)}, u32[]{:S(2)}, u32[]{:S(2)}) collective-permute-start(f32[4,128,128]{2,1,0:T(8,128)S(1)} %get-tuple-element.67.high), channel_id=1, source_target_pairs={{0,4},{4,8},{8,12},{12,16},{16,20},{20,24},{24,28},{28,32},{32,36}... | collective-permute-start | bytes 786440 | tf_op jit(solution)/shard_map/ppermute | solution.py:564
  252.8 5.6 %collective-permute-done.16.before = f32[4,128,128]{2,1,0:T(8,128)S(1)} collective-permute-done((f32[4,128,128]{2,1,0:T(8,128)S(1)}, f32[4,128,128]{2,1,0:T(8,128)S(1)}, u32[]{:S(2)}, u32[]{:S(2)}) %collective-permute-start.16) | collective-permute-done | bytes 262176 | tf_op jit(solution)/shard_map/ppermute | solution.py:564
  258.4 5.2 %collective-permute-done.17.after = f32[4,128,128]{2,1,0:T(8,128)S(1)} collective-permute-done((f32[4,128,128]{2,1,0:T(8,128)S(1)}, f32[4,128,128]{2,1,0:T(8,128)S(1)}, u32[]{:S(2)}, u32[]{:S(2)}) %collective-permute-start.17) | collective-permute-done | bytes 262176 | tf_op jit(solution)/shard_map/ppermute | solution.py:564
  265.8 11.4 %all_to_all.127 = f32[32,16,128]{2,1,0:T(8,128)S(1)} all-to-all(f32[32,16,128]{2,1,0:T(8,128)S(1)} %bitcast.47), channel_id=1, replica_groups=mesh['z'=8,'yl'=2,'x'=4,'yh'=2,'core'=2] {'yl','x','yh','core'}, dimensions={0} | all-to-all | bytes 524288 | tf_op jit(solution)/shard_map/all_to_all | solution.py:502
  279.6 7.1 %all-to-all-start.10 = ((f32[32,32,128]{2,1,0:T(8,128)}), f32[32,32,128]{2,1,0:T(8,128)S(1)}, u32[]{:S(2)}, u32[]{:S(2)}) async-start(f32[32,32,128]{2,1,0:T(8,128)} %bitcast.32), calls=%async_computation.10 | async-start | bytes 1048576 | tf_op jit(solution)/shard_map/all_to_all | solution.py:502
  290.4 5.3 %all-to-all-done.10 = f32[32,32,128]{2,1,0:T(8,128)S(1)} async-done(((f32[32,32,128]{2,1,0:T(8,128)}), f32[32,32,128]{2,1,0:T(8,128)S(1)}, u32[]{:S(2)}, u32[]{:S(2)}) %all-to-all-start.10) | async-done | bytes 524320 | tf_op jit(solution)/shard_map/all_to_all | solution.py:502
  297.1 6.4 %collective-permute-start.18 = (f32[4,64,128]{2,1,0:T(8,128)S(1)}, f32[4,64,128]{2,1,0:T(8,128)S(1)}, u32[]{:S(2)}, u32[]{:S(2)}) collective-permute-start(f32[4,64,128]{2,1,0:T(8,128)S(1)} %get-tuple-element.70.high), channel_id=1, source_target_pairs={{0,4},{4,8},{8,12},{12,16},{16,20},{20,24},{24,28},{28,32},{32,36}... | collective-permute-start | bytes 393224 | tf_op jit(solution)/shard_map/ppermute | solution.py:564
  307.3 5.2 %collective-permute-done.19.after = f32[4,64,128]{2,1,0:T(8,128)S(1)} collective-permute-done((f32[4,64,128]{2,1,0:T(8,128)S(1)}, f32[4,64,128]{2,1,0:T(8,128)S(1)}, u32[]{:S(2)}, u32[]{:S(2)}) %collective-permute-start.19) | collective-permute-done | bytes 131104 | tf_op jit(solution)/shard_map/ppermute | solution.py:564
  (99 shorter events, 55.7 us)
Async XLA Ops:
  1.5 1.3 collective-permute-start
  3.6 10.2 %collective-permute-start.1 = (f32[256,128]{1,0:T(8,128)S(1)}, f32[256,128]{1,0:T(8,128)S(1)}, u32[]{:S(2)}, u32[]{:S(2)}) collective-permute-start(f32[256,128]{1,0:T(8,128)S(1)} %pad_maximum_fusion.1), channel_id=1, source_target_pairs={{0,2},{2,0},{1,3},{3,1},{4,6},{6,4},{5,7},{7,5},{8,10},{10,8},{9,1... | collective-permute-start | bytes 393224 | tf_op jit(solution)/shard_map/ppermute | solution.py:513
  7.4 12.2 %all-to-all-start = ((f32[32,16,128]{2,1,0:T(8,128)}), f32[32,16,128]{2,1,0:T(8,128)S(1)}, u32[]{:S(2)}, u32[]{:S(2)}) async-start(f32[32,16,128]{2,1,0:T(8,128)} %bitcast.5), calls=%async_computation | async-start | bytes 524288 | tf_op jit(solution)/shard_map/all_to_all | solution.py:502
  13.9 33.3 %collective-permute-start.2 = (f32[512,128]{1,0:T(8,128)S(1)}, f32[512,128]{1,0:T(8,128)S(1)}, u32[]{:S(2)}, u32[]{:S(2)}) collective-permute-start(f32[512,128]{1,0:T(8,128)S(1)} %pad_maximum_fusion), channel_id=1, source_target_pairs={{0,0},{1,64},{2,128},{3,192},{32,32},{33,96},{34,160},{35,224},{64... | collective-permute-start | bytes 786440 | tf_op jit(solution)/shard_map/ppermute | solution.py:517
  14.6 32.6 %collective-permute-start.3 = (f32[512,128]{1,0:T(8,128)S(1)}, f32[512,128]{1,0:T(8,128)S(1)}, u32[]{:S(2)}, u32[]{:S(2)}) collective-permute-start(f32[512,128]{1,0:T(8,128)S(1)} %pad_maximum_fusion), channel_id=1, source_target_pairs={{0,32},{1,96},{2,160},{3,224},{32,0},{33,64},{34,128},{35,192},{64... | collective-permute-start | bytes 786440 | tf_op jit(solution)/shard_map/ppermute | solution.py:517
  19.6 27.5 %all-to-all-start.1 = ((f32[64,1,128]{2,1,0:T(1,128)}), f32[64,1,128]{2,1,0:T(1,128)S(1)}, u32[]{:S(2)}, u32[]{:S(2)}) async-start(f32[64,1,128]{2,1,0:T(1,128)} %bitcast.8), calls=%async_computation.1 | async-start | bytes 65536 | tf_op jit(solution)/shard_map/all_to_all | solution.py:529
  47.1 9.2 %copy-start.9 = (s32[8,128]{1,0:T(8,128)S(1)}, s32[8,128]{1,0:T(8,128)}, u32[]{:S(2)}) copy-start(s32[8,128]{1,0:T(8,128)} %own.1) | copy-start | bytes 12292
  49.1 7.2 %copy-start.4 = (bf16[2,2,32,8,128]{4,3,2,1,0:T(8,128)(2,1)S(1)}, bf16[2,2,32,8,128]{4,3,2,1,0:T(8,128)(2,1)}, u32[]{:S(2)}) copy-start(bf16[2,2,32,8,128]{4,3,2,1,0:T(8,128)(2,1)} %param.15) | copy-start | bytes 786436
  49.8 12.9 %all-to-all-start.2 = ((f32[32,16,128]{2,1,0:T(8,128)}), f32[32,16,128]{2,1,0:T(8,128)S(1)}, u32[]{:S(2)}, u32[]{:S(2)}) async-start(f32[32,16,128]{2,1,0:T(8,128)} %bitcast.14), calls=%async_computation.2 | async-start | bytes 524288 | tf_op jit(solution)/shard_map/all_to_all | solution.py:502
  56.6 12.9 %collective-permute-start.6 = (f32[264,128]{1,0:T(8,128)S(1)}, f32[264,128]{1,0:T(8,128)S(1)}, u32[]{:S(2)}, u32[]{:S(2)}) collective-permute-start(f32[264,128]{1,0:T(8,128)S(1)} %get-tuple-element.51), channel_id=1, source_target_pairs={{0,4},{4,8},{8,12},{12,16},{16,20},{20,24},{24,28},{28,32},{32,36}... | collective-permute-start | bytes 405512 | tf_op jit(solution)/shard_map/ppermute | solution.py:542
  57.5 12.0 %collective-permute-start.7 = (f32[264,128]{1,0:T(8,128)S(1)}, f32[264,128]{1,0:T(8,128)S(1)}, u32[]{:S(2)}, u32[]{:S(2)}) collective-permute-start(f32[264,128]{1,0:T(8,128)S(1)} %get-tuple-element.52), channel_id=1, source_target_pairs={{0,252},{4,0},{8,4},{12,8},{16,12},{20,16},{24,20},{28,24},{32,28}... | collective-permute-start | bytes 405512 | tf_op jit(solution)/shard_map/ppermute | solution.py:543
  63.3 9.3 %collective-permute-start.4 = (f32[4,64,128]{2,1,0:T(8,128)S(1)}, f32[4,64,128]{2,1,0:T(8,128)S(1)}, u32[]{:S(2)}, u32[]{:S(2)}) collective-permute-start(f32[4,64,128]{2,1,0:T(8,128)S(1)} %get-tuple-element.48.high), channel_id=1, source_target_pairs={{0,4},{4,8},{8,12},{12,16},{16,20},{20,24},{24,28},{28,32},{32,36}... | collective-permute-start | bytes 393224 | tf_op jit(solution)/shard_map/ppermute | solution.py:564
  69.4 8.3 %collective-permute-start.5 = (f32[4,64,128]{2,1,0:T(8,128)S(1)}, f32[4,64,128]{2,1,0:T(8,128)S(1)}, u32[]{:S(2)}, u32[]{:S(2)}) collective-permute-start(f32[4,64,128]{2,1,0:T(8,128)S(1)} %get-tuple-element.47.low), channel_id=1, source_target_pairs={{0,252},{4,0},{8,4},{12,8},{16,12},{20,16},{24,20},{28,24},{32,28}... | collective-permute-start | bytes 393224 | tf_op jit(solution)/shard_map/ppermute | solution.py:564
  82.3 15.6 %all-to-all-start.3 = ((f32[32,32,128]{2,1,0:T(8,128)}), f32[32,32,128]{2,1,0:T(8,128)S(1)}, u32[]{:S(2)}, u32[]{:S(2)}) async-start(f32[32,32,128]{2,1,0:T(8,128)} %bitcast.18), calls=%async_computation.3 | async-start | bytes 1048576 | tf_op jit(solution)/shard_map/all_to_all | solution.py:502
  89.4 1.8 collective-permute-start.8
  90.1 7.8 %collective-permute-start.9 = (f32[512,128]{1,0:T(8,128)S(1)}, f32[512,128]{1,0:T(8,128)S(1)}, u32[]{:S(2)}, u32[]{:S(2)}) collective-permute-start(f32[512,128]{1,0:T(8,128)S(1)} %get-tuple-element.56), channel_id=1, source_target_pairs={{0,32},{1,96},{2,160},{3,224},{32,0},{33,64},{34,128},{35,192},{64... | collective-permute-start | bytes 786440 | tf_op jit(solution)/shard_map/ppermute | solution.py:517
  141.2 8.6 %collective-permute-start.10 = (f32[4,128,128]{2,1,0:T(8,128)S(1)}, f32[4,128,128]{2,1,0:T(8,128)S(1)}, u32[]{:S(2)}, u32[]{:S(2)}) collective-permute-start(f32[4,128,128]{2,1,0:T(8,128)S(1)} %get-tuple-element.58.high), channel_id=1, source_target_pairs={{0,4},{4,8},{8,12},{12,16},{16,20},{20,24},{24,28},{28,32},{32,36}... | collective-permute-start | bytes 786440 | tf_op jit(solution)/shard_map/ppermute | solution.py:564
  144.0 10.8 %collective-permute-start.11 = (f32[4,128,128]{2,1,0:T(8,128)S(1)}, f32[4,128,128]{2,1,0:T(8,128)S(1)}, u32[]{:S(2)}, u32[]{:S(2)}) collective-permute-start(f32[4,128,128]{2,1,0:T(8,128)S(1)} %get-tuple-element.57.low), channel_id=1, source_target_pairs={{0,252},{4,0},{8,4},{12,8},{16,12},{20,16},{24,20},{28,24},{32,28}... | collective-permute-start | bytes 786440 | tf_op jit(solution)/shard_map/ppermute | solution.py:564
  157.0 11.4 %copy-start.6 = (f32[4,128,128]{2,1,0:T(8,128)S(1)}, f32[4,128,128]{2,1,0:T(8,128)}, u32[]{:S(2)}) copy-start(f32[4,128,128]{2,1,0:T(8,128)} %copy-done.5) | copy-start | bytes 786436
  171.4 12.9 %all-to-all-start.6 = ((f32[32,16,128]{2,1,0:T(8,128)}), f32[32,16,128]{2,1,0:T(8,128)S(1)}, u32[]{:S(2)}, u32[]{:S(2)}) async-start(f32[32,16,128]{2,1,0:T(8,128)} %bitcast.24), calls=%async_computation.6 | async-start | bytes 524288 | tf_op jit(solution)/shard_map/all_to_all | solution.py:502
  180.8 19.6 %collective-permute-start.14 = (f32[256,128]{1,0:T(8,128)}, f32[256,128]{1,0:T(8,128)S(1)}, u32[]{:S(2)}, u32[]{:S(2)}) collective-permute-start(f32[256,128]{1,0:T(8,128)} %get-tuple-element.64), channel_id=1, source_target_pairs={{0,4},{4,8},{8,12},{12,16},{16,20},{20,24},{24,28},{28,32},{32,36}... | collective-permute-start | bytes 393224 | tf_op jit(solution)/shard_map/ppermute | solution.py:587
  183.7 16.7 %collective-permute-start.15 = (f32[256,128]{1,0:T(8,128)}, f32[256,128]{1,0:T(8,128)S(1)}, u32[]{:S(2)}, u32[]{:S(2)}) collective-permute-start(f32[256,128]{1,0:T(8,128)} %get-tuple-element.65), channel_id=1, source_target_pairs={{0,252},{4,0},{8,4},{12,8},{16,12},{20,16},{24,20},{28,24},{32,28}... | collective-permute-start | bytes 393224 | tf_op jit(solution)/shard_map/ppermute | solution.py:588
  184.8 17.3 %collective-permute-start.12 = (f32[4,64,128]{2,1,0:T(8,128)S(1)}, f32[4,64,128]{2,1,0:T(8,128)S(1)}, u32[]{:S(2)}, u32[]{:S(2)}) collective-permute-start(f32[4,64,128]{2,1,0:T(8,128)S(1)} %get-tuple-element.62.high), channel_id=1, source_target_pairs={{0,4},{4,8},{8,12},{12,16},{16,20},{20,24},{24,28},{28,32},{32,36}... | collective-permute-start | bytes 393224 | tf_op jit(solution)/shard_map/ppermute | solution.py:564
  190.9 17.7 %collective-permute-start.13 = (f32[4,64,128]{2,1,0:T(8,128)S(1)}, f32[4,64,128]{2,1,0:T(8,128)S(1)}, u32[]{:S(2)}, u32[]{:S(2)}) collective-permute-start(f32[4,64,128]{2,1,0:T(8,128)S(1)} %get-tuple-element.61.low), channel_id=1, source_target_pairs={{0,252},{4,0},{8,4},{12,8},{16,12},{20,16},{24,20},{28,24},{32,28}... | collective-permute-start | bytes 393224 | tf_op jit(solution)/shard_map/ppermute | solution.py:564
  245.6 12.8 %collective-permute-start.16 = (f32[4,128,128]{2,1,0:T(8,128)S(1)}, f32[4,128,128]{2,1,0:T(8,128)S(1)}, u32[]{:S(2)}, u32[]{:S(2)}) collective-permute-start(f32[4,128,128]{2,1,0:T(8,128)S(1)} %get-tuple-element.67.high), channel_id=1, source_target_pairs={{0,4},{4,8},{8,12},{12,16},{16,20},{20,24},{24,28},{28,32},{32,36}... | collective-permute-start | bytes 786440 | tf_op jit(solution)/shard_map/ppermute | solution.py:564
  252.8 10.8 %collective-permute-start.17 = (f32[4,128,128]{2,1,0:T(8,128)S(1)}, f32[4,128,128]{2,1,0:T(8,128)S(1)}, u32[]{:S(2)}, u32[]{:S(2)}) collective-permute-start(f32[4,128,128]{2,1,0:T(8,128)S(1)} %get-tuple-element.66.low), channel_id=1, source_target_pairs={{0,252},{4,0},{8,4},{12,8},{16,12},{20,16},{24,20},{28,24},{32,28}... | collective-permute-start | bytes 786440 | tf_op jit(solution)/shard_map/ppermute | solution.py:564
  265.8 11.4 %copy-start.8 = (f32[4,128,128]{2,1,0:T(8,128)S(1)}, f32[4,128,128]{2,1,0:T(8,128)}, u32[]{:S(2)}) copy-start(f32[4,128,128]{2,1,0:T(8,128)} %copy-done.7) | copy-start | bytes 786436
  279.6 16.1 %all-to-all-start.10 = ((f32[32,32,128]{2,1,0:T(8,128)}), f32[32,32,128]{2,1,0:T(8,128)S(1)}, u32[]{:S(2)}, u32[]{:S(2)}) async-start(f32[32,32,128]{2,1,0:T(8,128)} %bitcast.32), calls=%async_computation.10 | async-start | bytes 1048576 | tf_op jit(solution)/shard_map/all_to_all | solution.py:502
  288.3 15.2 %collective-permute-start.20 = (f32[256,128]{1,0:T(8,128)S(1)}, f32[256,128]{1,0:T(8,128)S(1)}, u32[]{:S(2)}, u32[]{:S(2)}) collective-permute-start(f32[256,128]{1,0:T(8,128)S(1)} %get-tuple-element.72), channel_id=1, source_target_pairs={{0,4},{4,8},{8,12},{12,16},{16,20},{20,24},{24,28},{28,32},{32,36}... | collective-permute-start | bytes 393224 | tf_op jit(solution)/shard_map/ppermute | solution.py:587
  290.2 13.2 %collective-permute-start.21 = (f32[256,128]{1,0:T(8,128)S(1)}, f32[256,128]{1,0:T(8,128)S(1)}, u32[]{:S(2)}, u32[]{:S(2)}) collective-permute-start(f32[256,128]{1,0:T(8,128)S(1)} %get-tuple-element.73), channel_id=1, source_target_pairs={{0,252},{4,0},{8,4},{12,8},{16,12},{20,16},{24,20},{28,24},{32,28}... | collective-permute-start | bytes 393224 | tf_op jit(solution)/shard_map/ppermute | solution.py:588
  297.1 10.3 %collective-permute-start.18 = (f32[4,64,128]{2,1,0:T(8,128)S(1)}, f32[4,64,128]{2,1,0:T(8,128)S(1)}, u32[]{:S(2)}, u32[]{:S(2)}) collective-permute-start(f32[4,64,128]{2,1,0:T(8,128)S(1)} %get-tuple-element.70.high), channel_id=1, source_target_pairs={{0,4},{4,8},{8,12},{12,16},{16,20},{20,24},{24,28},{28,32},{32,36}... | collective-permute-start | bytes 393224 | tf_op jit(solution)/shard_map/ppermute | solution.py:564
  303.5 9.1 %collective-permute-start.19 = (f32[4,64,128]{2,1,0:T(8,128)S(1)}, f32[4,64,128]{2,1,0:T(8,128)S(1)}, u32[]{:S(2)}, u32[]{:S(2)}) collective-permute-start(f32[4,64,128]{2,1,0:T(8,128)S(1)} %get-tuple-element.69.low), channel_id=1, source_target_pairs={{0,252},{4,0},{8,4},{12,8},{16,12},{20,16},{24,20},{28,24},{32,28}... | collective-permute-start | bytes 393224 | tf_op jit(solution)/shard_map/ppermute | solution.py:564
  (13 other events, 56.9 us)

commit v2 on v1

--- a/solution.py
+++ b/solution.py
@@ -121,28 +121,30 @@
     request[...] = 32.0 * dot_nt(high, ranked) + dot_nt(low, ranked)
 
 
-def slots_kernel(here, source_row, ranks, weight, innovation, first, second):
+def slots_kernel(here, source_row, ranks, weight, innovation, shared, first, second):
     z, level = here[0], here[1]
     source, rank = source_row[...], ranks[...]
     row = iota((256, 512), 0)
     place = ((row >> 7) & 1) * 16 + (row & 15)
     for j, target in enumerate((first, second)):
-        tile = (2 * level + lax.rem(z + j, 2)) * 8 + ((row >> 4) & 7)
+        for k in range(4):
+            target[k * 64 : k * 64 + 64] = shared[k * 128 + 64 : k * 128 + 128]
+        tile = lax.rem(z + level + 4 * j + 3 * lax.rem(z, 2), 8) * 8 + ((row >> 4) & 7)
         mine = one_hot((source == tile) & (rank == place))
         for kind, values in enumerate((weight, innovation)):
             terms = split(values[...])
-            target[kind * 256 : kind * 256 + 256] = dot_nt(mine, terms[0]) + dot_nt(mine, terms[1])
+            target[256 + kind * 256 : 512 + kind * 256] = dot_nt(mine, terms[0]) + dot_nt(mine, terms[1])
 
 
 def load_matrices(here, first, second, matrices):
-    z = here[0]
+    turn = lax.rem(here[0] - 2 * here[1] + 8, 8)
     for j, part in enumerate((first, second)):
-        half = lax.rem(z + j, 2)
+        half = lax.bitwise_xor(lax.div(turn, 4), j)
         for k in range(4):
-            block = lax.bitwise_xor(lax.div(z, 2), k)
+            block = lax.bitwise_xor(lax.rem(turn, 4), k)
             rows = pl.ds(pl.multiple_of(block * 32, 32), 32)
             for var in range(2):
-                start = k * 128 + var * 32
+                start = k * 64 + var * 32
                 matrices[half * 2 + var, rows, :] = part[start : start + 32]
 
 
@@ -357,19 +359,19 @@
         terms[q] = jnp.concatenate(split(pair), axis=0)
     wanted = request[...].astype(i32)
     first, second = (wanted >> 5).astype(f32).astype(bf16), (wanted & 31).astype(f32).astype(bf16)
-    wide = iota((512, 256), 1)
+    wide = iota((256, 256), 1)
 
     def block(step, carry):
-        start = pl.multiple_of(step * 512, 512)
+        start = pl.multiple_of(step * 256, 256)
         sums = []
         for half in range(2):
-            column = slot_columns(first, second, start, 512, half)
+            column = slot_columns(first, second, start, 256, half)
             total = sum(dot_nt(one_hot(column - q * 256 == wide), terms[q]) for q in range(4))
             sums.append(total + pltpu.roll(total, 64, 1))
-        out[pl.ds(start, 512), :] = jnp.where(iota((512, 128), 1) < 64, sums[0], sums[1])
+        out[pl.ds(start, 256), :] = jnp.where(iota((256, 128), 1) < 64, sums[0], sums[1])
         return carry
 
-    lax.fori_loop(0, 2, block, 0)
+    lax.fori_loop(0, 4, block, 0)
 
 
 def last_kernel(low, high, before, after, members, weights, ens, out, final_ens, field):
@@ -379,27 +381,27 @@
         final_ens[pl.ds(lon, 64, stride=8), :] = ens[lon]
 
 
-def operators_kernel(here, arrived, first, second, first_slots, second_slots, out, stacked):
-    z = here[0]
+def operators_kernel(here, arrived, first, second, out, stacked):
+    turn = lax.rem(here[0] - 2 * here[1] + 8, 8)
     lane = iota((128, 128), 1) < 64
 
     def start(u, k, half):
-        level = lax.bitwise_xor(lax.div(z, 2), k)
+        level = lax.bitwise_xor(lax.rem(turn, 4), k)
         return pl.ds(pl.multiple_of((u * 4 + level) * 32 + half * 16, 16), 16)
 
-    for j, (part, slots) in enumerate(((first, first_slots), (second, second_slots))):
-        half = lax.rem(z + j, 2)
+    for j, part in enumerate((first, second)):
+        half = lax.bitwise_xor(lax.div(turn, 4), j)
         blocks = [
             jnp.concatenate([arrived[start(u, k, half), :] for u in range(8)], axis=0) for k in range(4)
         ]
-        operator = jnp.concatenate([part[k * 128 + 64 : k * 128 + 128] for k in range(4)], axis=0)
+        operator = part[0:256]
         for pair in range(2):
             even, odd = blocks[2 * pair], blocks[2 * pair + 1]
             lanes = slice(pair * 128, pair * 128 + 128)
             stacked[0:128, lanes] = jnp.where(lane, even, pltpu.roll(odd, 64, 1))
             stacked[128:256, lanes] = jnp.where(lane, pltpu.roll(even, 64, 1), odd)
         observed = three(dot_nn, stacked[...], operator)
-        departure = slots[0:256] * (observed - slots[256:512])
+        departure = part[256:512] * (observed - part[512:768])
         pulled = three(dot_nt, departure, operator)
         for pair in range(2):
             lanes = slice(pair * 128, pair * 128 + 128)
@@ -413,36 +415,46 @@
                     out[start(u, 2 * pair + side, half), :] = values[side][u * 16 : u * 16 + 16]
 
 
-def collect_kernel(request, arrived, perts, low, high, turned):
+def collect_kernel(request, arrived, perts, low, high, turned, places):
     value = arrived[...]
     first = value.astype(bf16).astype(f32)
     rest = value - first
     lane = iota((1024, 128), 1) < 64
-    stacked = jnp.concatenate(
-        [
-            jnp.where(lane, first, pltpu.roll(rest, 64, 1)),
-            jnp.where(lane, pltpu.roll(first, 64, 1), rest),
-        ],
-        axis=0,
-    )
-    turned[...] = stacked.T.astype(bf16)
+    turned[:, 0:1024] = jnp.where(lane, first, pltpu.roll(rest, 64, 1)).T.astype(bf16)
+    turned[:, 1024:2048] = jnp.where(lane, pltpu.roll(first, 64, 1), rest).T.astype(bf16)
     wanted = request[...].astype(i32)
     upper, lower = (wanted >> 5).astype(f32).astype(bf16), (wanted & 31).astype(f32).astype(bf16)
-    columns = [slot_columns(upper, lower, 0, 1024, half) for half in range(2)]
-    wide = iota((1024, 256), 1)
-    for q in range(4):
-        hits = jnp.concatenate([one_hot(columns[half] - q * 256 == wide) for half in range(2)], axis=0)
+    for half in range(2):
+        places[half * 1024 : half * 1024 + 1024] = jnp.broadcast_to(
+            slot_columns(upper, lower, 0, 1024, half), (1024, 128)
+        )
+
+    def pair(q, carry):
+        wide = iota((2048, 128), 1) + q * 256
+        hits = jnp.concatenate([one_hot(places[...] == wide), one_hot(places[...] == wide + 128)], axis=1)
         both = dot_nn(turned[...], hits)
         total = both[:64] + both[64:]
-        target = low if q < 2 else high
         for side in range(2):
-            place = (q % 2) * 2 + side
             gradient = total[:, side * 128 : side * 128 + 128]
-            target[place, 0:64] = gradient
             factor = perts[2 * q + side]
-            for e in range(2):
-                mixed = factor[e * 64 : e * 64 + 32] * gradient[:32] + factor[e * 64 + 32 : e * 64 + 64] * gradient[32:]
-                target[place, 64 + e * 32 : 96 + e * 32] = beta_ensemble * mixed
+            mixed = [
+                factor[e * 64 : e * 64 + 32] * gradient[:32] + factor[e * 64 + 32 : e * 64 + 64] * gradient[32:]
+                for e in range(2)
+            ]
+            value = jnp.concatenate([gradient] + [beta_ensemble * part for part in mixed], axis=0)
+            place = lax.rem(q, 2) * 2 + side
+
+            @pl.when(q < 2)
+            def _():
+                low[place] = value
+
+            @pl.when(q >= 2)
+            def _():
+                high[place] = value
+
+        return carry
+
+    lax.fori_loop(0, 4, pair, 0)
 
 
 def pull_kernel(owner, low, high, before, after, weights, packed, field):
@@ -511,27 +523,30 @@
     swap = [(0, 1), (1, 0)]
     shared = jnp.concatenate([shared, lax.ppermute(shared, "core", swap)], axis=0)
     shared = jnp.concatenate([shared, lax.ppermute(shared, "yh", swap)], axis=0)
-    exchange = [(z * 4 + l, (2 * l + (j + z) % 2) * 4 + z // 2) for j in range(2) for z in range(8) for l in range(4)]
+    exchange = [
+        (z * 4 + l, (z + l + 4 * j + 3 * (z % 2)) % 8 * 4 + z // 2) for j in range(2) for z in range(8) for l in range(4)
+    ]
 
     def spread(value, j):
         return lax.ppermute(value, ("z",) + LEV, exchange[j * 32 : j * 32 + 32])
 
-    matrices = [spread(shared, j) for j in range(2)]
     (packed,) = call(begin_kernel, [((512, 128), f32)], [((8, 64, 128), f32)], total=2)(
         owner, control_static.reshape(512, 128)
     )
-    arrived = to_plane(packed)
     source_row = obs_source.reshape(1, 512)
     request, ranks = call(request_kernel, [((64, 128), f32), ((1, 512), i32)], total=2)(
         source_row, obs_column.reshape(1, 512)
     )
-    request, arrived = lax.optimization_barrier((request, arrived))
+    matrices = shared.reshape(4, 128, 128)[:, :64].reshape(256, 128)
+    matrices = [spread(matrices, j) for j in range(2)]
+    request, arrived = lax.optimization_barrier((request, to_plane(packed)))
     wanted = lax.all_to_all(request, TILE, 0, 0, tiled=True)
     arrived, wanted, control_ens, ranks = lax.optimization_barrier((arrived, wanted, control_ens, ranks))
-    slots = call(slots_kernel, [((512, 128), f32), ((512, 128), f32)], smem=1, total=5)(
-        here, source_row, ranks, obs_weight, innovation
-    )
-    slots = [spread(slots[j], j) for j in range(2)]
+    parts = call(slots_kernel, [((768, 128), f32), ((768, 128), f32)], smem=1, total=6)(
+        here, source_row, ranks, obs_weight, innovation, shared
+    )
+    parts, arrived = lax.optimization_barrier((parts, arrived))
+    parts = [spread(parts[j], j) for j in range(2)]
 
     send_up, send_down, ens, perts = call(
         begin_members_kernel,
@@ -569,14 +584,16 @@
     for iteration in range(ITERS):
         low, high = call(edges_kernel, [half_shape, half_shape], total=2)(owner, to_plane(out))
         before, after = halos(low, high)
+        if iteration == 0:
+            before, after, parts = lax.optimization_barrier((before, after, parts))
         members = members_of(ens, ens_before, ens_after)
         (outgoing,) = call(
             observe_kernel, [((1024, 128), f32)], [scratch, ((4, 128, 256), bf16)], total=7
         )(wanted, low, high, before, after, members, faces)
-        (returned,) = call(operators_kernel, [((1024, 128), f32)], [((256, 256), f32)], smem=1, total=6)(
-            here, to_plane(outgoing), *matrices, *slots
+        (returned,) = call(operators_kernel, [((1024, 128), f32)], [((256, 256), f32)], smem=1, total=4)(
+            here, to_plane(outgoing), *parts
         )
-        low, high = call(collect_kernel, [mixed_shape, mixed_shape], [((128, 2048), bf16)], total=3)(
+        low, high = call(collect_kernel, [mixed_shape, mixed_shape], [((128, 2048), bf16), ((2048, 128), i32)], total=3)(
             wanted, to_plane(returned), perts
         )
         before, after = halos(low, high)

time: 320 us -> 295 us (0.922); the launches traced: 315 us -> 294 us
  waiting for transfers between devices: 71.6 us -> 60.4 us
  starting transfers between devices: 101 us -> 92.5 us
  blocking collectives: 91.1 us -> 85.4 us
    ppermute x10, starting transfers between devices: 38.1 us -> 25.2 us  [halos(): return (lax.ppermute(high, TILE, upward), lax.ppermute(low, TILE, downward))]
    ppermute x4, starting transfers between devices: 2.67 us -> 14.6 us  [spread(): return lax.ppermute(value, ('z',) + LEV, exchange[j * 32:j * 32 + 32])]
    ppermute x4, waiting for transfers between devices: 6.7 us -> 0.01 us  [spread(): return lax.ppermute(value, ('z',) + LEV, exchange[j * 32:j * 32 + 32])]
    all_to_all x5 -> x4, waiting for transfers between devices: 13.1 us -> 6.84 us  [to_plane(): return lax.all_to_all(value, PLANE, 0, 0, tiled=True)]
    ppermute x1, waiting for transfers between devices: 0.01 us -> 6.13 us  [on_device(): from_before = lax.ppermute(send_up, TILE, upward)]
    all_to_all x5 -> x6, blocking collectives: 91.1 us -> 85.4 us  [to_plane(): return lax.all_to_all(value, PLANE, 0, 0, tiled=True)]
    all_to_all x1, starting transfers between devices: 18.3 us -> 13 us  [on_device(): wanted = lax.all_to_all(request, TILE, 0, 0, tiled=True)]
    all_to_all x5 -> x4, starting transfers between devices: 32.8 us -> 28 us  [to_plane(): return lax.all_to_all(value, PLANE, 0, 0, tiled=True)]
  transfers between devices with their start and end apart: 28 -> 27, of which waited for: 16 -> 15; matrix products, arithmetic and copies ran while one was open for 0% -> 1% of each run, Pallas kernels for 5% -> 6%
where the time goes in v2:
time: 295 us; the launch traced here: 294 us
  starting transfers between devices  92.5 us (31%)
  blocking collectives  85.4 us (29%)
  waiting for transfers between devices  60.4 us (20%)
  Pallas kernels  48 us (16%)
  local copies, waits for them, and re-layouts  4.82 us (2%)
    all_to_all x6, blocking collectives, to_plane(): return lax.all_to_all(value, PLANE, 0, 0, tiled=True)  85.4 us
    ppermute x10, waiting for transfers between devices, halos(): return (lax.ppermute(high, TILE, upward), lax.ppermute(low, TILE, downward))  39.3 us
    all_to_all x4, starting transfers between devices, to_plane(): return lax.all_to_all(value, PLANE, 0, 0, tiled=True)  28 us
    ppermute x10, starting transfers between devices, halos(): return (lax.ppermute(high, TILE, upward), lax.ppermute(low, TILE, downward))  25.2 us
    ppermute x4, starting transfers between devices, spread(): return lax.ppermute(value, ('z',) + LEV, exchange[j * 32:j * 32 + 32])  14.6 us
    all_to_all x1, starting transfers between devices, on_device(): wanted = lax.all_to_all(request, TILE, 0, 0, tiled=True)  13 us
    pallas_call x2, Pallas kernels, on_device(): call(observe_kernel, [((1024, 128), f32)], [scratch, ((4, 128, 256), bf16...  9.02 us
    all_to_all x1, waiting for transfers between devices, on_device(): wanted = lax.all_to_all(request, TILE, 0, 0, tiled=True)  7.09 us
  transfers between devices with their start and end apart: 27, of which 15 were waited for; matrix products, arithmetic and copies ran while one was open for 1% of the time, Pallas kernels for 6%

profile of v2, /device:TPU:46, one launch (start us, length us, event | category | flops | bytes accessed | tf_op | source)
XLA Modules:
  0.0 293.9 jit_solution(10655107410423451316)
XLA Ops:
  7.1 6.4 %all-to-all-start = ((f32[32,16,128]{2,1,0:T(8,128)}), f32[32,16,128]{2,1,0:T(8,128)S(1)}, u32[]{:S(2)}, u32[]{:S(2)}) async-start(f32[32,16,128]{2,1,0:T(8,128)} %bitcast.5), calls=%async_computation | async-start | bytes 524288 | tf_op jit(solution)/shard_map/all_to_all | solution.py:514
  13.7 7.9 %collective-permute-start.2 = (f32[256,128]{1,0:T(8,128)S(1)}, f32[256,128]{1,0:T(8,128)S(1)}, u32[]{:S(2)}, u32[]{:S(2)}) collective-permute-start(f32[256,128]{1,0:T(8,128)S(1)} %bitcast.72), channel_id=1, source_target_pairs={{0,0},{1,32},{2,64},{3,96},{32,128},{33,160},{34,192},{35,224},{64... | collective-permute-start | bytes 393224 | tf_op jit(solution)/shard_map/ppermute | solution.py:531
  24.5 13.0 %all-to-all-start.1 = ((f32[64,1,128]{2,1,0:T(1,128)}), f32[64,1,128]{2,1,0:T(1,128)S(1)}, u32[]{:S(2)}, u32[]{:S(2)}) async-start(f32[64,1,128]{2,1,0:T(1,128)} %bitcast.8), calls=%async_computation.1 | async-start | bytes 65536 | tf_op jit(solution)/shard_map/all_to_all | solution.py:543
  37.6 7.1 %all-to-all-done.1 = f32[64,1,128]{2,1,0:T(1,128)S(1)} async-done(((f32[64,1,128]{2,1,0:T(1,128)}), f32[64,1,128]{2,1,0:T(1,128)S(1)}, u32[]{:S(2)}, u32[]{:S(2)}) %all-to-all-start.1) | async-done | bytes 32800 | tf_op jit(solution)/shard_map/all_to_all | solution.py:543
  49.4 6.9 %all-to-all-start.2 = ((f32[32,16,128]{2,1,0:T(8,128)}), f32[32,16,128]{2,1,0:T(8,128)S(1)}, u32[]{:S(2)}, u32[]{:S(2)}) async-start(f32[32,16,128]{2,1,0:T(8,128)} %bitcast.16), calls=%async_computation.2 | async-start | bytes 524288 | tf_op jit(solution)/shard_map/all_to_all | solution.py:514
  56.3 2.5 collective-permute-start.6
  61.9 5.1 %collective-permute-start.8 = (f32[264,128]{1,0:T(8,128)}, f32[264,128]{1,0:T(8,128)}, u32[]{:S(2)}, u32[]{:S(2)}) collective-permute-start(f32[264,128]{1,0:T(8,128)} %get-tuple-element.66), channel_id=1, source_target_pairs={{0,4},{4,8},{8,12},{12,16},{16,20},{20,24},{24,28},{28,32},{32,36}... | collective-permute-start | bytes 405512 | tf_op jit(solution)/shard_map/ppermute | solution.py:557
  67.6 5.1 %collective-permute-start.4 = (f32[4,64,128]{2,1,0:T(8,128)S(1)}, f32[4,64,128]{2,1,0:T(8,128)S(1)}, u32[]{:S(2)}, u32[]{:S(2)}) collective-permute-start(f32[4,64,128]{2,1,0:T(8,128)S(1)} %get-tuple-element.59.high), channel_id=1, source_target_pairs={{0,4},{4,8},{8,12},{12,16},{16,20},{20,24},{24,28},{28,32},{32,36}... | collective-permute-start | bytes 393224 | tf_op jit(solution)/shard_map/ppermute | solution.py:579
  72.7 6.1 %collective-permute-done.8 = f32[264,128]{1,0:T(8,128)} collective-permute-done((f32[264,128]{1,0:T(8,128)}, f32[264,128]{1,0:T(8,128)}, u32[]{:S(2)}, u32[]{:S(2)}) %collective-permute-start.8) | collective-permute-done | bytes 135200 | tf_op jit(solution)/shard_map/ppermute | solution.py:557
  84.5 4.4 %collective-permute-done.5.after = f32[4,64,128]{2,1,0:T(8,128)S(1)} collective-permute-done((f32[4,64,128]{2,1,0:T(8,128)S(1)}, f32[4,64,128]{2,1,0:T(8,128)S(1)}, u32[]{:S(2)}, u32[]{:S(2)}) %collective-permute-start.5) | collective-permute-done | bytes 131104 | tf_op jit(solution)/shard_map/ppermute | solution.py:579
  88.9 4.5 %shard_map.156 = f32[1024,128]{1,0:T(8,128)S(1)} custom-call(f32[64,128]{1,0:T(8,128)S(1)} %bitcast.55, f32[4,64,128]{2,1,0:T(8,128)S(1)} %get-tuple-element.58.low, f32[4,64,128]{2,1,0:T(8,128)S(1)} %get-tuple-element.59.high, f32[4,64,128]{2,1,0:T(8,128)S(1)} %collective-permute-done.4.before, f32[4,64,128]{2,1,0:T(8,128)S(1)} %collective-permute-done.5.after, ...), custom_call_target="tpu_custom_call" | custom-call | flops 100000000 | bytes 6000000 | tf_op jit(solution)/shard_map/pallas_call | solution.py:590
  93.4 18.2 %all_to_all.123 = f32[32,32,128]{2,1,0:T(8,128)S(1)} all-to-all(f32[32,32,128]{2,1,0:T(8,128)S(1)} %bitcast.43), channel_id=1, replica_groups=mesh['z'=8,'yl'=2,'x'=4,'yh'=2,'core'=2] {'yl','x','yh','core'}, dimensions={0} | all-to-all | bytes 1048576 | tf_op jit(solution)/shard_map/all_to_all | solution.py:514
  113.2 15.1 %all_to_all.124 = f32[32,32,128]{2,1,0:T(8,128)S(1)} all-to-all(f32[32,32,128]{2,1,0:T(8,128)S(1)} %bitcast.48), channel_id=1, replica_groups=mesh['z'=8,'yl'=2,'x'=4,'yh'=2,'core'=2] {'yl','x','yh','core'}, dimensions={0} | all-to-all | bytes 1048576 | tf_op jit(solution)/shard_map/all_to_all | solution.py:514
  130.5 4.0 %collective-permute-start.10 = (f32[4,128,128]{2,1,0:T(8,128)S(1)}, f32[4,128,128]{2,1,0:T(8,128)S(1)}, u32[]{:S(2)}, u32[]{:S(2)}) collective-permute-start(f32[4,128,128]{2,1,0:T(8,128)S(1)} %get-tuple-element.72.high), channel_id=1, source_target_pairs={{0,4},{4,8},{8,12},{12,16},{16,20},{20,24},{24,28},{28,32},{32,36}... | collective-permute-start | bytes 786440 | tf_op jit(solution)/shard_map/ppermute | solution.py:579
  134.5 5.6 %collective-permute-done.10.before = f32[4,128,128]{2,1,0:T(8,128)S(1)} collective-permute-done((f32[4,128,128]{2,1,0:T(8,128)S(1)}, f32[4,128,128]{2,1,0:T(8,128)S(1)}, u32[]{:S(2)}, u32[]{:S(2)}) %collective-permute-start.10) | collective-permute-done | bytes 262176 | tf_op jit(solution)/shard_map/ppermute | solution.py:579
  140.2 5.2 %collective-permute-done.11.after = f32[4,128,128]{2,1,0:T(8,128)S(1)} collective-permute-done((f32[4,128,128]{2,1,0:T(8,128)S(1)}, f32[4,128,128]{2,1,0:T(8,128)S(1)}, u32[]{:S(2)}, u32[]{:S(2)}) %collective-permute-start.11) | collective-permute-done | bytes 262176 | tf_op jit(solution)/shard_map/ppermute | solution.py:579
  147.5 11.4 %all_to_all.125 = f32[32,16,128]{2,1,0:T(8,128)S(1)} all-to-all(f32[32,16,128]{2,1,0:T(8,128)S(1)} %bitcast.51), channel_id=1, replica_groups=mesh['z'=8,'yl'=2,'x'=4,'yh'=2,'core'=2] {'yl','x','yh','core'}, dimensions={0} | all-to-all | bytes 524288 | tf_op jit(solution)/shard_map/all_to_all | solution.py:514
  161.2 7.7 %all-to-all-start.6 = ((f32[32,16,128]{2,1,0:T(8,128)}), f32[32,16,128]{2,1,0:T(8,128)}, u32[]{:S(2)}, u32[]{:S(2)}) async-start(f32[32,16,128]{2,1,0:T(8,128)} %bitcast.26), calls=%async_computation.6 | async-start | bytes 524288 | tf_op jit(solution)/shard_map/all_to_all | solution.py:514
  176.3 3.1 %collective-permute-start.12 = (f32[4,64,128]{2,1,0:T(8,128)S(1)}, f32[4,64,128]{2,1,0:T(8,128)S(1)}, u32[]{:S(2)}, u32[]{:S(2)}) collective-permute-start(f32[4,64,128]{2,1,0:T(8,128)S(1)} %get-tuple-element.76.high), channel_id=1, source_target_pairs={{0,4},{4,8},{8,12},{12,16},{16,20},{20,24},{24,28},{28,32},{32,36}... | collective-permute-start | bytes 393224 | tf_op jit(solution)/shard_map/ppermute | solution.py:579
  182.4 5.2 %collective-permute-done.13.after = f32[4,64,128]{2,1,0:T(8,128)S(1)} collective-permute-done((f32[4,64,128]{2,1,0:T(8,128)S(1)}, f32[4,64,128]{2,1,0:T(8,128)S(1)}, u32[]{:S(2)}, u32[]{:S(2)}) %collective-permute-start.13) | collective-permute-done | bytes 131104 | tf_op jit(solution)/shard_map/ppermute | solution.py:579
  187.6 4.5 %shard_map.164 = f32[1024,128]{1,0:T(8,128)S(1)} custom-call(f32[64,128]{1,0:T(8,128)S(1)} %bitcast.57, f32[4,64,128]{2,1,0:T(8,128)S(1)} %get-tuple-element.75.low, f32[4,64,128]{2,1,0:T(8,128)S(1)} %get-tuple-element.76.high, f32[4,64,128]{2,1,0:T(8,128)S(1)} %collective-permute-done.12.before, f32[4,64,128]{2,1,0:T(8,128)S(1)} %collective-permute-done.13.after, ...), custom_call_target="tpu_custom_call" | custom-call | flops 100000000 | bytes 6000000 | tf_op jit(solution)/shard_map/pallas_call | solution.py:590
  192.1 14.2 %all_to_all.126 = f32[32,32,128]{2,1,0:T(8,128)S(1)} all-to-all(f32[32,32,128]{2,1,0:T(8,128)S(1)} %bitcast.44), channel_id=1, replica_groups=mesh['z'=8,'yl'=2,'x'=4,'yh'=2,'core'=2] {'yl','x','yh','core'}, dimensions={0} | all-to-all | bytes 1048576 | tf_op jit(solution)/shard_map/all_to_all | solution.py:514
  207.9 15.1 %all_to_all.127 = f32[32,32,128]{2,1,0:T(8,128)S(1)} all-to-all(f32[32,32,128]{2,1,0:T(8,128)S(1)} %bitcast.46), channel_id=1, replica_groups=mesh['z'=8,'yl'=2,'x'=4,'yh'=2,'core'=2] {'yl','x','yh','core'}, dimensions={0} | all-to-all | bytes 1048576 | tf_op jit(solution)/shard_map/all_to_all | solution.py:514
  225.2 6.6 %collective-permute-start.16 = (f32[4,128,128]{2,1,0:T(8,128)S(1)}, f32[4,128,128]{2,1,0:T(8,128)S(1)}, u32[]{:S(2)}, u32[]{:S(2)}) collective-permute-start(f32[4,128,128]{2,1,0:T(8,128)S(1)} %get-tuple-element.81.high), channel_id=1, source_target_pairs={{0,4},{4,8},{8,12},{12,16},{16,20},{20,24},{24,28},{28,32},{32,36}... | collective-permute-start | bytes 786440 | tf_op jit(solution)/shard_map/ppermute | solution.py:579
  231.8 5.6 %collective-permute-done.16.before = f32[4,128,128]{2,1,0:T(8,128)S(1)} collective-permute-done((f32[4,128,128]{2,1,0:T(8,128)S(1)}, f32[4,128,128]{2,1,0:T(8,128)S(1)}, u32[]{:S(2)}, u32[]{:S(2)}) %collective-permute-start.16) | collective-permute-done | bytes 262176 | tf_op jit(solution)/shard_map/ppermute | solution.py:579
  237.5 5.2 %collective-permute-done.17.after = f32[4,128,128]{2,1,0:T(8,128)S(1)} collective-permute-done((f32[4,128,128]{2,1,0:T(8,128)S(1)}, f32[4,128,128]{2,1,0:T(8,128)S(1)}, u32[]{:S(2)}, u32[]{:S(2)}) %collective-permute-start.17) | collective-permute-done | bytes 262176 | tf_op jit(solution)/shard_map/ppermute | solution.py:579
  244.8 11.3 %all_to_all.128 = f32[32,16,128]{2,1,0:T(8,128)S(1)} all-to-all(f32[32,16,128]{2,1,0:T(8,128)S(1)} %bitcast.52), channel_id=1, replica_groups=mesh['z'=8,'yl'=2,'x'=4,'yh'=2,'core'=2] {'yl','x','yh','core'}, dimensions={0} | all-to-all | bytes 524288 | tf_op jit(solution)/shard_map/all_to_all | solution.py:514
  258.4 7.1 %all-to-all-start.10 = ((f32[32,32,128]{2,1,0:T(8,128)}), f32[32,32,128]{2,1,0:T(8,128)S(1)}, u32[]{:S(2)}, u32[]{:S(2)}) async-start(f32[32,32,128]{2,1,0:T(8,128)} %bitcast.34), calls=%async_computation.10 | async-start | bytes 1048576 | tf_op jit(solution)/shard_map/all_to_all | solution.py:514
  269.2 5.3 %all-to-all-done.10 = f32[32,32,128]{2,1,0:T(8,128)S(1)} async-done(((f32[32,32,128]{2,1,0:T(8,128)}), f32[32,32,128]{2,1,0:T(8,128)S(1)}, u32[]{:S(2)}, u32[]{:S(2)}) %all-to-all-start.10) | async-done | bytes 524320 | tf_op jit(solution)/shard_map/all_to_all | solution.py:514
  275.9 6.4 %collective-permute-start.18 = (f32[4,64,128]{2,1,0:T(8,128)S(1)}, f32[4,64,128]{2,1,0:T(8,128)S(1)}, u32[]{:S(2)}, u32[]{:S(2)}) collective-permute-start(f32[4,64,128]{2,1,0:T(8,128)S(1)} %get-tuple-element.84.high), channel_id=1, source_target_pairs={{0,4},{4,8},{8,12},{12,16},{16,20},{20,24},{24,28},{28,32},{32,36}... | collective-permute-start | bytes 393224 | tf_op jit(solution)/shard_map/ppermute | solution.py:579
  286.2 5.2 %collective-permute-done.19.after = f32[4,64,128]{2,1,0:T(8,128)S(1)} collective-permute-done((f32[4,64,128]{2,1,0:T(8,128)S(1)}, f32[4,64,128]{2,1,0:T(8,128)S(1)}, u32[]{:S(2)}, u32[]{:S(2)}) %collective-permute-start.19) | collective-permute-done | bytes 131104 | tf_op jit(solution)/shard_map/ppermute | solution.py:579
  291.3 2.6 shard_map.172
  (93 shorter events, 59.2 us)
Async XLA Ops:
  1.5 1.3 collective-permute-start
  3.5 10.0 %collective-permute-start.1 = (f32[256,128]{1,0:T(8,128)S(1)}, f32[256,128]{1,0:T(8,128)S(1)}, u32[]{:S(2)}, u32[]{:S(2)}) collective-permute-start(f32[256,128]{1,0:T(8,128)S(1)} %pad_maximum_fusion.1), channel_id=1, source_target_pairs={{0,2},{2,0},{1,3},{3,1},{4,6},{6,4},{5,7},{7,5},{8,10},{10,8},{9,1... | collective-permute-start | bytes 393224 | tf_op jit(solution)/shard_map/ppermute | solution.py:525
  7.1 17.4 %all-to-all-start = ((f32[32,16,128]{2,1,0:T(8,128)}), f32[32,16,128]{2,1,0:T(8,128)S(1)}, u32[]{:S(2)}, u32[]{:S(2)}) async-start(f32[32,16,128]{2,1,0:T(8,128)} %bitcast.5), calls=%async_computation | async-start | bytes 524288 | tf_op jit(solution)/shard_map/all_to_all | solution.py:514
  13.6 31.1 %copy-start.4 = (f32[128,512]{1,0:T(8,128)S(1)}, f32[128,512]{1,0:T(8,128)}, u32[]{:S(2)}) copy-start(f32[128,512]{1,0:T(8,128)} %innovation.1) | copy-start | bytes 786436
  13.6 31.1 %copy-start.3 = (f32[128,512]{1,0:T(8,128)S(1)}, f32[128,512]{1,0:T(8,128)}, u32[]{:S(2)}) copy-start(f32[128,512]{1,0:T(8,128)} %weight.1) | copy-start | bytes 786436
  13.7 33.0 %collective-permute-start.2 = (f32[256,128]{1,0:T(8,128)S(1)}, f32[256,128]{1,0:T(8,128)S(1)}, u32[]{:S(2)}, u32[]{:S(2)}) collective-permute-start(f32[256,128]{1,0:T(8,128)S(1)} %bitcast.72), channel_id=1, source_target_pairs={{0,0},{1,32},{2,64},{3,96},{32,128},{33,160},{34,192},{35,224},{64... | collective-permute-start | bytes 393224 | tf_op jit(solution)/shard_map/ppermute | solution.py:531
  21.5 25.1 %collective-permute-start.3 = (f32[256,128]{1,0:T(8,128)S(1)}, f32[256,128]{1,0:T(8,128)S(1)}, u32[]{:S(2)}, u32[]{:S(2)}) collective-permute-start(f32[256,128]{1,0:T(8,128)S(1)} %bitcast.73), channel_id=1, source_target_pairs={{0,128},{1,160},{2,192},{3,224},{32,0},{33,32},{34,64},{35,96},{64... | collective-permute-start | bytes 393224 | tf_op jit(solution)/shard_map/ppermute | solution.py:531
  24.5 20.2 %all-to-all-start.1 = ((f32[64,1,128]{2,1,0:T(1,128)}), f32[64,1,128]{2,1,0:T(1,128)S(1)}, u32[]{:S(2)}, u32[]{:S(2)}) async-start(f32[64,1,128]{2,1,0:T(1,128)} %bitcast.8), calls=%async_computation.1 | async-start | bytes 65536 | tf_op jit(solution)/shard_map/all_to_all | solution.py:543
  49.4 11.7 %copy-start.7 = (s32[8,128]{1,0:T(8,128)S(1)}, s32[8,128]{1,0:T(8,128)}, u32[]{:S(2)}) copy-start(s32[8,128]{1,0:T(8,128)} %own.1) | copy-start | bytes 12292
  49.4 11.7 %copy-start.1 = (f32[2,32,8,128]{3,2,1,0:T(8,128)S(1)}, f32[2,32,8,128]{3,2,1,0:T(8,128)}, u32[]{:S(2)}) copy-start(f32[2,32,8,128]{3,2,1,0:T(8,128)} %param.14) | copy-start | bytes 786436
  49.4 11.7 %copy-start.2 = (bf16[2,2,32,8,128]{4,3,2,1,0:T(8,128)(2,1)S(1)}, bf16[2,2,32,8,128]{4,3,2,1,0:T(8,128)(2,1)}, u32[]{:S(2)}) copy-start(bf16[2,2,32,8,128]{4,3,2,1,0:T(8,128)(2,1)} %param.15) | copy-start | bytes 786436
  49.4 17.7 %all-to-all-start.2 = ((f32[32,16,128]{2,1,0:T(8,128)}), f32[32,16,128]{2,1,0:T(8,128)S(1)}, u32[]{:S(2)}, u32[]{:S(2)}) async-start(f32[32,16,128]{2,1,0:T(8,128)} %bitcast.16), calls=%async_computation.2 | async-start | bytes 524288 | tf_op jit(solution)/shard_map/all_to_all | solution.py:514
  56.3 28.2 %collective-permute-start.6 = (f32[768,128]{1,0:T(8,128)}, f32[768,128]{1,0:T(8,128)S(1)}, u32[]{:S(2)}, u32[]{:S(2)}) collective-permute-start(f32[768,128]{1,0:T(8,128)} %get-tuple-element.60), channel_id=1, source_target_pairs={{0,0},{1,32},{2,64},{3,96},{32,128},{33,160},{34,192},{35,224},{64... | collective-permute-start | bytes 1179656 | tf_op jit(solution)/shard_map/ppermute | solution.py:531
  58.7 25.7 %collective-permute-start.7 = (f32[768,128]{1,0:T(8,128)S(1)}, f32[768,128]{1,0:T(8,128)S(1)}, u32[]{:S(2)}, u32[]{:S(2)}) collective-permute-start(f32[768,128]{1,0:T(8,128)S(1)} %get-tuple-element.61), channel_id=1, source_target_pairs={{0,128},{1,160},{2,192},{3,224},{32,0},{33,32},{34,64},{35,96},{64... | collective-permute-start | bytes 1179656 | tf_op jit(solution)/shard_map/ppermute | solution.py:531
  61.9 16.9 %collective-permute-start.8 = (f32[264,128]{1,0:T(8,128)}, f32[264,128]{1,0:T(8,128)}, u32[]{:S(2)}, u32[]{:S(2)}) collective-permute-start(f32[264,128]{1,0:T(8,128)} %get-tuple-element.66), channel_id=1, source_target_pairs={{0,4},{4,8},{8,12},{12,16},{16,20},{20,24},{24,28},{28,32},{32,36}... | collective-permute-start | bytes 405512 | tf_op jit(solution)/shard_map/ppermute | solution.py:557
  67.0 13.5 %collective-permute-start.9 = (f32[264,128]{1,0:T(8,128)S(1)}, f32[264,128]{1,0:T(8,128)}, u32[]{:S(2)}, u32[]{:S(2)}) collective-permute-start(f32[264,128]{1,0:T(8,128)S(1)} %get-tuple-element.67), channel_id=1, source_target_pairs={{0,252},{4,0},{8,4},{12,8},{16,12},{20,16},{24,20},{28,24},{32,28}... | collective-permute-start | bytes 405512 | tf_op jit(solution)/shard_map/ppermute | solution.py:558
  67.6 16.9 %collective-permute-start.4 = (f32[4,64,128]{2,1,0:T(8,128)S(1)}, f32[4,64,128]{2,1,0:T(8,128)S(1)}, u32[]{:S(2)}, u32[]{:S(2)}) collective-permute-start(f32[4,64,128]{2,1,0:T(8,128)S(1)} %get-tuple-element.59.high), channel_id=1, source_target_pairs={{0,4},{4,8},{8,12},{12,16},{16,20},{20,24},{24,28},{28,32},{32,36}... | collective-permute-start | bytes 393224 | tf_op jit(solution)/shard_map/ppermute | solution.py:579
  78.8 10.0 %collective-permute-start.5 = (f32[4,64,128]{2,1,0:T(8,128)S(1)}, f32[4,64,128]{2,1,0:T(8,128)S(1)}, u32[]{:S(2)}, u32[]{:S(2)}) collective-permute-start(f32[4,64,128]{2,1,0:T(8,128)S(1)} %get-tuple-element.58.low), channel_id=1, source_target_pairs={{0,252},{4,0},{8,4},{12,8},{16,12},{20,16},{24,20},{28,24},{32,28}... | collective-permute-start | bytes 393224 | tf_op jit(solution)/shard_map/ppermute | solution.py:579
  130.5 9.7 %collective-permute-start.10 = (f32[4,128,128]{2,1,0:T(8,128)S(1)}, f32[4,128,128]{2,1,0:T(8,128)S(1)}, u32[]{:S(2)}, u32[]{:S(2)}) collective-permute-start(f32[4,128,128]{2,1,0:T(8,128)S(1)} %get-tuple-element.72.high), channel_id=1, source_target_pairs={{0,4},{4,8},{8,12},{12,16},{16,20},{20,24},{24,28},{28,32},{32,36}... | collective-permute-start | bytes 786440 | tf_op jit(solution)/shard_map/ppermute | solution.py:579
  134.5 10.8 %collective-permute-start.11 = (f32[4,128,128]{2,1,0:T(8,128)S(1)}, f32[4,128,128]{2,1,0:T(8,128)S(1)}, u32[]{:S(2)}, u32[]{:S(2)}) collective-permute-start(f32[4,128,128]{2,1,0:T(8,128)S(1)} %get-tuple-element.71.low), channel_id=1, source_target_pairs={{0,252},{4,0},{8,4},{12,8},{16,12},{20,16},{24,20},{28,24},{32,28}... | collective-permute-start | bytes 786440 | tf_op jit(solution)/shard_map/ppermute | solution.py:579
  161.2 13.6 %all-to-all-start.6 = ((f32[32,16,128]{2,1,0:T(8,128)}), f32[32,16,128]{2,1,0:T(8,128)}, u32[]{:S(2)}, u32[]{:S(2)}) async-start(f32[32,16,128]{2,1,0:T(8,128)} %bitcast.26), calls=%async_computation.6 | async-start | bytes 524288 | tf_op jit(solution)/shard_map/all_to_all | solution.py:514
  171.2 8.1 %collective-permute-start.14 = (f32[256,128]{1,0:T(8,128)}, f32[256,128]{1,0:T(8,128)S(1)}, u32[]{:S(2)}, u32[]{:S(2)}) collective-permute-start(f32[256,128]{1,0:T(8,128)} %get-tuple-element.78), channel_id=1, source_target_pairs={{0,4},{4,8},{8,12},{12,16},{16,20},{20,24},{24,28},{28,32},{32,36}... | collective-permute-start | bytes 393224 | tf_op jit(solution)/shard_map/ppermute | solution.py:604
  171.2 8.8 %collective-permute-start.15 = (f32[256,128]{1,0:T(8,128)}, f32[256,128]{1,0:T(8,128)S(1)}, u32[]{:S(2)}, u32[]{:S(2)}) collective-permute-start(f32[256,128]{1,0:T(8,128)} %get-tuple-element.79), channel_id=1, source_target_pairs={{0,252},{4,0},{8,4},{12,8},{16,12},{20,16},{24,20},{28,24},{32,28}... | collective-permute-start | bytes 393224 | tf_op jit(solution)/shard_map/ppermute | solution.py:605
  176.3 6.1 %collective-permute-start.12 = (f32[4,64,128]{2,1,0:T(8,128)S(1)}, f32[4,64,128]{2,1,0:T(8,128)S(1)}, u32[]{:S(2)}, u32[]{:S(2)}) collective-permute-start(f32[4,64,128]{2,1,0:T(8,128)S(1)} %get-tuple-element.76.high), channel_id=1, source_target_pairs={{0,4},{4,8},{8,12},{12,16},{16,20},{20,24},{24,28},{28,32},{32,36}... | collective-permute-start | bytes 393224 | tf_op jit(solution)/shard_map/ppermute | solution.py:579
  179.3 8.2 %collective-permute-start.13 = (f32[4,64,128]{2,1,0:T(8,128)S(1)}, f32[4,64,128]{2,1,0:T(8,128)S(1)}, u32[]{:S(2)}, u32[]{:S(2)}) collective-permute-start(f32[4,64,128]{2,1,0:T(8,128)S(1)} %get-tuple-element.75.low), channel_id=1, source_target_pairs={{0,252},{4,0},{8,4},{12,8},{16,12},{20,16},{24,20},{28,24},{32,28}... | collective-permute-start | bytes 393224 | tf_op jit(solution)/shard_map/ppermute | solution.py:579
  225.2 12.2 %collective-permute-start.16 = (f32[4,128,128]{2,1,0:T(8,128)S(1)}, f32[4,128,128]{2,1,0:T(8,128)S(1)}, u32[]{:S(2)}, u32[]{:S(2)}) collective-permute-start(f32[4,128,128]{2,1,0:T(8,128)S(1)} %get-tuple-element.81.high), channel_id=1, source_target_pairs={{0,4},{4,8},{8,12},{12,16},{16,20},{20,24},{24,28},{28,32},{32,36}... | collective-permute-start | bytes 786440 | tf_op jit(solution)/shard_map/ppermute | solution.py:579
  231.8 10.8 %collective-permute-start.17 = (f32[4,128,128]{2,1,0:T(8,128)S(1)}, f32[4,128,128]{2,1,0:T(8,128)S(1)}, u32[]{:S(2)}, u32[]{:S(2)}) collective-permute-start(f32[4,128,128]{2,1,0:T(8,128)S(1)} %get-tuple-element.80.low), channel_id=1, source_target_pairs={{0,252},{4,0},{8,4},{12,8},{16,12},{20,16},{24,20},{28,24},{32,28}... | collective-permute-start | bytes 786440 | tf_op jit(solution)/shard_map/ppermute | solution.py:579
  258.4 16.1 %all-to-all-start.10 = ((f32[32,32,128]{2,1,0:T(8,128)}), f32[32,32,128]{2,1,0:T(8,128)S(1)}, u32[]{:S(2)}, u32[]{:S(2)}) async-start(f32[32,32,128]{2,1,0:T(8,128)} %bitcast.34), calls=%async_computation.10 | async-start | bytes 1048576 | tf_op jit(solution)/shard_map/all_to_all | solution.py:514
  267.1 15.1 %collective-permute-start.20 = (f32[256,128]{1,0:T(8,128)S(1)}, f32[256,128]{1,0:T(8,128)S(1)}, u32[]{:S(2)}, u32[]{:S(2)}) collective-permute-start(f32[256,128]{1,0:T(8,128)S(1)} %get-tuple-element.86), channel_id=1, source_target_pairs={{0,4},{4,8},{8,12},{12,16},{16,20},{20,24},{24,28},{28,32},{32,36}... | collective-permute-start | bytes 393224 | tf_op jit(solution)/shard_map/ppermute | solution.py:604
  269.0 13.3 %collective-permute-start.21 = (f32[256,128]{1,0:T(8,128)S(1)}, f32[256,128]{1,0:T(8,128)S(1)}, u32[]{:S(2)}, u32[]{:S(2)}) collective-permute-start(f32[256,128]{1,0:T(8,128)S(1)} %get-tuple-element.87), channel_id=1, source_target_pairs={{0,252},{4,0},{8,4},{12,8},{16,12},{20,16},{24,20},{28,24},{32,28}... | collective-permute-start | bytes 393224 | tf_op jit(solution)/shard_map/ppermute | solution.py:605
  275.9 10.2 %collective-permute-start.18 = (f32[4,64,128]{2,1,0:T(8,128)S(1)}, f32[4,64,128]{2,1,0:T(8,128)S(1)}, u32[]{:S(2)}, u32[]{:S(2)}) collective-permute-start(f32[4,64,128]{2,1,0:T(8,128)S(1)} %get-tuple-element.84.high), channel_id=1, source_target_pairs={{0,4},{4,8},{8,12},{12,16},{16,20},{20,24},{24,28},{28,32},{32,36}... | collective-permute-start | bytes 393224 | tf_op jit(solution)/shard_map/ppermute | solution.py:579
  282.3 9.0 %collective-permute-start.19 = (f32[4,64,128]{2,1,0:T(8,128)S(1)}, f32[4,64,128]{2,1,0:T(8,128)S(1)}, u32[]{:S(2)}, u32[]{:S(2)}) collective-permute-start(f32[4,64,128]{2,1,0:T(8,128)S(1)} %get-tuple-element.83.low), channel_id=1, source_target_pairs={{0,252},{4,0},{8,4},{12,8},{16,12},{20,16},{24,20},{28,24},{32,28}... | collective-permute-start | bytes 393224 | tf_op jit(solution)/shard_map/ppermute | solution.py:579
  (9 other events, 72.6 us)

commit v3 on v2

--- a/solution.py
+++ b/solution.py
@@ -129,6 +129,7 @@
     for j, target in enumerate((first, second)):
         for k in range(4):
             target[k * 64 : k * 64 + 64] = shared[k * 128 + 64 : k * 128 + 128]
+            target[768 + k * 64 : 832 + k * 64] = shared[k * 128 : k * 128 + 64]
         tile = lax.rem(z + level + 4 * j + 3 * lax.rem(z, 2), 8) * 8 + ((row >> 4) & 7)
         mine = one_hot((source == tile) & (rank == place))
         for kind, values in enumerate((weight, innovation)):
@@ -144,7 +145,7 @@
             block = lax.bitwise_xor(lax.rem(turn, 4), k)
             rows = pl.ds(pl.multiple_of(block * 32, 32), 32)
             for var in range(2):
-                start = k * 64 + var * 32
+                start = 768 + k * 64 + var * 32
                 matrices[half * 2 + var, rows, :] = part[start : start + 32]
 
 
@@ -537,16 +538,13 @@
     request, ranks = call(request_kernel, [((64, 128), f32), ((1, 512), i32)], total=2)(
         source_row, obs_column.reshape(1, 512)
     )
-    matrices = shared.reshape(4, 128, 128)[:, :64].reshape(256, 128)
-    matrices = [spread(matrices, j) for j in range(2)]
-    request, arrived = lax.optimization_barrier((request, to_plane(packed)))
+    parts = call(slots_kernel, [((1024, 128), f32), ((1024, 128), f32)], smem=1, total=6)(
+        here, source_row, ranks, obs_weight, innovation, shared
+    )
+    request, parts, arrived = lax.optimization_barrier((request, parts, to_plane(packed)))
+    parts = [spread(parts[j], j) for j in range(2)]
     wanted = lax.all_to_all(request, TILE, 0, 0, tiled=True)
-    arrived, wanted, control_ens, ranks = lax.optimization_barrier((arrived, wanted, control_ens, ranks))
-    parts = call(slots_kernel, [((768, 128), f32), ((768, 128), f32)], smem=1, total=6)(
-        here, source_row, ranks, obs_weight, innovation, shared
-    )
-    parts, arrived = lax.optimization_barrier((parts, arrived))
-    parts = [spread(parts[j], j) for j in range(2)]
+    arrived, wanted, parts, control_ens = lax.optimization_barrier((arrived, wanted, parts, control_ens))
 
     send_up, send_down, ens, perts = call(
         begin_members_kernel,
@@ -565,7 +563,7 @@
         [((4, 128, 128), f32)],
         smem=1,
         total=4,
-    )(here, arrived, *matrices)
+    )(here, arrived, *parts)
 
     (faces,) = call(weights_kernel, [((2, 5, 16, 128), f32)], [((2, 24, 128), f32)], smem=1, total=4)(
         scales, marks_before, scale_class, marks_after
@@ -584,8 +582,6 @@
     for iteration in range(ITERS):
         low, high = call(edges_kernel, [half_shape, half_shape], total=2)(owner, to_plane(out))
         before, after = halos(low, high)
-        if iteration == 0:
-            before, after, parts = lax.optimization_barrier((before, after, parts))
         members = members_of(ens, ens_before, ens_after)
         (outgoing,) = call(
             observe_kernel, [((1024, 128), f32)], [scratch, ((4, 128, 256), bf16)], total=7
@@ -610,7 +606,7 @@
             [((4, 128, 128), f32)],
             smem=1,
             total=5,
-        )(here, to_plane(packed), *matrices, state)
+        )(here, to_plane(packed), *parts, state)
         if not last:
             state = results[0]
         out = results[-1]

time: 295 us -> 290 us (0.983)
  blocking collectives: 85.4 us -> 107 us
  starting transfers between devices: 92.5 us -> 74.8 us
  waiting for transfers between devices: 60.4 us -> 55 us
    all_to_all x0 -> x1, blocking collectives: none -> 26.3 us  [on_device(): wanted = lax.all_to_all(request, TILE, 0, 0, tiled=True)]
    all_to_all x1 -> x0, starting transfers between devices: 13 us -> none  [on_device(): wanted = lax.all_to_all(request, TILE, 0, 0, tiled=True)]
    all_to_all x1 -> x0, waiting for transfers between devices: 7.09 us -> none  [on_device(): wanted = lax.all_to_all(request, TILE, 0, 0, tiled=True)]
    all_to_all x4, waiting for transfers between devices: 6.84 us -> 13.2 us  [to_plane(): return lax.all_to_all(value, PLANE, 0, 0, tiled=True)]
    ppermute x1, waiting for transfers between devices: 6.13 us -> 0.01 us  [on_device(): from_before = lax.ppermute(send_up, TILE, upward)]
    ppermute x4 -> x2, starting transfers between devices: 14.6 us -> 9.65 us  [spread(): return lax.ppermute(value, ('z',) + LEV, exchange[j * 32:j * 32 + 32])]
    all_to_all x6, blocking collectives: 85.4 us -> 80.9 us  [to_plane(): return lax.all_to_all(value, PLANE, 0, 0, tiled=True)]
    ppermute x1, starting transfers between devices: 5.13 us -> 1.56 us  [on_device(): from_before = lax.ppermute(send_up, TILE, upward)]
  transfers between devices with their start and end apart: 27 -> 24, of which waited for: 15 -> 16; matrix products, arithmetic and copies ran while one was open for 1% -> 0% of each run, Pallas kernels for 6% -> 6%
where the time goes in v3:
time: 290 us; the launch traced here: 289 us
  blocking collectives  107 us (37%)
  starting transfers between devices  74.8 us (26%)
  waiting for transfers between devices  55 us (19%)
  Pallas kernels  46 us (16%)
  local copies, waits for them, and re-layouts  3.32 us (1%)
    all_to_all x6, blocking collectives, to_plane(): return lax.all_to_all(value, PLANE, 0, 0, tiled=True)  80.9 us
    ppermute x10, waiting for transfers between devices, halos(): return (lax.ppermute(high, TILE, upward), lax.ppermute(low, TILE, downward))  41.1 us
    ppermute x10, starting transfers between devices, halos(): return (lax.ppermute(high, TILE, upward), lax.ppermute(low, TILE, downward))  28.3 us
    all_to_all x4, starting transfers between devices, to_plane(): return lax.all_to_all(value, PLANE, 0, 0, tiled=True)  28.3 us
    all_to_all x1, blocking collectives, on_device(): wanted = lax.all_to_all(request, TILE, 0, 0, tiled=True)  26.3 us
    all_to_all x4, waiting for transfers between devices, to_plane(): return lax.all_to_all(value, PLANE, 0, 0, tiled=True)  13.2 us
    ppermute x2, starting transfers between devices, spread(): return lax.ppermute(value, ('z',) + LEV, exchange[j * 32:j * 32 + 32])  9.65 us
    pallas_call x2, Pallas kernels, on_device(): call(observe_kernel, [((1024, 128), f32)], [scratch, ((4, 128, 256), bf16...  9.03 us
  transfers between devices with their start and end apart: 24, of which 16 were waited for; matrix products, arithmetic and copies ran while one was open for 0% of the time, Pallas kernels for 6%

profile of v3, /device:TPU:46, one launch (start us, length us, event | category | flops | bytes accessed | tf_op | source)
XLA Modules:
  0.0 289.2 jit_solution(1371253935916775487)
XLA Ops:
  3.5 2.4 collective-permute-start.1
  7.1 6.3 %all-to-all-start = ((f32[32,16,128]{2,1,0:T(8,128)}), f32[32,16,128]{2,1,0:T(8,128)S(1)}, u32[]{:S(2)}, u32[]{:S(2)}) async-start(f32[32,16,128]{2,1,0:T(8,128)} %bitcast.9), calls=%async_computation | async-start | bytes 524288 | tf_op jit(solution)/shard_map/all_to_all | solution.py:515
  19.2 7.7 %collective-permute-start.2 = (f32[1024,128]{1,0:T(8,128)S(1)}, f32[1024,128]{1,0:T(8,128)S(1)}, u32[]{:S(2)}, u32[]{:S(2)}) collective-permute-start(f32[1024,128]{1,0:T(8,128)S(1)} %get-tuple-element.49), channel_id=1, source_target_pairs={{0,0},{1,32},{2,64},{3,96},{32,128},{33,160},{34,192},{35,224},{64... | collective-permute-start | bytes 1572872 | tf_op jit(solution)/shard_map/ppermute | solution.py:532
  28.9 26.3 %all_to_all.123 = f32[64,1,128]{2,1,0:T(1,128)S(1)} all-to-all(f32[64,1,128]{2,1,0:T(1,128)S(1)} %bitcast.60), channel_id=1, replica_groups=mesh['z'=8,'yl'=2,'x'=4,'yh'=2,'core'=2] {'z','yl','x'}, dimensions={0} | all-to-all | bytes 65536 | tf_op jit(solution)/shard_map/all_to_all | solution.py:546
  57.9 7.2 %all-to-all-start.2 = ((f32[32,16,128]{2,1,0:T(8,128)}), f32[32,16,128]{2,1,0:T(8,128)S(1)}, u32[]{:S(2)}, u32[]{:S(2)}) async-start(f32[32,16,128]{2,1,0:T(8,128)} %bitcast.14), calls=%async_computation.2 | async-start | bytes 524288 | tf_op jit(solution)/shard_map/all_to_all | solution.py:515
  67.4 4.1 %all-to-all-done.2 = f32[32,16,128]{2,1,0:T(8,128)S(1)} async-done(((f32[32,16,128]{2,1,0:T(8,128)}), f32[32,16,128]{2,1,0:T(8,128)S(1)}, u32[]{:S(2)}, u32[]{:S(2)}) %all-to-all-start.2) | async-done | bytes 262176 | tf_op jit(solution)/shard_map/all_to_all | solution.py:515
  72.0 6.8 %collective-permute-start.4 = (f32[4,64,128]{2,1,0:T(8,128)S(1)}, f32[4,64,128]{2,1,0:T(8,128)S(1)}, u32[]{:S(2)}, u32[]{:S(2)}) collective-permute-start(f32[4,64,128]{2,1,0:T(8,128)S(1)} %get-tuple-element.57.high), channel_id=1, source_target_pairs={{0,4},{4,8},{8,12},{12,16},{16,20},{20,24},{24,28},{28,32},{32,36}... | collective-permute-start | bytes 393224 | tf_op jit(solution)/shard_map/ppermute | solution.py:577
  82.0 5.2 %collective-permute-done.5.after = f32[4,64,128]{2,1,0:T(8,128)S(1)} collective-permute-done((f32[4,64,128]{2,1,0:T(8,128)S(1)}, f32[4,64,128]{2,1,0:T(8,128)S(1)}, u32[]{:S(2)}, u32[]{:S(2)}) %collective-permute-start.5) | collective-permute-done | bytes 131104 | tf_op jit(solution)/shard_map/ppermute | solution.py:577
  87.2 4.5 %shard_map.156 = f32[1024,128]{1,0:T(8,128)S(1)} custom-call(f32[64,128]{1,0:T(8,128)S(1)} %bitcast.52, f32[4,64,128]{2,1,0:T(8,128)S(1)} %get-tuple-element.56.low, f32[4,64,128]{2,1,0:T(8,128)S(1)} %get-tuple-element.57.high, f32[4,64,128]{2,1,0:T(8,128)S(1)} %collective-permute-done.4.before, f32[4,64,128]{2,1,0:T(8,128)S(1)} %collective-permute-done.5.after, ...), custom_call_target="tpu_custom_call" | custom-call | flops 100000000 | bytes 6000000 | tf_op jit(solution)/shard_map/pallas_call | solution.py:586
  91.7 14.0 %all_to_all.124 = f32[32,32,128]{2,1,0:T(8,128)S(1)} all-to-all(f32[32,32,128]{2,1,0:T(8,128)S(1)} %bitcast.45), channel_id=1, replica_groups=mesh['z'=8,'yl'=2,'x'=4,'yh'=2,'core'=2] {'yl','x','yh','core'}, dimensions={0} | all-to-all | bytes 1048576 | tf_op jit(solution)/shard_map/all_to_all | solution.py:515
  107.3 15.1 %all_to_all.125 = f32[32,32,128]{2,1,0:T(8,128)S(1)} all-to-all(f32[32,32,128]{2,1,0:T(8,128)S(1)} %bitcast.39), channel_id=1, replica_groups=mesh['z'=8,'yl'=2,'x'=4,'yh'=2,'core'=2] {'yl','x','yh','core'}, dimensions={0} | all-to-all | bytes 1048576 | tf_op jit(solution)/shard_map/all_to_all | solution.py:515
  124.6 4.3 %collective-permute-start.8 = (f32[4,128,128]{2,1,0:T(8,128)S(1)}, f32[4,128,128]{2,1,0:T(8,128)S(1)}, u32[]{:S(2)}, u32[]{:S(2)}) collective-permute-start(f32[4,128,128]{2,1,0:T(8,128)S(1)} %get-tuple-element.64.high), channel_id=1, source_target_pairs={{0,4},{4,8},{8,12},{12,16},{16,20},{20,24},{24,28},{28,32},{32,36}... | collective-permute-start | bytes 786440 | tf_op jit(solution)/shard_map/ppermute | solution.py:577
  128.9 5.6 %collective-permute-done.8.before = f32[4,128,128]{2,1,0:T(8,128)S(1)} collective-permute-done((f32[4,128,128]{2,1,0:T(8,128)S(1)}, f32[4,128,128]{2,1,0:T(8,128)S(1)}, u32[]{:S(2)}, u32[]{:S(2)}) %collective-permute-start.8) | collective-permute-done | bytes 262176 | tf_op jit(solution)/shard_map/ppermute | solution.py:577
  134.6 5.2 %collective-permute-done.9.after = f32[4,128,128]{2,1,0:T(8,128)S(1)} collective-permute-done((f32[4,128,128]{2,1,0:T(8,128)S(1)}, f32[4,128,128]{2,1,0:T(8,128)S(1)}, u32[]{:S(2)}, u32[]{:S(2)}) %collective-permute-start.9) | collective-permute-done | bytes 262176 | tf_op jit(solution)/shard_map/ppermute | solution.py:577
  141.9 11.4 %all_to_all.126 = f32[32,16,128]{2,1,0:T(8,128)S(1)} all-to-all(f32[32,16,128]{2,1,0:T(8,128)S(1)} %bitcast.49), channel_id=1, replica_groups=mesh['z'=8,'yl'=2,'x'=4,'yh'=2,'core'=2] {'yl','x','yh','core'}, dimensions={0} | all-to-all | bytes 524288 | tf_op jit(solution)/shard_map/all_to_all | solution.py:515
  155.6 7.7 %all-to-all-start.6 = ((f32[32,16,128]{2,1,0:T(8,128)}), f32[32,16,128]{2,1,0:T(8,128)}, u32[]{:S(2)}, u32[]{:S(2)}) async-start(f32[32,16,128]{2,1,0:T(8,128)} %bitcast.24), calls=%async_computation.6 | async-start | bytes 524288 | tf_op jit(solution)/shard_map/all_to_all | solution.py:515
  163.3 2.3 shard_map.162
  170.6 5.1 %collective-permute-start.10 = (f32[4,64,128]{2,1,0:T(8,128)S(1)}, f32[4,64,128]{2,1,0:T(8,128)S(1)}, u32[]{:S(2)}, u32[]{:S(2)}) collective-permute-start(f32[4,64,128]{2,1,0:T(8,128)S(1)} %get-tuple-element.68.high), channel_id=1, source_target_pairs={{0,4},{4,8},{8,12},{12,16},{16,20},{20,24},{24,28},{28,32},{32,36}... | collective-permute-start | bytes 393224 | tf_op jit(solution)/shard_map/ppermute | solution.py:577
  178.8 5.2 %collective-permute-done.11.after = f32[4,64,128]{2,1,0:T(8,128)S(1)} collective-permute-done((f32[4,64,128]{2,1,0:T(8,128)S(1)}, f32[4,64,128]{2,1,0:T(8,128)S(1)}, u32[]{:S(2)}, u32[]{:S(2)}) %collective-permute-start.11) | collective-permute-done | bytes 131104 | tf_op jit(solution)/shard_map/ppermute | solution.py:577
  184.0 4.5 %shard_map.164 = f32[1024,128]{1,0:T(8,128)S(1)} custom-call(f32[64,128]{1,0:T(8,128)S(1)} %bitcast.54, f32[4,64,128]{2,1,0:T(8,128)S(1)} %get-tuple-element.67.low, f32[4,64,128]{2,1,0:T(8,128)S(1)} %get-tuple-element.68.high, f32[4,64,128]{2,1,0:T(8,128)S(1)} %collective-permute-done.10.before, f32[4,64,128]{2,1,0:T(8,128)S(1)} %collective-permute-done.11.after, ...), custom_call_target="tpu_custom_call" | custom-call | flops 100000000 | bytes 6000000 | tf_op jit(solution)/shard_map/pallas_call | solution.py:586
  188.5 14.0 %all_to_all.127 = f32[32,32,128]{2,1,0:T(8,128)S(1)} all-to-all(f32[32,32,128]{2,1,0:T(8,128)S(1)} %bitcast.46), channel_id=1, replica_groups=mesh['z'=8,'yl'=2,'x'=4,'yh'=2,'core'=2] {'yl','x','yh','core'}, dimensions={0} | all-to-all | bytes 1048576 | tf_op jit(solution)/shard_map/all_to_all | solution.py:515
  204.1 15.1 %all_to_all.128 = f32[32,32,128]{2,1,0:T(8,128)S(1)} all-to-all(f32[32,32,128]{2,1,0:T(8,128)S(1)} %bitcast.41), channel_id=1, replica_groups=mesh['z'=8,'yl'=2,'x'=4,'yh'=2,'core'=2] {'yl','x','yh','core'}, dimensions={0} | all-to-all | bytes 1048576 | tf_op jit(solution)/shard_map/all_to_all | solution.py:515
  221.4 5.7 %collective-permute-start.14 = (f32[4,128,128]{2,1,0:T(8,128)S(1)}, f32[4,128,128]{2,1,0:T(8,128)S(1)}, u32[]{:S(2)}, u32[]{:S(2)}) collective-permute-start(f32[4,128,128]{2,1,0:T(8,128)S(1)} %get-tuple-element.73.high), channel_id=1, source_target_pairs={{0,4},{4,8},{8,12},{12,16},{16,20},{20,24},{24,28},{28,32},{32,36}... | collective-permute-start | bytes 786440 | tf_op jit(solution)/shard_map/ppermute | solution.py:577
  227.1 5.6 %collective-permute-done.14.before = f32[4,128,128]{2,1,0:T(8,128)S(1)} collective-permute-done((f32[4,128,128]{2,1,0:T(8,128)S(1)}, f32[4,128,128]{2,1,0:T(8,128)S(1)}, u32[]{:S(2)}, u32[]{:S(2)}) %collective-permute-start.14) | collective-permute-done | bytes 262176 | tf_op jit(solution)/shard_map/ppermute | solution.py:577
  232.7 5.2 %collective-permute-done.15.after = f32[4,128,128]{2,1,0:T(8,128)S(1)} collective-permute-done((f32[4,128,128]{2,1,0:T(8,128)S(1)}, f32[4,128,128]{2,1,0:T(8,128)S(1)}, u32[]{:S(2)}, u32[]{:S(2)}) %collective-permute-start.15) | collective-permute-done | bytes 262176 | tf_op jit(solution)/shard_map/ppermute | solution.py:577
  240.0 11.3 %all_to_all.129 = f32[32,16,128]{2,1,0:T(8,128)S(1)} all-to-all(f32[32,16,128]{2,1,0:T(8,128)S(1)} %bitcast.50), channel_id=1, replica_groups=mesh['z'=8,'yl'=2,'x'=4,'yh'=2,'core'=2] {'yl','x','yh','core'}, dimensions={0} | all-to-all | bytes 524288 | tf_op jit(solution)/shard_map/all_to_all | solution.py:515
  251.3 2.4 shard_map.168
  253.7 7.1 %all-to-all-start.10 = ((f32[32,32,128]{2,1,0:T(8,128)}), f32[32,32,128]{2,1,0:T(8,128)S(1)}, u32[]{:S(2)}, u32[]{:S(2)}) async-start(f32[32,32,128]{2,1,0:T(8,128)} %bitcast.32), calls=%async_computation.10 | async-start | bytes 1048576 | tf_op jit(solution)/shard_map/all_to_all | solution.py:515
  264.5 5.3 %all-to-all-done.10 = f32[32,32,128]{2,1,0:T(8,128)S(1)} async-done(((f32[32,32,128]{2,1,0:T(8,128)}), f32[32,32,128]{2,1,0:T(8,128)S(1)}, u32[]{:S(2)}, u32[]{:S(2)}) %all-to-all-start.10) | async-done | bytes 524320 | tf_op jit(solution)/shard_map/all_to_all | solution.py:515
  271.2 6.4 %collective-permute-start.16 = (f32[4,64,128]{2,1,0:T(8,128)S(1)}, f32[4,64,128]{2,1,0:T(8,128)S(1)}, u32[]{:S(2)}, u32[]{:S(2)}) collective-permute-start(f32[4,64,128]{2,1,0:T(8,128)S(1)} %get-tuple-element.76.high), channel_id=1, source_target_pairs={{0,4},{4,8},{8,12},{12,16},{16,20},{20,24},{24,28},{28,32},{32,36}... | collective-permute-start | bytes 393224 | tf_op jit(solution)/shard_map/ppermute | solution.py:577
  281.4 5.2 %collective-permute-done.17.after = f32[4,64,128]{2,1,0:T(8,128)S(1)} collective-permute-done((f32[4,64,128]{2,1,0:T(8,128)S(1)}, f32[4,64,128]{2,1,0:T(8,128)S(1)}, u32[]{:S(2)}, u32[]{:S(2)}) %collective-permute-start.17) | collective-permute-done | bytes 131104 | tf_op jit(solution)/shard_map/ppermute | solution.py:577
  286.6 2.6 shard_map.172
  (87 shorter events, 51.4 us)
Async XLA Ops:
  0.6 5.3 %copy-start = (f32[2,32,8,128]{3,2,1,0:T(8,128)S(1)}, f32[2,32,8,128]{3,2,1,0:T(8,128)}, u32[]{:S(2)}) copy-start(f32[2,32,8,128]{3,2,1,0:T(8,128)} %param.13) | copy-start | bytes 786436
  1.5 1.3 collective-permute-start
  3.5 11.1 %collective-permute-start.1 = (f32[256,128]{1,0:T(8,128)S(1)}, f32[256,128]{1,0:T(8,128)S(1)}, u32[]{:S(2)}, u32[]{:S(2)}) collective-permute-start(f32[256,128]{1,0:T(8,128)S(1)} %pad_maximum_fusion.1), channel_id=1, source_target_pairs={{0,2},{2,0},{1,3},{3,1},{4,6},{6,4},{5,7},{7,5},{8,10},{10,8},{9,1... | collective-permute-start | bytes 393224 | tf_op jit(solution)/shard_map/ppermute | solution.py:526
  7.1 12.1 %all-to-all-start = ((f32[32,16,128]{2,1,0:T(8,128)}), f32[32,16,128]{2,1,0:T(8,128)S(1)}, u32[]{:S(2)}, u32[]{:S(2)}) async-start(f32[32,16,128]{2,1,0:T(8,128)} %bitcast.9), calls=%async_computation | async-start | bytes 524288 | tf_op jit(solution)/shard_map/all_to_all | solution.py:515
  14.6 1.0 copy-start.4
  19.2 36.0 %collective-permute-start.2 = (f32[1024,128]{1,0:T(8,128)S(1)}, f32[1024,128]{1,0:T(8,128)S(1)}, u32[]{:S(2)}, u32[]{:S(2)}) collective-permute-start(f32[1024,128]{1,0:T(8,128)S(1)} %get-tuple-element.49), channel_id=1, source_target_pairs={{0,0},{1,32},{2,64},{3,96},{32,128},{33,160},{34,192},{35,224},{64... | collective-permute-start | bytes 1572872 | tf_op jit(solution)/shard_map/ppermute | solution.py:532
  26.9 28.2 %collective-permute-start.3 = (f32[1024,128]{1,0:T(8,128)S(1)}, f32[1024,128]{1,0:T(8,128)S(1)}, u32[]{:S(2)}, u32[]{:S(2)}) collective-permute-start(f32[1024,128]{1,0:T(8,128)S(1)} %get-tuple-element.50), channel_id=1, source_target_pairs={{0,128},{1,160},{2,192},{3,224},{32,0},{33,32},{34,64},{35,96},{64... | collective-permute-start | bytes 1572872 | tf_op jit(solution)/shard_map/ppermute | solution.py:532
  55.2 9.9 %copy-start.7 = (s32[8,128]{1,0:T(8,128)S(1)}, s32[8,128]{1,0:T(8,128)}, u32[]{:S(2)}) copy-start(s32[8,128]{1,0:T(8,128)} %own.1) | copy-start | bytes 12292
  57.9 7.2 %copy-start.1 = (f32[2,32,8,128]{3,2,1,0:T(8,128)S(1)}, f32[2,32,8,128]{3,2,1,0:T(8,128)}, u32[]{:S(2)}) copy-start(f32[2,32,8,128]{3,2,1,0:T(8,128)} %param.14) | copy-start | bytes 786436
  57.9 7.3 %copy-start.2 = (bf16[2,2,32,8,128]{4,3,2,1,0:T(8,128)(2,1)S(1)}, bf16[2,2,32,8,128]{4,3,2,1,0:T(8,128)(2,1)}, u32[]{:S(2)}) copy-start(bf16[2,2,32,8,128]{4,3,2,1,0:T(8,128)(2,1)} %param.15) | copy-start | bytes 786436
  57.9 13.6 %all-to-all-start.2 = ((f32[32,16,128]{2,1,0:T(8,128)}), f32[32,16,128]{2,1,0:T(8,128)S(1)}, u32[]{:S(2)}, u32[]{:S(2)}) async-start(f32[32,16,128]{2,1,0:T(8,128)} %bitcast.14), calls=%async_computation.2 | async-start | bytes 524288 | tf_op jit(solution)/shard_map/all_to_all | solution.py:515
  65.3 13.6 %collective-permute-start.6 = (f32[264,128]{1,0:T(8,128)S(1)}, f32[264,128]{1,0:T(8,128)S(1)}, u32[]{:S(2)}, u32[]{:S(2)}) collective-permute-start(f32[264,128]{1,0:T(8,128)S(1)} %get-tuple-element.60), channel_id=1, source_target_pairs={{0,4},{4,8},{8,12},{12,16},{16,20},{20,24},{24,28},{28,32},{32,36}... | collective-permute-start | bytes 405512 | tf_op jit(solution)/shard_map/ppermute | solution.py:555
  66.9 12.0 %collective-permute-start.7 = (f32[264,128]{1,0:T(8,128)S(1)}, f32[264,128]{1,0:T(8,128)S(1)}, u32[]{:S(2)}, u32[]{:S(2)}) collective-permute-start(f32[264,128]{1,0:T(8,128)S(1)} %get-tuple-element.61), channel_id=1, source_target_pairs={{0,252},{4,0},{8,4},{12,8},{16,12},{20,16},{24,20},{28,24},{32,28}... | collective-permute-start | bytes 405512 | tf_op jit(solution)/shard_map/ppermute | solution.py:556
  72.0 6.8 %copy-start.12 = (f32[8]{0:T(128)S(1)}, f32[8]{0:T(128)}, u32[]{:S(2)}) copy-start(f32[8]{0:T(128)} %param.20) | copy-start | bytes 100
  72.0 6.8 %copy-start.13 = (f32[8]{0:T(128)S(1)}, f32[8]{0:T(128)}, u32[]{:S(2)}) copy-start(f32[8]{0:T(128)} %param.19) | copy-start | bytes 100
  72.0 9.9 %collective-permute-start.4 = (f32[4,64,128]{2,1,0:T(8,128)S(1)}, f32[4,64,128]{2,1,0:T(8,128)S(1)}, u32[]{:S(2)}, u32[]{:S(2)}) collective-permute-start(f32[4,64,128]{2,1,0:T(8,128)S(1)} %get-tuple-element.57.high), channel_id=1, source_target_pairs={{0,4},{4,8},{8,12},{12,16},{16,20},{20,24},{24,28},{28,32},{32,36}... | collective-permute-start | bytes 393224 | tf_op jit(solution)/shard_map/ppermute | solution.py:577
  78.8 8.4 %collective-permute-start.5 = (f32[4,64,128]{2,1,0:T(8,128)S(1)}, f32[4,64,128]{2,1,0:T(8,128)S(1)}, u32[]{:S(2)}, u32[]{:S(2)}) collective-permute-start(f32[4,64,128]{2,1,0:T(8,128)S(1)} %get-tuple-element.56.low), channel_id=1, source_target_pairs={{0,252},{4,0},{8,4},{12,8},{16,12},{20,16},{24,20},{28,24},{32,28}... | collective-permute-start | bytes 393224 | tf_op jit(solution)/shard_map/ppermute | solution.py:577
  124.6 10.0 %collective-permute-start.8 = (f32[4,128,128]{2,1,0:T(8,128)S(1)}, f32[4,128,128]{2,1,0:T(8,128)S(1)}, u32[]{:S(2)}, u32[]{:S(2)}) collective-permute-start(f32[4,128,128]{2,1,0:T(8,128)S(1)} %get-tuple-element.64.high), channel_id=1, source_target_pairs={{0,4},{4,8},{8,12},{12,16},{16,20},{20,24},{24,28},{28,32},{32,36}... | collective-permute-start | bytes 786440 | tf_op jit(solution)/shard_map/ppermute | solution.py:577
  128.9 10.8 %collective-permute-start.9 = (f32[4,128,128]{2,1,0:T(8,128)S(1)}, f32[4,128,128]{2,1,0:T(8,128)S(1)}, u32[]{:S(2)}, u32[]{:S(2)}) collective-permute-start(f32[4,128,128]{2,1,0:T(8,128)S(1)} %get-tuple-element.63.low), channel_id=1, source_target_pairs={{0,252},{4,0},{8,4},{12,8},{16,12},{20,16},{24,20},{28,24},{32,28}... | collective-permute-start | bytes 786440 | tf_op jit(solution)/shard_map/ppermute | solution.py:577
  141.9 11.4 %copy-start.6 = (f32[4,128,128]{2,1,0:T(8,128)S(1)}, f32[4,128,128]{2,1,0:T(8,128)}, u32[]{:S(2)}) copy-start(f32[4,128,128]{2,1,0:T(8,128)} %copy-done.5) | copy-start | bytes 786436
  155.6 13.6 %all-to-all-start.6 = ((f32[32,16,128]{2,1,0:T(8,128)}), f32[32,16,128]{2,1,0:T(8,128)}, u32[]{:S(2)}, u32[]{:S(2)}) async-start(f32[32,16,128]{2,1,0:T(8,128)} %bitcast.24), calls=%async_computation.6 | async-start | bytes 524288 | tf_op jit(solution)/shard_map/all_to_all | solution.py:515
  165.6 10.1 %collective-permute-start.12 = (f32[256,128]{1,0:T(8,128)}, f32[256,128]{1,0:T(8,128)S(1)}, u32[]{:S(2)}, u32[]{:S(2)}) collective-permute-start(f32[256,128]{1,0:T(8,128)} %get-tuple-element.70), channel_id=1, source_target_pairs={{0,4},{4,8},{8,12},{12,16},{16,20},{20,24},{24,28},{28,32},{32,36}... | collective-permute-start | bytes 393224 | tf_op jit(solution)/shard_map/ppermute | solution.py:600
  167.6 8.4 %collective-permute-start.13 = (f32[256,128]{1,0:T(8,128)}, f32[256,128]{1,0:T(8,128)S(1)}, u32[]{:S(2)}, u32[]{:S(2)}) collective-permute-start(f32[256,128]{1,0:T(8,128)} %get-tuple-element.71), channel_id=1, source_target_pairs={{0,252},{4,0},{8,4},{12,8},{16,12},{20,16},{24,20},{28,24},{32,28}... | collective-permute-start | bytes 393224 | tf_op jit(solution)/shard_map/ppermute | solution.py:601
  170.6 8.1 %collective-permute-start.10 = (f32[4,64,128]{2,1,0:T(8,128)S(1)}, f32[4,64,128]{2,1,0:T(8,128)S(1)}, u32[]{:S(2)}, u32[]{:S(2)}) collective-permute-start(f32[4,64,128]{2,1,0:T(8,128)S(1)} %get-tuple-element.68.high), channel_id=1, source_target_pairs={{0,4},{4,8},{8,12},{12,16},{16,20},{20,24},{24,28},{28,32},{32,36}... | collective-permute-start | bytes 393224 | tf_op jit(solution)/shard_map/ppermute | solution.py:577
  175.7 8.2 %collective-permute-start.11 = (f32[4,64,128]{2,1,0:T(8,128)S(1)}, f32[4,64,128]{2,1,0:T(8,128)S(1)}, u32[]{:S(2)}, u32[]{:S(2)}) collective-permute-start(f32[4,64,128]{2,1,0:T(8,128)S(1)} %get-tuple-element.67.low), channel_id=1, source_target_pairs={{0,252},{4,0},{8,4},{12,8},{16,12},{20,16},{24,20},{28,24},{32,28}... | collective-permute-start | bytes 393224 | tf_op jit(solution)/shard_map/ppermute | solution.py:577
  221.4 11.3 %collective-permute-start.14 = (f32[4,128,128]{2,1,0:T(8,128)S(1)}, f32[4,128,128]{2,1,0:T(8,128)S(1)}, u32[]{:S(2)}, u32[]{:S(2)}) collective-permute-start(f32[4,128,128]{2,1,0:T(8,128)S(1)} %get-tuple-element.73.high), channel_id=1, source_target_pairs={{0,4},{4,8},{8,12},{12,16},{16,20},{20,24},{24,28},{28,32},{32,36}... | collective-permute-start | bytes 786440 | tf_op jit(solution)/shard_map/ppermute | solution.py:577
  227.1 10.8 %collective-permute-start.15 = (f32[4,128,128]{2,1,0:T(8,128)S(1)}, f32[4,128,128]{2,1,0:T(8,128)S(1)}, u32[]{:S(2)}, u32[]{:S(2)}) collective-permute-start(f32[4,128,128]{2,1,0:T(8,128)S(1)} %get-tuple-element.72.low), channel_id=1, source_target_pairs={{0,252},{4,0},{8,4},{12,8},{16,12},{20,16},{24,20},{28,24},{32,28}... | collective-permute-start | bytes 786440 | tf_op jit(solution)/shard_map/ppermute | solution.py:577
  253.7 16.1 %all-to-all-start.10 = ((f32[32,32,128]{2,1,0:T(8,128)}), f32[32,32,128]{2,1,0:T(8,128)S(1)}, u32[]{:S(2)}, u32[]{:S(2)}) async-start(f32[32,32,128]{2,1,0:T(8,128)} %bitcast.32), calls=%async_computation.10 | async-start | bytes 1048576 | tf_op jit(solution)/shard_map/all_to_all | solution.py:515
  262.4 15.2 %collective-permute-start.18 = (f32[256,128]{1,0:T(8,128)S(1)}, f32[256,128]{1,0:T(8,128)S(1)}, u32[]{:S(2)}, u32[]{:S(2)}) collective-permute-start(f32[256,128]{1,0:T(8,128)S(1)} %get-tuple-element.78), channel_id=1, source_target_pairs={{0,4},{4,8},{8,12},{12,16},{16,20},{20,24},{24,28},{28,32},{32,36}... | collective-permute-start | bytes 393224 | tf_op jit(solution)/shard_map/ppermute | solution.py:600
  264.3 13.3 %collective-permute-start.19 = (f32[256,128]{1,0:T(8,128)S(1)}, f32[256,128]{1,0:T(8,128)S(1)}, u32[]{:S(2)}, u32[]{:S(2)}) collective-permute-start(f32[256,128]{1,0:T(8,128)S(1)} %get-tuple-element.79), channel_id=1, source_target_pairs={{0,252},{4,0},{8,4},{12,8},{16,12},{20,16},{24,20},{28,24},{32,28}... | collective-permute-start | bytes 393224 | tf_op jit(solution)/shard_map/ppermute | solution.py:601
  271.2 10.3 %collective-permute-start.16 = (f32[4,64,128]{2,1,0:T(8,128)S(1)}, f32[4,64,128]{2,1,0:T(8,128)S(1)}, u32[]{:S(2)}, u32[]{:S(2)}) collective-permute-start(f32[4,64,128]{2,1,0:T(8,128)S(1)} %get-tuple-element.76.high), channel_id=1, source_target_pairs={{0,4},{4,8},{8,12},{12,16},{16,20},{20,24},{24,28},{28,32},{32,36}... | collective-permute-start | bytes 393224 | tf_op jit(solution)/shard_map/ppermute | solution.py:577
  277.6 9.1 %collective-permute-start.17 = (f32[4,64,128]{2,1,0:T(8,128)S(1)}, f32[4,64,128]{2,1,0:T(8,128)S(1)}, u32[]{:S(2)}, u32[]{:S(2)}) collective-permute-start(f32[4,64,128]{2,1,0:T(8,128)S(1)} %get-tuple-element.75.low), channel_id=1, source_target_pairs={{0,252},{4,0},{8,4},{12,8},{16,12},{20,16},{24,20},{28,24},{32,28}... | collective-permute-start | bytes 393224 | tf_op jit(solution)/shard_map/ppermute | solution.py:577
  (6 other events, 4.6 us)

commit v4 on v3

--- a/solution.py
+++ b/solution.py
@@ -360,19 +360,19 @@
         terms[q] = jnp.concatenate(split(pair), axis=0)
     wanted = request[...].astype(i32)
     first, second = (wanted >> 5).astype(f32).astype(bf16), (wanted & 31).astype(f32).astype(bf16)
-    wide = iota((256, 256), 1)
+    wide = iota((512, 256), 1)
 
     def block(step, carry):
-        start = pl.multiple_of(step * 256, 256)
+        start = pl.multiple_of(step * 512, 512)
         sums = []
         for half in range(2):
-            column = slot_columns(first, second, start, 256, half)
+            column = slot_columns(first, second, start, 512, half)
             total = sum(dot_nt(one_hot(column - q * 256 == wide), terms[q]) for q in range(4))
             sums.append(total + pltpu.roll(total, 64, 1))
-        out[pl.ds(start, 256), :] = jnp.where(iota((256, 128), 1) < 64, sums[0], sums[1])
+        out[pl.ds(start, 512), :] = jnp.where(iota((512, 128), 1) < 64, sums[0], sums[1])
         return carry
 
-    lax.fori_loop(0, 4, block, 0)
+    lax.fori_loop(0, 2, block, 0)
 
 
 def last_kernel(low, high, before, after, members, weights, ens, out, final_ens, field):

time: 290 us -> 288 us (level)
  no operation moved by 1% of the time
where the time goes in v4:
time: 288 us
  blocking collectives  107 us (37%)
  starting transfers between devices  74.8 us (26%)
  waiting for transfers between devices  55 us (19%)
  Pallas kernels  44.4 us (15%)
  local copies, waits for them, and re-layouts  3.32 us (1%)
    all_to_all x6, blocking collectives, to_plane(): return lax.all_to_all(value, PLANE, 0, 0, tiled=True)  80.9 us
    ppermute x10, waiting for transfers between devices, halos(): return (lax.ppermute(high, TILE, upward), lax.ppermute(low, TILE, downward))  41.1 us
    ppermute x10, starting transfers between devices, halos(): return (lax.ppermute(high, TILE, upward), lax.ppermute(low, TILE, downward))  28.3 us
    all_to_all x4, starting transfers between devices, to_plane(): return lax.all_to_all(value, PLANE, 0, 0, tiled=True)  28.3 us
    all_to_all x1, blocking collectives, on_device(): wanted = lax.all_to_all(request, TILE, 0, 0, tiled=True)  26.3 us
    all_to_all x4, waiting for transfers between devices, to_plane(): return lax.all_to_all(value, PLANE, 0, 0, tiled=True)  13.2 us
    ppermute x2, starting transfers between devices, spread(): return lax.ppermute(value, ('z',) + LEV, exchange[j * 32:j * 32 + 32])  9.65 us
    pallas_call x2, Pallas kernels, on_device(): call(observe_kernel, [((1024, 128), f32)], [scratch, ((4, 128, 256), bf16...  7.38 us
  transfers between devices with their start and end apart: 24, of which 16 were waited for; matrix products, arithmetic and copies ran while one was open for 0% of the time, Pallas kernels for 6%

profile of v4, /device:TPU:46, one launch (start us, length us, event | category | flops | bytes accessed | tf_op | source)
XLA Modules:
  0.0 287.5 jit_solution(2183109512825539014)
XLA Ops:
  3.5 2.4 collective-permute-start.1
  7.1 6.3 %all-to-all-start = ((f32[32,16,128]{2,1,0:T(8,128)}), f32[32,16,128]{2,1,0:T(8,128)S(1)}, u32[]{:S(2)}, u32[]{:S(2)}) async-start(f32[32,16,128]{2,1,0:T(8,128)} %bitcast.9), calls=%async_computation | async-start | bytes 524288 | tf_op jit(solution)/shard_map/all_to_all | solution.py:515
  19.2 7.7 %collective-permute-start.2 = (f32[1024,128]{1,0:T(8,128)S(1)}, f32[1024,128]{1,0:T(8,128)S(1)}, u32[]{:S(2)}, u32[]{:S(2)}) collective-permute-start(f32[1024,128]{1,0:T(8,128)S(1)} %get-tuple-element.49), channel_id=1, source_target_pairs={{0,0},{1,32},{2,64},{3,96},{32,128},{33,160},{34,192},{35,224},{64... | collective-permute-start | bytes 1572872 | tf_op jit(solution)/shard_map/ppermute | solution.py:532
  28.9 26.3 %all_to_all.123 = f32[64,1,128]{2,1,0:T(1,128)S(1)} all-to-all(f32[64,1,128]{2,1,0:T(1,128)S(1)} %bitcast.60), channel_id=1, replica_groups=mesh['z'=8,'yl'=2,'x'=4,'yh'=2,'core'=2] {'z','yl','x'}, dimensions={0} | all-to-all | bytes 65536 | tf_op jit(solution)/shard_map/all_to_all | solution.py:546
  57.9 7.2 %all-to-all-start.2 = ((f32[32,16,128]{2,1,0:T(8,128)}), f32[32,16,128]{2,1,0:T(8,128)S(1)}, u32[]{:S(2)}, u32[]{:S(2)}) async-start(f32[32,16,128]{2,1,0:T(8,128)} %bitcast.14), calls=%async_computation.2 | async-start | bytes 524288 | tf_op jit(solution)/shard_map/all_to_all | solution.py:515
  67.4 4.1 %all-to-all-done.2 = f32[32,16,128]{2,1,0:T(8,128)S(1)} async-done(((f32[32,16,128]{2,1,0:T(8,128)}), f32[32,16,128]{2,1,0:T(8,128)S(1)}, u32[]{:S(2)}, u32[]{:S(2)}) %all-to-all-start.2) | async-done | bytes 262176 | tf_op jit(solution)/shard_map/all_to_all | solution.py:515
  72.0 6.8 %collective-permute-start.4 = (f32[4,64,128]{2,1,0:T(8,128)S(1)}, f32[4,64,128]{2,1,0:T(8,128)S(1)}, u32[]{:S(2)}, u32[]{:S(2)}) collective-permute-start(f32[4,64,128]{2,1,0:T(8,128)S(1)} %get-tuple-element.57.high), channel_id=1, source_target_pairs={{0,4},{4,8},{8,12},{12,16},{16,20},{20,24},{24,28},{28,32},{32,36}... | collective-permute-start | bytes 393224 | tf_op jit(solution)/shard_map/ppermute | solution.py:577
  82.0 5.2 %collective-permute-done.5.after = f32[4,64,128]{2,1,0:T(8,128)S(1)} collective-permute-done((f32[4,64,128]{2,1,0:T(8,128)S(1)}, f32[4,64,128]{2,1,0:T(8,128)S(1)}, u32[]{:S(2)}, u32[]{:S(2)}) %collective-permute-start.5) | collective-permute-done | bytes 131104 | tf_op jit(solution)/shard_map/ppermute | solution.py:577
  87.2 3.7 %shard_map.156 = f32[1024,128]{1,0:T(8,128)S(1)} custom-call(f32[64,128]{1,0:T(8,128)S(1)} %bitcast.52, f32[4,64,128]{2,1,0:T(8,128)S(1)} %get-tuple-element.56.low, f32[4,64,128]{2,1,0:T(8,128)S(1)} %get-tuple-element.57.high, f32[4,64,128]{2,1,0:T(8,128)S(1)} %collective-permute-done.4.before, f32[4,64,128]{2,1,0:T(8,128)S(1)} %collective-permute-done.5.after, ...), custom_call_target="tpu_custom_call" | custom-call | flops 100000000 | bytes 6000000 | tf_op jit(solution)/shard_map/pallas_call | solution.py:586
  90.9 14.0 %all_to_all.124 = f32[32,32,128]{2,1,0:T(8,128)S(1)} all-to-all(f32[32,32,128]{2,1,0:T(8,128)S(1)} %bitcast.45), channel_id=1, replica_groups=mesh['z'=8,'yl'=2,'x'=4,'yh'=2,'core'=2] {'yl','x','yh','core'}, dimensions={0} | all-to-all | bytes 1048576 | tf_op jit(solution)/shard_map/all_to_all | solution.py:515
  106.5 15.1 %all_to_all.125 = f32[32,32,128]{2,1,0:T(8,128)S(1)} all-to-all(f32[32,32,128]{2,1,0:T(8,128)S(1)} %bitcast.39), channel_id=1, replica_groups=mesh['z'=8,'yl'=2,'x'=4,'yh'=2,'core'=2] {'yl','x','yh','core'}, dimensions={0} | all-to-all | bytes 1048576 | tf_op jit(solution)/shard_map/all_to_all | solution.py:515
  123.8 4.4 %collective-permute-start.8 = (f32[4,128,128]{2,1,0:T(8,128)S(1)}, f32[4,128,128]{2,1,0:T(8,128)S(1)}, u32[]{:S(2)}, u32[]{:S(2)}) collective-permute-start(f32[4,128,128]{2,1,0:T(8,128)S(1)} %get-tuple-element.64.high), channel_id=1, source_target_pairs={{0,4},{4,8},{8,12},{12,16},{16,20},{20,24},{24,28},{28,32},{32,36}... | collective-permute-start | bytes 786440 | tf_op jit(solution)/shard_map/ppermute | solution.py:577
  128.1 5.6 %collective-permute-done.8.before = f32[4,128,128]{2,1,0:T(8,128)S(1)} collective-permute-done((f32[4,128,128]{2,1,0:T(8,128)S(1)}, f32[4,128,128]{2,1,0:T(8,128)S(1)}, u32[]{:S(2)}, u32[]{:S(2)}) %collective-permute-start.8) | collective-permute-done | bytes 262176 | tf_op jit(solution)/shard_map/ppermute | solution.py:577
  133.7 5.2 %collective-permute-done.9.after = f32[4,128,128]{2,1,0:T(8,128)S(1)} collective-permute-done((f32[4,128,128]{2,1,0:T(8,128)S(1)}, f32[4,128,128]{2,1,0:T(8,128)S(1)}, u32[]{:S(2)}, u32[]{:S(2)}) %collective-permute-start.9) | collective-permute-done | bytes 262176 | tf_op jit(solution)/shard_map/ppermute | solution.py:577
  141.1 11.4 %all_to_all.126 = f32[32,16,128]{2,1,0:T(8,128)S(1)} all-to-all(f32[32,16,128]{2,1,0:T(8,128)S(1)} %bitcast.49), channel_id=1, replica_groups=mesh['z'=8,'yl'=2,'x'=4,'yh'=2,'core'=2] {'yl','x','yh','core'}, dimensions={0} | all-to-all | bytes 524288 | tf_op jit(solution)/shard_map/all_to_all | solution.py:515
  154.8 7.7 %all-to-all-start.6 = ((f32[32,16,128]{2,1,0:T(8,128)}), f32[32,16,128]{2,1,0:T(8,128)}, u32[]{:S(2)}, u32[]{:S(2)}) async-start(f32[32,16,128]{2,1,0:T(8,128)} %bitcast.24), calls=%async_computation.6 | async-start | bytes 524288 | tf_op jit(solution)/shard_map/all_to_all | solution.py:515
  162.5 2.3 shard_map.162
  169.8 5.1 %collective-permute-start.10 = (f32[4,64,128]{2,1,0:T(8,128)S(1)}, f32[4,64,128]{2,1,0:T(8,128)S(1)}, u32[]{:S(2)}, u32[]{:S(2)}) collective-permute-start(f32[4,64,128]{2,1,0:T(8,128)S(1)} %get-tuple-element.68.high), channel_id=1, source_target_pairs={{0,4},{4,8},{8,12},{12,16},{16,20},{20,24},{24,28},{28,32},{32,36}... | collective-permute-start | bytes 393224 | tf_op jit(solution)/shard_map/ppermute | solution.py:577
  177.9 5.2 %collective-permute-done.11.after = f32[4,64,128]{2,1,0:T(8,128)S(1)} collective-permute-done((f32[4,64,128]{2,1,0:T(8,128)S(1)}, f32[4,64,128]{2,1,0:T(8,128)S(1)}, u32[]{:S(2)}, u32[]{:S(2)}) %collective-permute-start.11) | collective-permute-done | bytes 131104 | tf_op jit(solution)/shard_map/ppermute | solution.py:577
  183.1 3.7 %shard_map.164 = f32[1024,128]{1,0:T(8,128)S(1)} custom-call(f32[64,128]{1,0:T(8,128)S(1)} %bitcast.54, f32[4,64,128]{2,1,0:T(8,128)S(1)} %get-tuple-element.67.low, f32[4,64,128]{2,1,0:T(8,128)S(1)} %get-tuple-element.68.high, f32[4,64,128]{2,1,0:T(8,128)S(1)} %collective-permute-done.10.before, f32[4,64,128]{2,1,0:T(8,128)S(1)} %collective-permute-done.11.after, ...), custom_call_target="tpu_custom_call" | custom-call | flops 100000000 | bytes 6000000 | tf_op jit(solution)/shard_map/pallas_call | solution.py:586
  186.8 14.0 %all_to_all.127 = f32[32,32,128]{2,1,0:T(8,128)S(1)} all-to-all(f32[32,32,128]{2,1,0:T(8,128)S(1)} %bitcast.46), channel_id=1, replica_groups=mesh['z'=8,'yl'=2,'x'=4,'yh'=2,'core'=2] {'yl','x','yh','core'}, dimensions={0} | all-to-all | bytes 1048576 | tf_op jit(solution)/shard_map/all_to_all | solution.py:515
  202.4 15.1 %all_to_all.128 = f32[32,32,128]{2,1,0:T(8,128)S(1)} all-to-all(f32[32,32,128]{2,1,0:T(8,128)S(1)} %bitcast.41), channel_id=1, replica_groups=mesh['z'=8,'yl'=2,'x'=4,'yh'=2,'core'=2] {'yl','x','yh','core'}, dimensions={0} | all-to-all | bytes 1048576 | tf_op jit(solution)/shard_map/all_to_all | solution.py:515
  219.7 5.7 %collective-permute-start.14 = (f32[4,128,128]{2,1,0:T(8,128)S(1)}, f32[4,128,128]{2,1,0:T(8,128)S(1)}, u32[]{:S(2)}, u32[]{:S(2)}) collective-permute-start(f32[4,128,128]{2,1,0:T(8,128)S(1)} %get-tuple-element.73.high), channel_id=1, source_target_pairs={{0,4},{4,8},{8,12},{12,16},{16,20},{20,24},{24,28},{28,32},{32,36}... | collective-permute-start | bytes 786440 | tf_op jit(solution)/shard_map/ppermute | solution.py:577
  225.4 5.6 %collective-permute-done.14.before = f32[4,128,128]{2,1,0:T(8,128)S(1)} collective-permute-done((f32[4,128,128]{2,1,0:T(8,128)S(1)}, f32[4,128,128]{2,1,0:T(8,128)S(1)}, u32[]{:S(2)}, u32[]{:S(2)}) %collective-permute-start.14) | collective-permute-done | bytes 262176 | tf_op jit(solution)/shard_map/ppermute | solution.py:577
  231.0 5.2 %collective-permute-done.15.after = f32[4,128,128]{2,1,0:T(8,128)S(1)} collective-permute-done((f32[4,128,128]{2,1,0:T(8,128)S(1)}, f32[4,128,128]{2,1,0:T(8,128)S(1)}, u32[]{:S(2)}, u32[]{:S(2)}) %collective-permute-start.15) | collective-permute-done | bytes 262176 | tf_op jit(solution)/shard_map/ppermute | solution.py:577
  238.4 11.3 %all_to_all.129 = f32[32,16,128]{2,1,0:T(8,128)S(1)} all-to-all(f32[32,16,128]{2,1,0:T(8,128)S(1)} %bitcast.50), channel_id=1, replica_groups=mesh['z'=8,'yl'=2,'x'=4,'yh'=2,'core'=2] {'yl','x','yh','core'}, dimensions={0} | all-to-all | bytes 524288 | tf_op jit(solution)/shard_map/all_to_all | solution.py:515
  249.6 2.4 shard_map.168
  252.0 7.1 %all-to-all-start.10 = ((f32[32,32,128]{2,1,0:T(8,128)}), f32[32,32,128]{2,1,0:T(8,128)S(1)}, u32[]{:S(2)}, u32[]{:S(2)}) async-start(f32[32,32,128]{2,1,0:T(8,128)} %bitcast.32), calls=%async_computation.10 | async-start | bytes 1048576 | tf_op jit(solution)/shard_map/all_to_all | solution.py:515
  262.8 5.3 %all-to-all-done.10 = f32[32,32,128]{2,1,0:T(8,128)S(1)} async-done(((f32[32,32,128]{2,1,0:T(8,128)}), f32[32,32,128]{2,1,0:T(8,128)S(1)}, u32[]{:S(2)}, u32[]{:S(2)}) %all-to-all-start.10) | async-done | bytes 524320 | tf_op jit(solution)/shard_map/all_to_all | solution.py:515
  269.5 6.4 %collective-permute-start.16 = (f32[4,64,128]{2,1,0:T(8,128)S(1)}, f32[4,64,128]{2,1,0:T(8,128)S(1)}, u32[]{:S(2)}, u32[]{:S(2)}) collective-permute-start(f32[4,64,128]{2,1,0:T(8,128)S(1)} %get-tuple-element.76.high), channel_id=1, source_target_pairs={{0,4},{4,8},{8,12},{12,16},{16,20},{20,24},{24,28},{28,32},{32,36}... | collective-permute-start | bytes 393224 | tf_op jit(solution)/shard_map/ppermute | solution.py:577
  279.8 5.2 %collective-permute-done.17.after = f32[4,64,128]{2,1,0:T(8,128)S(1)} collective-permute-done((f32[4,64,128]{2,1,0:T(8,128)S(1)}, f32[4,64,128]{2,1,0:T(8,128)S(1)}, u32[]{:S(2)}, u32[]{:S(2)}) %collective-permute-start.17) | collective-permute-done | bytes 131104 | tf_op jit(solution)/shard_map/ppermute | solution.py:577
  285.0 2.6 shard_map.172
  (87 shorter events, 51.4 us)
Async XLA Ops:
  0.6 5.3 %copy-start = (f32[2,32,8,128]{3,2,1,0:T(8,128)S(1)}, f32[2,32,8,128]{3,2,1,0:T(8,128)}, u32[]{:S(2)}) copy-start(f32[2,32,8,128]{3,2,1,0:T(8,128)} %param.13) | copy-start | bytes 786436
  1.5 1.3 collective-permute-start
  3.5 11.1 %collective-permute-start.1 = (f32[256,128]{1,0:T(8,128)S(1)}, f32[256,128]{1,0:T(8,128)S(1)}, u32[]{:S(2)}, u32[]{:S(2)}) collective-permute-start(f32[256,128]{1,0:T(8,128)S(1)} %pad_maximum_fusion.1), channel_id=1, source_target_pairs={{0,2},{2,0},{1,3},{3,1},{4,6},{6,4},{5,7},{7,5},{8,10},{10,8},{9,1... | collective-permute-start | bytes 393224 | tf_op jit(solution)/shard_map/ppermute | solution.py:526
  7.1 12.1 %all-to-all-start = ((f32[32,16,128]{2,1,0:T(8,128)}), f32[32,16,128]{2,1,0:T(8,128)S(1)}, u32[]{:S(2)}, u32[]{:S(2)}) async-start(f32[32,16,128]{2,1,0:T(8,128)} %bitcast.9), calls=%async_computation | async-start | bytes 524288 | tf_op jit(solution)/shard_map/all_to_all | solution.py:515
  14.6 1.0 copy-start.4
  19.2 36.0 %collective-permute-start.2 = (f32[1024,128]{1,0:T(8,128)S(1)}, f32[1024,128]{1,0:T(8,128)S(1)}, u32[]{:S(2)}, u32[]{:S(2)}) collective-permute-start(f32[1024,128]{1,0:T(8,128)S(1)} %get-tuple-element.49), channel_id=1, source_target_pairs={{0,0},{1,32},{2,64},{3,96},{32,128},{33,160},{34,192},{35,224},{64... | collective-permute-start | bytes 1572872 | tf_op jit(solution)/shard_map/ppermute | solution.py:532
  26.9 28.2 %collective-permute-start.3 = (f32[1024,128]{1,0:T(8,128)S(1)}, f32[1024,128]{1,0:T(8,128)S(1)}, u32[]{:S(2)}, u32[]{:S(2)}) collective-permute-start(f32[1024,128]{1,0:T(8,128)S(1)} %get-tuple-element.50), channel_id=1, source_target_pairs={{0,128},{1,160},{2,192},{3,224},{32,0},{33,32},{34,64},{35,96},{64... | collective-permute-start | bytes 1572872 | tf_op jit(solution)/shard_map/ppermute | solution.py:532
  55.2 9.9 %copy-start.7 = (s32[8,128]{1,0:T(8,128)S(1)}, s32[8,128]{1,0:T(8,128)}, u32[]{:S(2)}) copy-start(s32[8,128]{1,0:T(8,128)} %own.1) | copy-start | bytes 12292
  57.9 7.2 %copy-start.1 = (f32[2,32,8,128]{3,2,1,0:T(8,128)S(1)}, f32[2,32,8,128]{3,2,1,0:T(8,128)}, u32[]{:S(2)}) copy-start(f32[2,32,8,128]{3,2,1,0:T(8,128)} %param.14) | copy-start | bytes 786436
  57.9 7.3 %copy-start.2 = (bf16[2,2,32,8,128]{4,3,2,1,0:T(8,128)(2,1)S(1)}, bf16[2,2,32,8,128]{4,3,2,1,0:T(8,128)(2,1)}, u32[]{:S(2)}) copy-start(bf16[2,2,32,8,128]{4,3,2,1,0:T(8,128)(2,1)} %param.15) | copy-start | bytes 786436
  57.9 13.6 %all-to-all-start.2 = ((f32[32,16,128]{2,1,0:T(8,128)}), f32[32,16,128]{2,1,0:T(8,128)S(1)}, u32[]{:S(2)}, u32[]{:S(2)}) async-start(f32[32,16,128]{2,1,0:T(8,128)} %bitcast.14), calls=%async_computation.2 | async-start | bytes 524288 | tf_op jit(solution)/shard_map/all_to_all | solution.py:515
  65.3 13.6 %collective-permute-start.6 = (f32[264,128]{1,0:T(8,128)S(1)}, f32[264,128]{1,0:T(8,128)S(1)}, u32[]{:S(2)}, u32[]{:S(2)}) collective-permute-start(f32[264,128]{1,0:T(8,128)S(1)} %get-tuple-element.60), channel_id=1, source_target_pairs={{0,4},{4,8},{8,12},{12,16},{16,20},{20,24},{24,28},{28,32},{32,36}... | collective-permute-start | bytes 405512 | tf_op jit(solution)/shard_map/ppermute | solution.py:555
  66.9 12.0 %collective-permute-start.7 = (f32[264,128]{1,0:T(8,128)S(1)}, f32[264,128]{1,0:T(8,128)S(1)}, u32[]{:S(2)}, u32[]{:S(2)}) collective-permute-start(f32[264,128]{1,0:T(8,128)S(1)} %get-tuple-element.61), channel_id=1, source_target_pairs={{0,252},{4,0},{8,4},{12,8},{16,12},{20,16},{24,20},{28,24},{32,28}... | collective-permute-start | bytes 405512 | tf_op jit(solution)/shard_map/ppermute | solution.py:556
  72.0 6.8 %copy-start.12 = (f32[8]{0:T(128)S(1)}, f32[8]{0:T(128)}, u32[]{:S(2)}) copy-start(f32[8]{0:T(128)} %param.20) | copy-start | bytes 100
  72.0 6.8 %copy-start.13 = (f32[8]{0:T(128)S(1)}, f32[8]{0:T(128)}, u32[]{:S(2)}) copy-start(f32[8]{0:T(128)} %param.19) | copy-start | bytes 100
  72.0 9.9 %collective-permute-start.4 = (f32[4,64,128]{2,1,0:T(8,128)S(1)}, f32[4,64,128]{2,1,0:T(8,128)S(1)}, u32[]{:S(2)}, u32[]{:S(2)}) collective-permute-start(f32[4,64,128]{2,1,0:T(8,128)S(1)} %get-tuple-element.57.high), channel_id=1, source_target_pairs={{0,4},{4,8},{8,12},{12,16},{16,20},{20,24},{24,28},{28,32},{32,36}... | collective-permute-start | bytes 393224 | tf_op jit(solution)/shard_map/ppermute | solution.py:577
  78.8 8.4 %collective-permute-start.5 = (f32[4,64,128]{2,1,0:T(8,128)S(1)}, f32[4,64,128]{2,1,0:T(8,128)S(1)}, u32[]{:S(2)}, u32[]{:S(2)}) collective-permute-start(f32[4,64,128]{2,1,0:T(8,128)S(1)} %get-tuple-element.56.low), channel_id=1, source_target_pairs={{0,252},{4,0},{8,4},{12,8},{16,12},{20,16},{24,20},{28,24},{32,28}... | collective-permute-start | bytes 393224 | tf_op jit(solution)/shard_map/ppermute | solution.py:577
  123.8 10.0 %collective-permute-start.8 = (f32[4,128,128]{2,1,0:T(8,128)S(1)}, f32[4,128,128]{2,1,0:T(8,128)S(1)}, u32[]{:S(2)}, u32[]{:S(2)}) collective-permute-start(f32[4,128,128]{2,1,0:T(8,128)S(1)} %get-tuple-element.64.high), channel_id=1, source_target_pairs={{0,4},{4,8},{8,12},{12,16},{16,20},{20,24},{24,28},{28,32},{32,36}... | collective-permute-start | bytes 786440 | tf_op jit(solution)/shard_map/ppermute | solution.py:577
  128.1 10.8 %collective-permute-start.9 = (f32[4,128,128]{2,1,0:T(8,128)S(1)}, f32[4,128,128]{2,1,0:T(8,128)S(1)}, u32[]{:S(2)}, u32[]{:S(2)}) collective-permute-start(f32[4,128,128]{2,1,0:T(8,128)S(1)} %get-tuple-element.63.low), channel_id=1, source_target_pairs={{0,252},{4,0},{8,4},{12,8},{16,12},{20,16},{24,20},{28,24},{32,28}... | collective-permute-start | bytes 786440 | tf_op jit(solution)/shard_map/ppermute | solution.py:577
  141.1 11.4 %copy-start.6 = (f32[4,128,128]{2,1,0:T(8,128)S(1)}, f32[4,128,128]{2,1,0:T(8,128)}, u32[]{:S(2)}) copy-start(f32[4,128,128]{2,1,0:T(8,128)} %copy-done.5) | copy-start | bytes 786436
  154.8 13.6 %all-to-all-start.6 = ((f32[32,16,128]{2,1,0:T(8,128)}), f32[32,16,128]{2,1,0:T(8,128)}, u32[]{:S(2)}, u32[]{:S(2)}) async-start(f32[32,16,128]{2,1,0:T(8,128)} %bitcast.24), calls=%async_computation.6 | async-start | bytes 524288 | tf_op jit(solution)/shard_map/all_to_all | solution.py:515
  164.8 10.1 %collective-permute-start.12 = (f32[256,128]{1,0:T(8,128)}, f32[256,128]{1,0:T(8,128)S(1)}, u32[]{:S(2)}, u32[]{:S(2)}) collective-permute-start(f32[256,128]{1,0:T(8,128)} %get-tuple-element.70), channel_id=1, source_target_pairs={{0,4},{4,8},{8,12},{12,16},{16,20},{20,24},{24,28},{28,32},{32,36}... | collective-permute-start | bytes 393224 | tf_op jit(solution)/shard_map/ppermute | solution.py:600
  166.8 8.4 %collective-permute-start.13 = (f32[256,128]{1,0:T(8,128)}, f32[256,128]{1,0:T(8,128)S(1)}, u32[]{:S(2)}, u32[]{:S(2)}) collective-permute-start(f32[256,128]{1,0:T(8,128)} %get-tuple-element.71), channel_id=1, source_target_pairs={{0,252},{4,0},{8,4},{12,8},{16,12},{20,16},{24,20},{28,24},{32,28}... | collective-permute-start | bytes 393224 | tf_op jit(solution)/shard_map/ppermute | solution.py:601
  169.8 8.1 %collective-permute-start.10 = (f32[4,64,128]{2,1,0:T(8,128)S(1)}, f32[4,64,128]{2,1,0:T(8,128)S(1)}, u32[]{:S(2)}, u32[]{:S(2)}) collective-permute-start(f32[4,64,128]{2,1,0:T(8,128)S(1)} %get-tuple-element.68.high), channel_id=1, source_target_pairs={{0,4},{4,8},{8,12},{12,16},{16,20},{20,24},{24,28},{28,32},{32,36}... | collective-permute-start | bytes 393224 | tf_op jit(solution)/shard_map/ppermute | solution.py:577
  174.9 8.2 %collective-permute-start.11 = (f32[4,64,128]{2,1,0:T(8,128)S(1)}, f32[4,64,128]{2,1,0:T(8,128)S(1)}, u32[]{:S(2)}, u32[]{:S(2)}) collective-permute-start(f32[4,64,128]{2,1,0:T(8,128)S(1)} %get-tuple-element.67.low), channel_id=1, source_target_pairs={{0,252},{4,0},{8,4},{12,8},{16,12},{20,16},{24,20},{28,24},{32,28}... | collective-permute-start | bytes 393224 | tf_op jit(solution)/shard_map/ppermute | solution.py:577
  219.7 11.3 %collective-permute-start.14 = (f32[4,128,128]{2,1,0:T(8,128)S(1)}, f32[4,128,128]{2,1,0:T(8,128)S(1)}, u32[]{:S(2)}, u32[]{:S(2)}) collective-permute-start(f32[4,128,128]{2,1,0:T(8,128)S(1)} %get-tuple-element.73.high), channel_id=1, source_target_pairs={{0,4},{4,8},{8,12},{12,16},{16,20},{20,24},{24,28},{28,32},{32,36}... | collective-permute-start | bytes 786440 | tf_op jit(solution)/shard_map/ppermute | solution.py:577
  225.4 10.8 %collective-permute-start.15 = (f32[4,128,128]{2,1,0:T(8,128)S(1)}, f32[4,128,128]{2,1,0:T(8,128)S(1)}, u32[]{:S(2)}, u32[]{:S(2)}) collective-permute-start(f32[4,128,128]{2,1,0:T(8,128)S(1)} %get-tuple-element.72.low), channel_id=1, source_target_pairs={{0,252},{4,0},{8,4},{12,8},{16,12},{20,16},{24,20},{28,24},{32,28}... | collective-permute-start | bytes 786440 | tf_op jit(solution)/shard_map/ppermute | solution.py:577
  252.0 16.1 %all-to-all-start.10 = ((f32[32,32,128]{2,1,0:T(8,128)}), f32[32,32,128]{2,1,0:T(8,128)S(1)}, u32[]{:S(2)}, u32[]{:S(2)}) async-start(f32[32,32,128]{2,1,0:T(8,128)} %bitcast.32), calls=%async_computation.10 | async-start | bytes 1048576 | tf_op jit(solution)/shard_map/all_to_all | solution.py:515
  260.7 15.2 %collective-permute-start.18 = (f32[256,128]{1,0:T(8,128)S(1)}, f32[256,128]{1,0:T(8,128)S(1)}, u32[]{:S(2)}, u32[]{:S(2)}) collective-permute-start(f32[256,128]{1,0:T(8,128)S(1)} %get-tuple-element.78), channel_id=1, source_target_pairs={{0,4},{4,8},{8,12},{12,16},{16,20},{20,24},{24,28},{28,32},{32,36}... | collective-permute-start | bytes 393224 | tf_op jit(solution)/shard_map/ppermute | solution.py:600
  262.7 13.3 %collective-permute-start.19 = (f32[256,128]{1,0:T(8,128)S(1)}, f32[256,128]{1,0:T(8,128)S(1)}, u32[]{:S(2)}, u32[]{:S(2)}) collective-permute-start(f32[256,128]{1,0:T(8,128)S(1)} %get-tuple-element.79), channel_id=1, source_target_pairs={{0,252},{4,0},{8,4},{12,8},{16,12},{20,16},{24,20},{28,24},{32,28}... | collective-permute-start | bytes 393224 | tf_op jit(solution)/shard_map/ppermute | solution.py:601
  269.5 10.3 %collective-permute-start.16 = (f32[4,64,128]{2,1,0:T(8,128)S(1)}, f32[4,64,128]{2,1,0:T(8,128)S(1)}, u32[]{:S(2)}, u32[]{:S(2)}) collective-permute-start(f32[4,64,128]{2,1,0:T(8,128)S(1)} %get-tuple-element.76.high), channel_id=1, source_target_pairs={{0,4},{4,8},{8,12},{12,16},{16,20},{20,24},{24,28},{28,32},{32,36}... | collective-permute-start | bytes 393224 | tf_op jit(solution)/shard_map/ppermute | solution.py:577
  275.9 9.0 %collective-permute-start.17 = (f32[4,64,128]{2,1,0:T(8,128)S(1)}, f32[4,64,128]{2,1,0:T(8,128)S(1)}, u32[]{:S(2)}, u32[]{:S(2)}) collective-permute-start(f32[4,64,128]{2,1,0:T(8,128)S(1)} %get-tuple-element.75.low), channel_id=1, source_target_pairs={{0,252},{4,0},{8,4},{12,8},{16,12},{20,16},{24,20},{28,24},{32,28}... | collective-permute-start | bytes 393224 | tf_op jit(solution)/shard_map/ppermute | solution.py:577
  (6 other events, 4.6 us)
